TPU v7x, 32 devices: a whole 2x2x4 slice. The times are simulated.
32 devices in a mesh: dp: 8 (over z, core), tensor: 4 (over y, x).
Axes of the slice: x: 2, y: 2, z: 4, core: 2. Of those that a mesh axis runs over, the one named last changes fastest.
Arguments:
- hidden_acts: bfloat16 [16384, 14336], P('dp', 'tensor'), may hold values from -6 to 6
- out_grads: bfloat16 [16384, 4096], P('dp', 'tensor'), may hold values from -6 to 6
- proj_in: bfloat16 [14336, 64], P('tensor'), may hold values from -0.046875 to 0.046875
- proj_out: bfloat16 [4096, 64], P('tensor'), may hold values from -0.09375 to 0.09375
- segments: int32 [32, 16384], P(None, 'dp'), may hold values from 0 to 1, as said below
- doc_counts: int32 [8], P('dp'), may hold values from 10 to 32
Outputs:
- doc_grads: bfloat16 [256, 4096], P('dp', 'tensor')
- fisher: float32 [4096, 4096], P('dp', 'tensor')
Inputs may be any that keep to these rules, and one draw needn't show every extreme that they name: `segments`: every token belongs to exactly one slot of its shard; within one shard's 2048 tokens the slots 0 to 31 are contiguous runs in that order, each holding at least one token.
All inputs are finite; a program needn't handle non-finite values.
Results may differ from a plain program's by a relative error of at most 0.0062.
Values may be sent and summed in bfloat16 or wider, within the bound.
No kernel may reach another device: no remote copies, remote signals or barrier semaphores. Data moves between devices by JAX's collectives and lax.ppermute only.
A program may use at most 64 MiB of HBM per device.

v0:
```python
import jax
import jax.numpy as jnp
from jax import lax
from jax.sharding import PartitionSpec as P

RANK = 64


def doc_sums_of(seg_live, dy_proj, x_proj):
    row_count = x_proj.shape[0]
    block_rows = 512
    summed = jnp.zeros((seg_live.shape[0], RANK * RANK), jnp.float32)
    for offset in range(0, row_count, block_rows):
        outer = (
            (
                dy_proj[offset : offset + block_rows, :, None]
                * x_proj[offset : offset + block_rows, None, :]
            )
            .reshape(block_rows, RANK * RANK)
            .astype(jnp.bfloat16)
        )
        summed = summed + jnp.dot(
            seg_live[:, offset : offset + block_rows], outer, preferred_element_type=jnp.float32
        )
    return summed


def transpose_product(left, right):
    return lax.dot_general(
        left, right, (((0,), (0,)), ((), ())), preferred_element_type=jnp.float32
    )


def per_device(hidden_acts, out_grads, proj_in, proj_out, segments, doc_counts):
    x_part = jnp.dot(hidden_acts, proj_in, preferred_element_type=jnp.float32)
    dy_part = jnp.dot(out_grads, proj_out, preferred_element_type=jnp.float32)
    partial_proj = jnp.concatenate([dy_part, x_part], axis=1)
    doc_total = segments.shape[0]
    live_docs = (jnp.arange(doc_total, dtype=jnp.int32) < doc_counts[0]).astype(jnp.int32)
    seg_int = segments * live_docs[:, None]
    seg_live = seg_int.astype(jnp.bfloat16)
    local_tokens = jnp.sum(seg_int).astype(jnp.float32)
    stacked = lax.psum(partial_proj, "tensor")
    doc_sums = doc_sums_of(seg_live, stacked[:, :RANK], stacked[:, RANK:])
    doc_grads = doc_sums.astype(jnp.bfloat16)
    col_width = doc_grads.shape[1] // lax.axis_size("tensor")
    col_block = lax.dynamic_slice_in_dim(
        doc_grads, lax.axis_index("tensor") * col_width, col_width, 1
    )
    total_tokens = lax.psum(local_tokens, "dp")
    dp_size = lax.axis_size("dp")
    row_width = doc_grads.shape[1] // dp_size
    split_rows = doc_grads.reshape(doc_total, dp_size, row_width)
    gathered_rows = lax.all_to_all(
        split_rows, "dp", split_axis=1, concat_axis=0, tiled=True
    ).reshape(doc_total * dp_size, row_width)
    fisher_block = transpose_product(
        gathered_rows, lax.all_gather(col_block, "dp", axis=0, tiled=True)
    )
    return (col_block, fisher_block / total_tokens)


def solution(mesh):
    return jax.shard_map(
        per_device,
        mesh=mesh,
        in_specs=(
            P("dp", "tensor"),
            P("dp", "tensor"),
            P("tensor", None),
            P("tensor", None),
            P(None, "dp"),
            P("dp"),
        ),
        out_specs=(P("dp", "tensor"), P("dp", "tensor")),
        check_vma=False,
    )
```

profile of v0, /device:TPU:0, one launch (start us, length us, event | category | flops | bytes accessed | tf_op | source)
XLA Modules:
  0.0 138.1 jit_solution(17943158903537048808)
XLA Ops:
  7.2 0.0 copy-start
  7.2 0.0 all-reduce.2.cloned.1.call-start
  7.2 3.6 %fusion.7 = f32[2048,64]{0,1:T(8,128)S(1)} fusion(bf16[2048,1024]{1,0:T(8,128)(2,1)} %param.7, bf16[1024,64]{0,1:T(8,128)(2,1)} %param.9), kind=kOutput, calls=%fused_computation.21 | convolution fusion | flops 268435456 | bytes 4849664 | tf_op jit(solution)/shard_map/dot_general | solution.py:36
  10.9 0.0 copy-done
  10.9 0.0 copy-start.2
  10.9 9.7 %fusion.8 = f32[2048,64]{0,1:T(8,128)S(1)} fusion(bf16[2048,3584]{1,0:T(8,128)(2,1)} %param.6, bf16[3584,64]{0,1:T(8,128)(2,1)S(1)} %copy-done), kind=kOutput, calls=%fused_computation.22 | convolution fusion | flops 939524096 | bytes 15663104 | tf_op jit(solution)/shard_map/dot_general | solution.py:35
  20.6 1.0 pad_maximum_fusion
  21.6 0.0 all-reduce.2.cloned.1.call-update
  22.3 0.0 copy-done.2
  22.3 0.8 multiply_reduce_fusion
  23.1 53.9 %all-reduce.2.cloned.1.call-done = f32[2048,128]{0,1:T(8,128)} async-done(((f32[2048,128]{0,1:T(8,128)}), f32[2048,128]{0,1:T(8,128)}) %all-reduce.2.cloned.1.call-update) | async-done | bytes 1048592 | tf_op jit(solution)/shard_map/psum | solution.py:43
  77.0 1.4 fusion.6
  78.3 3.3 %multiply_convert_fusion.2 = (bf16[512,64,64]{0,2,1:T(8,128)(2,1)S(1)}, bf16[512,64,64]{0,2,1:T(8,128)(2,1)S(1)}) fusion(f32[512,64]{0,1:T(8,128)S(1)} %get-tuple-element.6, f32[512,64]{0,1:T(8,128)S(1)} %get-tuple-element.7, f32[512,64]{0,1:T(8,128)S(1)} %get-tuple-element.8, f32[512,64]{0,1:T(8,128)S(1)} %get-tuple-element.9), kind=kLoop, calls=%fused_computation.2 | loop fusion | flops 8388608 | bytes 8912896 | tf_op jit(solution)/shard_map/convert_element_type | solution.py:20
  81.6 1.3 fusion.4
  82.9 1.3 convolution_add_fusion.2
  84.2 3.3 %multiply_convert_fusion = (bf16[512,64,64]{0,2,1:T(8,128)(2,1)S(1)}, bf16[512,64,64]{0,2,1:T(8,128)(2,1)S(1)}) fusion(f32[512,64]{0,1:T(8,128)S(1)} %get-tuple-element.3, f32[512,64]{0,1:T(8,128)S(1)} %get-tuple-element.2, f32[512,64]{0,1:T(8,128)S(1)} %get-tuple-element.4, f32[512,64]{0,1:T(8,128)S(1)} %get-tuple-element.5), kind=kLoop, calls=%fused_computation | loop fusion | flops 8388608 | bytes 8912896 | tf_op jit(solution)/shard_map/convert_element_type | solution.py:20
  87.5 1.3 convolution_add_fusion.1
  88.8 1.3 fusion
  90.2 0.7 copy.19
  90.9 4.6 %all-to-all-start = ((bf16[32,8,512]{2,0,1:T(8,128)(2,1)}), bf16[32,8,512]{2,0,1:T(8,128)(2,1)S(1)}, u32[]{:S(2)}, u32[]{:S(2)}) async-start(bf16[32,8,512]{2,0,1:T(8,128)(2,1)} %bitcast.23), calls=%async_computation | async-start | bytes 524288 | tf_op jit(solution)/shard_map/all_to_all | solution.py:54
  96.2 17.8 %psum.15 = f32[]{:T(128)} all-reduce(f32[]{:T(128)S(6)} %convert_element_type.51), channel_id=1, replica_groups=mesh['dp'=8,'tensor'=4] {'dp'}, use_global_device_ids=true, to_apply=%region_2.0 | all-reduce | flops 1 | bytes 8 | tf_op jit(solution)/shard_map/psum | solution.py:50
  113.9 0.0 copy-start.1
  113.9 14.9 %all_gather.3 = bf16[256,1024]{1,0:T(8,128)(2,1)S(1)} all-gather(bf16[32,1024]{1,0:T(8,128)(2,1)S(1)} %constant_dynamic-slice_fusion), channel_id=1, replica_groups=mesh['dp'=8,'tensor'=4] {'dp'}, dimensions={0}, use_global_device_ids=true | all-gather | bytes 589824 | tf_op jit(solution)/shard_map/all_gather | solution.py:58
  128.9 0.0 all-to-all-done
  128.9 2.4 %convolution_divide_fusion = f32[512,1024]{1,0:T(8,128)} fusion(bf16[256,512]{1,0:T(8,128)(2,1)S(1)} %bitcast.30, bf16[256,1024]{1,0:T(8,128)(2,1)S(1)} %all_gather.3, f32[]{:T(128)} %psum.15), kind=kOutput, calls=%fused_computation.8 | convolution fusion | flops 268959744 | bytes 2883588 | tf_op jit(solution)/shard_map/dot_general | solution.py:29
  131.3 0.0 copy-done.1
  (2 shorter events, 0.0 us)
Async XLA Ops:
  7.2 3.7 %copy-start = (bf16[3584,64]{0,1:T(8,128)(2,1)S(1)}, bf16[3584,64]{0,1:T(8,128)(2,1)}, u32[]{:S(2)}) copy-start(bf16[3584,64]{0,1:T(8,128)(2,1)} %param.8) | copy-start | bytes 1376260
  7.2 69.8 %all-reduce.2.cloned.1.call-start = ((), (), s32[]{:S(2)}) async-start(), calls=%async_computation.1 | async-start | bytes 2097152 | tf_op jit(solution)/shard_map/psum | solution.py:43
  10.9 11.5 %copy-start.2 = (s32[32,2048]{1,0:T(8,128)S(1)}, s32[32,2048]{1,0:T(8,128)}, u32[]{:S(2)}) copy-start(s32[32,2048]{1,0:T(8,128)} %param.10) | copy-start | bytes 786436
  90.9 38.0 %all-to-all-start = ((bf16[32,8,512]{2,0,1:T(8,128)(2,1)}), bf16[32,8,512]{2,0,1:T(8,128)(2,1)S(1)}, u32[]{:S(2)}, u32[]{:S(2)}) async-start(bf16[32,8,512]{2,0,1:T(8,128)(2,1)} %bitcast.23), calls=%async_computation | async-start | bytes 524288 | tf_op jit(solution)/shard_map/all_to_all | solution.py:54
  113.9 17.3 %copy-start.1 = (bf16[32,1024]{1,0:T(8,128)(2,1)}, bf16[32,1024]{1,0:T(8,128)(2,1)S(1)}, u32[]{:S(2)}) copy-start(bf16[32,1024]{1,0:T(8,128)(2,1)S(1)} %constant_dynamic-slice_fusion) | copy-start | bytes 196612
Sparse Core Ops, SparseCore 0:
  21.8 55.1 all-reduce.1
where the time goes:
time: 138 us
  waiting for transfers between devices  53.9 us (39%)
  blocking collectives  32.7 us (24%)
  matrix products  21 us (15%)
  between operations  15.4 us (11%)
  other arithmetic  8.34 us (6%)
  starting transfers between devices  4.65 us (3%)
  local copies, waits for them, and re-layouts  2.11 us (2%)
    psum x1, waiting for transfers between devices, per_device(): stacked = lax.psum(partial_proj, 'tensor')  53.9 us
    psum x1, blocking collectives, per_device(): total_tokens = lax.psum(local_tokens, 'dp')  17.8 us
    all_gather x1, blocking collectives, per_device(): lax.all_gather(col_block, 'dp', axis=0, tiled=True)  14.9 us
    dot_general x1, matrix products, per_device(): x_part = jnp.dot(hidden_acts, proj_in, preferred_element_type=jnp.float32)  9.71 us
    convert_element_type x2, other arithmetic, doc_sums_of(): outer = (dy_proj[offset:offset + block_rows, :, None] * x_proj[offset:off...  6.53 us
    dot_general x4, matrix products, doc_sums_of(): jnp.dot(seg_live[:, offset:offset + block_rows], outer, preferred_element...  5.29 us
    all_to_all x1, starting transfers between devices, per_device(): lax.all_to_all(split_rows, 'dp', split_axis=1, concat_axis=0, tiled=True)  4.61 us
    dot_general x1, matrix products, per_device(): dy_part = jnp.dot(out_grads, proj_out, preferred_element_type=jnp.float32)  3.63 us
  transfers between devices with their start and end apart: 2, of which 1 were waited for; matrix products, arithmetic and copies ran while one was open for 1% of the time, Pallas kernels for 0%

commit v1 on v0

v1 whole, which is shorter than its diff:
```python
import functools

import jax
import jax.numpy as jnp
from jax import lax
from jax.experimental import pallas as pl
from jax.experimental.pallas import tpu as pltpu
from jax.sharding import PartitionSpec as P

BF16 = jnp.bfloat16
F32 = jnp.float32
NT = (((1,), (1,)), ((), ()))
TN = (((0,), (0,)), ((), ()))


def peer_of(idx, step, size):
    if size & (size - 1) == 0:
        return idx ^ step
    return lax.rem(step + size - idx, size)


def swap(value, axis, step):
    size = lax.axis_size(axis)
    pairs = []
    for idx in range(size):
        other = idx ^ step if size & (size - 1) == 0 else (step - idx) % size
        pairs.append((idx, other))
    return lax.ppermute(value, axis, pairs)


def smem():
    return pl.BlockSpec(memory_space=pltpu.SMEM)


def dy_kernel(tensor_size, pos_ref, counts_ref, seg_ref, grads_ref, proj_ref, *rest):
    outs, count_ref, weights = rest[:tensor_size], rest[tensor_size], rest[tensor_size + 1]
    step = pl.program_id(0)
    rank = proj_ref.shape[0]
    part = rank // tensor_size

    @pl.when(step == 0)
    def _():
        row = lax.broadcasted_iota(jnp.int32, (rank, rank), 0)
        col = lax.broadcasted_iota(jnp.int32, (rank, rank), 1)
        source = peer_of(pos_ref[0], row // part, tensor_size) * part + row % part
        pick = jnp.where(col == source, 1.0, 0.0).astype(BF16)
        weights[...] = jnp.dot(pick, proj_ref[...], preferred_element_type=F32).astype(BF16)
        count_ref[...] = jnp.zeros_like(count_ref)

    partial = lax.dot_general(weights[...], grads_ref[...], NT, preferred_element_type=F32)
    for k in range(tensor_size):
        outs[k][...] = partial[k * part : (k + 1) * part, :].astype(outs[k].dtype)
    docs = lax.broadcasted_iota(jnp.int32, seg_ref.shape, 0)
    live = jnp.where(docs < counts_ref[0], seg_ref[...], 0)
    count_ref[...] += jnp.sum(live).astype(F32)


def dy_partials(pos, counts, seg, grads, proj_t, tensor_size):
    tokens, width = grads.shape
    rank = proj_t.shape[0]
    part = rank // tensor_size
    tile = min(512, tokens)
    docs = seg.shape[0]
    outs = [
        jax.ShapeDtypeStruct((part, tokens), F32 if k == 0 else BF16) for k in range(tensor_size)
    ]
    return pl.pallas_call(
        functools.partial(dy_kernel, tensor_size),
        grid=(tokens // tile,),
        in_specs=[
            smem(),
            smem(),
            pl.BlockSpec((docs, tile), lambda i: (0, i)),
            pl.BlockSpec((tile, width), lambda i: (i, 0)),
            pl.BlockSpec((rank, width), lambda i: (0, 0)),
        ],
        out_specs=[pl.BlockSpec((part, tile), lambda i: (0, i)) for _ in outs]
        + [pl.BlockSpec((8, 128), lambda i: (0, 0))],
        out_shape=outs + [jax.ShapeDtypeStruct((8, 128), F32)],
        scratch_shapes=[pltpu.VMEM((rank, width), BF16)],
        cost_estimate=pl.CostEstimate(
            flops=2 * tokens * width * rank, bytes_accessed=2 * tokens * width, transcendentals=0
        ),
        name="dy_partials",
    )(pos, counts, seg, grads, proj_t)


def x_kernel(steps, pos_ref, acts_ref, proj_ref, *outs):
    step, sub = pl.program_id(0), pl.program_id(1)
    tile = acts_ref.shape[0]
    partial = lax.dot_general(proj_ref[...], acts_ref[...], NT, preferred_element_type=F32)
    cols = pl.ds(pl.multiple_of(sub * tile, tile), tile)
    for n in range(len(steps)):

        @pl.when(step == n)
        def _():
            outs[n][:, cols] = partial.astype(outs[n].dtype)


def x_partials(pos, acts, proj_t, steps, tensor_size, dtype):
    tokens, width = acts.shape
    rank = proj_t.shape[0]
    chunk = tokens // tensor_size
    tile = min(256, chunk)
    per_chunk = chunk // tile
    first = steps[0]

    def token_block(n, j, pos_ref):
        return peer_of(pos_ref[0], n + first, tensor_size) * per_chunk + j, 0

    outs = [jax.ShapeDtypeStruct((rank, chunk), dtype) for _ in steps]
    flops = 2 * chunk * len(steps) * width * rank
    return pl.pallas_call(
        functools.partial(x_kernel, steps),
        grid_spec=pltpu.PrefetchScalarGridSpec(
            num_scalar_prefetch=1,
            grid=(len(steps), per_chunk),
            in_specs=[
                pl.BlockSpec((tile, width), token_block),
                pl.BlockSpec((rank, width), lambda n, j, p: (0, 0)),
            ],
            out_specs=[pl.BlockSpec((rank, chunk), lambda n, j, p: (0, 0)) for _ in outs],
        ),
        out_shape=outs,
        cost_estimate=pl.CostEstimate(
            flops=flops, bytes_accessed=2 * chunk * len(steps) * width, transcendentals=0
        ),
        name="x_partials",
    )(pos, acts, proj_t)


def docs_kernel(tensor_size, pos_ref, counts_ref, seg_ref, *rest):
    dy_parts, xs = rest[:tensor_size], rest[tensor_size : 2 * tensor_size]
    out_ref, dy_ref, sums_ref = rest[2 * tensor_size :]
    docs, tokens = seg_ref.shape
    part = dy_parts[0].shape[0]
    rows = dy_ref.shape[0]
    rank, chunk = xs[0].shape
    total = dy_parts[0][...]
    for other in dy_parts[1:]:
        total = total + other[...].astype(F32)
    if rows > part:
        total = jnp.concatenate([total, jnp.zeros((rows - part, tokens), F32)], axis=0)
    dy_ref[...] = total
    sums = jnp.zeros((docs * rows, rank), F32)
    doc = lax.broadcasted_iota(jnp.int32, (docs, chunk), 0)
    for k in range(tensor_size):
        start = peer_of(pos_ref[0], k, tensor_size) * chunk
        cols = pl.ds(pl.multiple_of(start, chunk), chunk)
        seg = jnp.where(doc < counts_ref[0], seg_ref[:, cols], 0).astype(F32).astype(BF16)
        dy = dy_ref[:, cols]
        high = dy.astype(BF16)
        low = (dy - high.astype(F32)).astype(BF16)
        for piece in (high, low):
            masked = (seg[:, None, :] * piece[None, :, :]).reshape(docs * rows, chunk)
            sums = sums + lax.dot_general(masked, xs[k][...], NT, preferred_element_type=F32)
    sums_ref[...] = sums
    lanes = 128 // rank
    for a in range(0, part, lanes):
        pieces = [sums_ref[pl.ds(a + n, docs, stride=rows), :] for n in range(lanes)]
        wide = pieces[0] if lanes == 1 else jnp.concatenate(pieces, axis=1)
        out_ref[:, a * rank : (a + lanes) * rank] = wide.astype(BF16)


def doc_sums(pos, counts, seg, dy_parts, xs):
    tensor_size = len(xs)
    docs, tokens = seg.shape
    part = dy_parts[0].shape[0]
    rank = xs[0].shape[0]
    rows = -(-part // 16) * 16
    vmem = pl.BlockSpec(memory_space=pltpu.VMEM)
    return pl.pallas_call(
        functools.partial(docs_kernel, tensor_size),
        in_specs=[smem(), smem()] + [vmem] * (1 + 2 * tensor_size),
        out_specs=vmem,
        out_shape=jax.ShapeDtypeStruct((docs, part * rank), BF16),
        scratch_shapes=[pltpu.VMEM((rows, tokens), F32), pltpu.VMEM((docs * rows, rank), F32)],
        cost_estimate=pl.CostEstimate(
            flops=4 * docs * rows * tokens * rank, bytes_accessed=1 << 20, transcendentals=0
        ),
        name="doc_sums",
    )(pos, counts, seg, *dy_parts, *xs)


def fisher_kernel(shards, total_ref, *rest):
    rows, cols, out_ref = rest[:shards], rest[shards : 2 * shards], rest[2 * shards]
    left = jnp.concatenate([r[...] for r in rows], axis=0)
    right = jnp.concatenate([c[...] for c in cols], axis=0)
    product = lax.dot_general(left, right, TN, preferred_element_type=F32)
    out_ref[...] = product / total_ref[0:1, 0:1]


def fisher_block(total, rows, cols):
    shards = len(rows)
    docs, height = rows[0].shape
    width = cols[0].shape[1]
    tile = min(128, height)
    return pl.pallas_call(
        functools.partial(fisher_kernel, shards),
        grid=(height // tile,),
        in_specs=[pl.BlockSpec((8, 128), lambda i: (0, 0))]
        + [pl.BlockSpec((docs, tile), lambda i: (0, i)) for _ in rows]
        + [pl.BlockSpec((docs, width), lambda i: (0, 0)) for _ in cols],
        out_specs=pl.BlockSpec((tile, width), lambda i: (i, 0)),
        out_shape=jax.ShapeDtypeStruct((height, width), F32),
        cost_estimate=pl.CostEstimate(
            flops=2 * docs * shards * height * width,
            bytes_accessed=4 * height * width,
            transcendentals=0,
        ),
        name="fisher_block",
    )(total, *rows, *cols)


def per_device(hidden_acts, out_grads, proj_in, proj_out, segments, doc_counts):
    tensor_size, dp_size = lax.axis_size("tensor"), lax.axis_size("dp")
    pos = lax.axis_index("tensor").astype(jnp.int32).reshape(1)
    shard = lax.axis_index("dp").astype(jnp.int32)
    steps = range(1, tensor_size)

    *dy_parts, count = dy_partials(
        pos, doc_counts, segments, out_grads, proj_out.T, tensor_size
    )
    dy_parts = [dy_parts[0]] + [swap(dy_parts[k], "tensor", k) for k in steps]

    step = 1
    while step < dp_size:
        count = count + swap(count, "dp", step)
        step *= 2

    proj_t = proj_in.T
    sent = x_partials(pos, hidden_acts, proj_t, tuple(steps), tensor_size, BF16)
    received = [swap(sent[k - 1], "tensor", k) for k in steps]
    (own,) = x_partials(pos, hidden_acts, proj_t, (0,), tensor_size, F32)
    for other in received:
        own = own + other.astype(F32)
    own = own.astype(BF16)
    xs = [own] + [swap(own, "tensor", k) for k in steps]

    grads = doc_sums(pos, doc_counts, segments, dy_parts, xs)
    cols = [grads]
    for j in range(2, dp_size, 2):
        cols += [None, swap(grads, "dp", j)]
    cols.append(None)
    for j in range(1, dp_size, 2):
        cols[j] = swap(cols[j - 1], "dp", 1)
    blocks = jnp.stack([grads] + [swap(grads, "tensor", k) for k in steps])
    share = dp_size // tensor_size
    height = grads.shape[1] // share
    rows = []
    for j in range(dp_size):
        target = peer_of(shard, j, dp_size)
        block = peer_of(pos[0], target // share, tensor_size)
        piece = lax.dynamic_slice(
            blocks, (block, 0, target % share * height), (1, grads.shape[0], height)
        )[0]
        rows.append(piece if j == 0 else swap(piece, "dp", j))
    return grads, fisher_block(count, rows, cols)


def solution(mesh):
    return jax.shard_map(
        per_device,
        mesh=mesh,
        in_specs=(
            P("dp", "tensor"),
            P("dp", "tensor"),
            P("tensor", None),
            P("tensor", None),
            P(None, "dp"),
            P("dp"),
        ),
        out_specs=(P("dp", "tensor"), P("dp", "tensor")),
        check_vma=False,
    )
```

time: 138 us -> 74.6 us (0.54)
  waiting for transfers between devices: 53.9 us -> 13.1 us
  blocking collectives: 32.7 us -> 0 us
  starting transfers between devices: 4.65 us -> 31 us
  Pallas kernels: 0 us -> 24.1 us
  matrix products: 21 us -> 0 us
  between operations: 15.4 us -> 1.52 us
  other arithmetic: 8.34 us -> 2.45 us
    psum x1 -> x0, waiting for transfers between devices: 53.9 us -> none  [per_device(): stacked = lax.psum(partial_proj, 'tensor')]
    ppermute x0 -> x29, starting transfers between devices: none -> 31 us  [swap(): return lax.ppermute(value, axis, pairs)]
    pallas_call x0 -> x5, Pallas kernels: none -> 24.1 us  [the longest x2 11.9 us: x_partials(): pl.pallas_call(functools.partial(x_kernel, steps), grid_spec=pltpu.Prefet...]
    dot_general x7 -> x0, matrix products: 21 us -> none  [the longest x1 9.71 us: per_device(): x_part = jnp.dot(hidden_acts, proj_in, preferred_element_type=jnp.float32)]
    psum x1 -> x0, blocking collectives: 17.8 us -> none  [per_device(): total_tokens = lax.psum(local_tokens, 'dp')]
    all_gather x1 -> x0, blocking collectives: 14.9 us -> none  [per_device(): lax.all_gather(col_block, 'dp', axis=0, tiled=True)]
    ppermute x0 -> x29, waiting for transfers between devices: none -> 13.1 us  [swap(): return lax.ppermute(value, axis, pairs)]
    convert_element_type x3 -> x1, other arithmetic: 6.53 us -> 0.94 us  [per_device(): own = own.astype(BF16)]
  transfers between devices with their start and end apart: 2 -> 29, of which waited for: 1 -> 10; matrix products, arithmetic and copies ran while one was open for 1% -> 4% of each run, Pallas kernels for 0% -> 11%
where the time goes in v1:
time: 74.6 us; the launch traced here: 74.1 us
  starting transfers between devices  31 us (42%)
  Pallas kernels  24.1 us (32%)
  waiting for transfers between devices  13.1 us (18%)
  other arithmetic  2.45 us (3%)
  local copies, waits for them, and re-layouts  1.88 us (3%)
  between operations  1.52 us (2%)
    ppermute x29, starting transfers between devices, swap(): return lax.ppermute(value, axis, pairs)  31 us
    ppermute x29, waiting for transfers between devices, swap(): return lax.ppermute(value, axis, pairs)  13.1 us
    pallas_call x2, Pallas kernels, x_partials(): pl.pallas_call(functools.partial(x_kernel, steps), grid_spec=pltpu.Prefet...  11.9 us
    pallas_call x1, Pallas kernels, dy_partials(): pl.pallas_call(functools.partial(dy_kernel, tensor_size), grid=(tokens //...  4.89 us
    pallas_call x1, Pallas kernels, fisher_block(): pl.pallas_call(functools.partial(fisher_kernel, shards), grid=(height //...  4.14 us
    pallas_call x1, Pallas kernels, doc_sums(): pl.pallas_call(functools.partial(docs_kernel, tensor_size), in_specs=[sme...  3.14 us
  transfers between devices with their start and end apart: 29, of which 10 were waited for; matrix products, arithmetic and copies ran while one was open for 4% of the time, Pallas kernels for 11%

profile of v1, /device:TPU:0, one launch (start us, length us, event | category | flops | bytes accessed | tf_op | source)
XLA Modules:
  0.0 74.1 jit_solution(5315786532076284578)
XLA Ops:
  0.6 8.3 %x_partials.3 = (bf16[64,512]{1,0:T(8,128)(2,1)}, bf16[64,512]{1,0:T(8,128)(2,1)}, bf16[64,512]{1,0:T(8,128)(2,1)}) custom-call(s32[1]{0:T(128)} %bitcast.pos_ref, bf16[2048,3584]{1,0:T(8,128)(2,1)} %acts_ref.3, bf16[64,3584]{1,0:T(8,128)(2,1)} %bitcast.23), custom_call_target="tpu_custom_call" | custom-call | flops 704643072 | bytes 11010048 | tf_op jit(solution)/shard_map/x_partials/pallas_call | solution.py:113
  9.0 3.0 %collective-permute-start.3 = (bf16[64,512]{1,0:T(8,128)(2,1)}, bf16[64,512]{1,0:T(8,128)(2,1)S(1)}, u32[]{:S(2)}, u32[]{:S(2)}) collective-permute-start(bf16[64,512]{1,0:T(8,128)(2,1)} %get-tuple-element.14), channel_id=1, source_target_pairs={{0,1},{1,0},{2,3},{3,2},{4,5},{5,4},{6,7},{7,6},{8,9},{9,8},{10,11... | collective-permute-start | bytes 196616 | tf_op jit(solution)/shard_map/ppermute | solution.py:28
  11.9 1.5 %collective-permute-start.4 = (bf16[64,512]{1,0:T(8,128)(2,1)}, bf16[64,512]{1,0:T(8,128)(2,1)S(1)}, u32[]{:S(2)}, u32[]{:S(2)}) collective-permute-start(bf16[64,512]{1,0:T(8,128)(2,1)} %get-tuple-element.15), channel_id=1, source_target_pairs={{0,2},{1,3},{2,0},{3,1},{4,6},{5,7},{6,4},{7,5},{8,10},{9,11},{10,... | collective-permute-start | bytes 196616 | tf_op jit(solution)/shard_map/ppermute | solution.py:28
  13.4 0.0 collective-permute-start.5
  14.1 4.9 %dy_partials.1 = (f32[16,2048]{1,0:T(8,128)}, bf16[16,2048]{1,0:T(8,128)(2,1)}, bf16[16,2048]{1,0:T(8,128)(2,1)}, bf16[16,2048]{1,0:T(8,128)(2,1)}, f32[8,128]{1,0:T(8,128)}) custom-call(s32[1]{0:T(128)} %bitcast.pos_ref, s32[1]{0:T(128)S(6)} %copy.8.counts_ref, s32[32,2048]{1,0:T(8,128)} %seg_ref.3, bf16[2048,1024]{1,0:T(8,128)(2,1)} %grads_ref.1, ...), custom_call_target="tpu_custom_call" | custom-call | flops 268435456 | bytes 4194304 | tf_op jit(solution)/shard_map/dy_partials/pallas_call | solution.py:67
  19.0 2.0 %collective-permute-start = (bf16[16,2048]{1,0:T(8,128)(2,1)}, bf16[16,2048]{1,0:T(8,128)(2,1)S(1)}, u32[]{:S(2)}, u32[]{:S(2)}) collective-permute-start(bf16[16,2048]{1,0:T(8,128)(2,1)} %get-tuple-element.11), channel_id=1, source_target_pairs={{0,1},{1,0},{2,3},{3,2},{4,5},{5,4},{6,7},{7,6},{8,9},{9,8},{10,11... | collective-permute-start | bytes 196616 | tf_op jit(solution)/shard_map/ppermute | solution.py:28
  21.0 1.5 %collective-permute-start.1 = (bf16[16,2048]{1,0:T(8,128)(2,1)}, bf16[16,2048]{1,0:T(8,128)(2,1)S(1)}, u32[]{:S(2)}, u32[]{:S(2)}) collective-permute-start(bf16[16,2048]{1,0:T(8,128)(2,1)} %get-tuple-element.12), channel_id=1, source_target_pairs={{0,2},{1,3},{2,0},{3,1},{4,6},{5,7},{6,4},{7,5},{8,10},{9,11},{10,... | collective-permute-start | bytes 196616 | tf_op jit(solution)/shard_map/ppermute | solution.py:28
  22.5 3.6 %x_partials.2 = f32[64,512]{1,0:T(8,128)} custom-call(s32[1]{0:T(128)} %bitcast.pos_ref, bf16[2048,3584]{1,0:T(8,128)(2,1)} %acts_ref.3, bf16[64,3584]{1,0:T(8,128)(2,1)} %bitcast.24), custom_call_target="tpu_custom_call" | custom-call | flops 234881024 | bytes 3670016 | tf_op jit(solution)/shard_map/x_partials/pallas_call | solution.py:113
  26.1 0.0 collective-permute-start.2
  26.2 0.0 collective-permute-done.4
  26.2 0.0 collective-permute-done.5
  26.2 0.9 %add_convert_fusion.rest_4_ = bf16[64,512]{1,0:T(8,128)(2,1)S(1)} fusion(bf16[64,512]{1,0:T(8,128)(2,1)S(1)} %collective-permute-done.5, bf16[64,512]{1,0:T(8,128)(2,1)S(1)} %collective-permute-done.4, f32[64,512]{1,0:T(8,128)} %x_partials.2, bf16[64,512]{1,0:T(8,128)(2,1)S(1)} %collective-permute-done.3), kind=kLoop, calls=%fused_computation.1 | loop fusion | flops 229376 | bytes 393216 | tf_op jit(solution)/shard_map/convert_element_type | solution.py:237
  27.1 3.0 %collective-permute-start.8 = (bf16[64,512]{1,0:T(8,128)(2,1)S(1)}, bf16[64,512]{1,0:T(8,128)(2,1)S(1)}, u32[]{:S(2)}, u32[]{:S(2)}) collective-permute-start(bf16[64,512]{1,0:T(8,128)(2,1)S(1)} %add_convert_fusion.rest_4_), channel_id=1, source_target_pairs={{0,3},{1,2},{2,1},{3,0},{4,7},{5,6},{6,5},{7,4},{8,11},{9,10},{10,... | collective-permute-start | bytes 196616 | tf_op jit(solution)/shard_map/ppermute | solution.py:28
  30.1 0.5 collective-permute-start.7
  30.6 0.0 collective-permute-done.rest_1_
  30.6 0.1 collective-permute-start.6
  30.7 0.7 collective-permute-done.2.rest_3_
  31.4 1.6 %collective-permute-done.8.rest_7_ = bf16[64,512]{1,0:T(8,128)(2,1)S(1)} collective-permute-done((bf16[64,512]{1,0:T(8,128)(2,1)S(1)}, bf16[64,512]{1,0:T(8,128)(2,1)S(1)}, u32[]{:S(2)}, u32[]{:S(2)}) %collective-permute-start.8) | collective-permute-done | bytes 65568 | tf_op jit(solution)/shard_map/ppermute | solution.py:28
  33.0 1.4 %collective-permute-done.7.rest_6_ = bf16[64,512]{1,0:T(8,128)(2,1)S(1)} collective-permute-done((bf16[64,512]{1,0:T(8,128)(2,1)S(1)}, bf16[64,512]{1,0:T(8,128)(2,1)S(1)}, u32[]{:S(2)}, u32[]{:S(2)}) %collective-permute-start.7) | collective-permute-done | bytes 65568 | tf_op jit(solution)/shard_map/ppermute | solution.py:28
  34.3 0.5 collective-permute-done.6.rest_5_
  34.9 0.1 copy-done.21
  35.0 0.5 copy-done.22
  35.5 3.1 %doc_sums.1.rest_8_ = bf16[32,1024]{1,0:T(8,128)(2,1)} custom-call(s32[1]{0:T(128)} %bitcast.pos_ref, s32[1]{0:T(128)S(6)} %copy.8.counts_ref, s32[32,2048]{1,0:T(8,128)} %seg_ref.3, f32[16,2048]{1,0:T(8,128)} %get-tuple-element.10.rest_0_, bf16[16,2048]{1,0:T(8,128)(2,1)} %copy-done.16, bf16[16,2048]{1,0:T(8,128)(2,1)} %copy-done.17, ...), custom_call_target="tpu_custom_call" | custom-call | flops 268435456 | bytes 1048576 | tf_op jit(solution)/shard_map/doc_sums/pallas_call | solution.py:172
  38.6 1.5 %collective-permute-start.14 = (bf16[32,1024]{1,0:T(8,128)(2,1)}, bf16[32,1024]{1,0:T(8,128)(2,1)S(1)}, u32[]{:S(2)}, u32[]{:S(2)}) collective-permute-start(bf16[32,1024]{1,0:T(8,128)(2,1)} %doc_sums.1.rest_8_), channel_id=1, source_target_pairs={{0,3},{1,2},{2,1},{3,0},{4,7},{5,6},{6,5},{7,4},{8,11},{9,10},{10,... | collective-permute-start | bytes 196616 | tf_op jit(solution)/shard_map/ppermute | solution.py:28
  40.1 0.2 collective-permute-start.13
  40.3 1.8 %collective-permute-start.12 = (bf16[32,1024]{1,0:T(8,128)(2,1)}, bf16[32,1024]{1,0:T(8,128)(2,1)S(1)}, u32[]{:S(2)}, u32[]{:S(2)}) collective-permute-start(bf16[32,1024]{1,0:T(8,128)(2,1)} %doc_sums.1.rest_8_), channel_id=1, source_target_pairs={{0,1},{1,0},{2,3},{3,2},{4,5},{5,4},{6,7},{7,6},{8,9},{9,8},{10,11... | collective-permute-start | bytes 196616 | tf_op jit(solution)/shard_map/ppermute | solution.py:28
  42.1 0.0 collective-permute-start.9
  42.1 1.2 %collective-permute-done.9 = f32[8,128]{1,0:T(8,128)S(1)} collective-permute-done((f32[8,128]{1,0:T(8,128)S(1)}, f32[8,128]{1,0:T(8,128)S(1)}, u32[]{:S(2)}, u32[]{:S(2)}) %collective-permute-start.9) | collective-permute-done | bytes 4128 | tf_op jit(solution)/shard_map/ppermute | solution.py:28
  43.3 1.6 %collective-permute-start.10 = (f32[8,128]{1,0:T(8,128)S(1)}, f32[8,128]{1,0:T(8,128)S(1)}, u32[]{:S(2)}, u32[]{:S(2)}) collective-permute-start(f32[8,128]{1,0:T(8,128)S(1)} %add.102), channel_id=1, source_target_pairs={{0,8},{4,12},{8,0},{12,4},{16,24},{20,28},{24,16},{28,20},{1,9},{5... | collective-permute-start | bytes 12296 | tf_op jit(solution)/shard_map/ppermute | solution.py:28
  44.9 2.0 %collective-permute-done.10 = f32[8,128]{1,0:T(8,128)S(1)} collective-permute-done((f32[8,128]{1,0:T(8,128)S(1)}, f32[8,128]{1,0:T(8,128)S(1)}, u32[]{:S(2)}, u32[]{:S(2)}) %collective-permute-start.10) | collective-permute-done | bytes 4128 | tf_op jit(solution)/shard_map/ppermute | solution.py:28
  46.9 2.6 %collective-permute-start.11 = (f32[8,128]{1,0:T(8,128)S(1)}, f32[8,128]{1,0:T(8,128)S(1)}, u32[]{:S(2)}, u32[]{:S(2)}) collective-permute-start(f32[8,128]{1,0:T(8,128)S(1)} %add.103), channel_id=1, source_target_pairs={{0,16},{4,20},{8,24},{12,28},{16,0},{20,4},{24,8},{28,12},{1,17},{... | collective-permute-start | bytes 12296 | tf_op jit(solution)/shard_map/ppermute | solution.py:28
  49.5 1.3 %collective-permute-start.27 = (bf16[32,1024]{1,0:T(8,128)(2,1)}, bf16[32,1024]{1,0:T(8,128)(2,1)S(1)}, u32[]{:S(2)}, u32[]{:S(2)}) collective-permute-start(bf16[32,1024]{1,0:T(8,128)(2,1)} %doc_sums.1.rest_8_), channel_id=1, source_target_pairs={{0,24},{4,28},{8,16},{12,20},{16,8},{20,12},{24,0},{28,4},{1,25},{... | collective-permute-start | bytes 196616 | tf_op jit(solution)/shard_map/ppermute | solution.py:28
  50.8 0.0 collective-permute-done.14
  50.8 1.7 %collective-permute-start.25 = (bf16[32,1024]{1,0:T(8,128)(2,1)}, bf16[32,1024]{1,0:T(8,128)(2,1)S(1)}, u32[]{:S(2)}, u32[]{:S(2)}) collective-permute-start(bf16[32,1024]{1,0:T(8,128)(2,1)} %doc_sums.1.rest_8_), channel_id=1, source_target_pairs={{0,16},{4,20},{8,24},{12,28},{16,0},{20,4},{24,8},{28,12},{1,17},{... | collective-permute-start | bytes 196616 | tf_op jit(solution)/shard_map/ppermute | solution.py:28
  52.5 0.0 collective-permute-done.13
  52.5 1.4 %collective-permute-start.23 = (bf16[32,1024]{1,0:T(8,128)(2,1)}, bf16[32,1024]{1,0:T(8,128)(2,1)S(1)}, u32[]{:S(2)}, u32[]{:S(2)}) collective-permute-start(bf16[32,1024]{1,0:T(8,128)(2,1)} %doc_sums.1.rest_8_), channel_id=1, source_target_pairs={{0,8},{4,12},{8,0},{12,4},{16,24},{20,28},{24,16},{28,20},{1,9},{5... | collective-permute-start | bytes 196616 | tf_op jit(solution)/shard_map/ppermute | solution.py:28
  53.9 0.0 collective-permute-done.12
  53.9 0.0 collective-permute-start.22
  53.9 0.9 %pad_maximum_fusion = bf16[4,32,1024]{2,1,0:T(8,128)(2,1)S(1)} fusion(bf16[1,32,1024]{2,1,0:T(8,128)(2,1)S(1)} %bitcast.27, bf16[1,32,1024]{2,1,0:T(8,128)(2,1)S(1)} %bitcast.28, bf16[1,32,1024]{2,1,0:T(8,128)(2,1)S(1)} %bitcast.29, bf16[1,32,1024]{2,1,0:T(8,128)(2,1)} %bitcast.25), kind=kLoop, calls=%fused_computation | loop fusion | flops 393216 | bytes 524288 | tf_op jit(solution)/shard_map/stack | solution.py:247
  54.8 0.7 dynamic-slice_bitcast_fusion
  55.5 0.0 collective-permute-done.11
  55.5 1.4 %collective-permute-start.21 = (bf16[32,512]{1,0:T(8,128)(2,1)S(1)}, bf16[32,512]{1,0:T(8,128)(2,1)S(1)}, u32[]{:S(2)}, u32[]{:S(2)}) collective-permute-start(bf16[32,512]{1,0:T(8,128)(2,1)S(1)} %get-tuple-element.18), channel_id=1, source_target_pairs={{0,28},{4,24},{8,20},{12,16},{16,12},{20,8},{24,4},{28,0},{1,29},{... | collective-permute-start | bytes 98312 | tf_op jit(solution)/shard_map/ppermute | solution.py:28
  56.9 0.0 collective-permute-done.27.rest_14_
  56.9 2.5 %collective-permute-start.20 = (bf16[32,512]{1,0:T(8,128)(2,1)S(1)}, bf16[32,512]{1,0:T(8,128)(2,1)S(1)}, u32[]{:S(2)}, u32[]{:S(2)}) collective-permute-start(bf16[32,512]{1,0:T(8,128)(2,1)S(1)} %get-tuple-element.19), channel_id=1, source_target_pairs={{0,24},{4,28},{8,16},{12,20},{16,8},{20,12},{24,0},{28,4},{1,25},{... | collective-permute-start | bytes 98312 | tf_op jit(solution)/shard_map/ppermute | solution.py:28
  59.4 0.0 collective-permute-done.25.rest_12_
  59.4 0.0 collective-permute-start.19
  59.4 2.3 %collective-permute-start.18 = (bf16[32,512]{1,0:T(8,128)(2,1)S(1)}, bf16[32,512]{1,0:T(8,128)(2,1)S(1)}, u32[]{:S(2)}, u32[]{:S(2)}) collective-permute-start(bf16[32,512]{1,0:T(8,128)(2,1)S(1)} %get-tuple-element.21), channel_id=1, source_target_pairs={{0,16},{4,20},{8,24},{12,28},{16,0},{20,4},{24,8},{28,12},{1,17},{... | collective-permute-start | bytes 98312 | tf_op jit(solution)/shard_map/ppermute | solution.py:28
  61.7 0.0 collective-permute-done.22.rest_9_
  61.7 0.0 collective-permute-start.17
  61.7 0.5 collective-permute-start.28
  62.2 0.4 collective-permute-done.20.rest_6_
  62.6 1.3 %collective-permute-done.19.rest_5_ = bf16[32,512]{1,0:T(8,128)(2,1)S(1)} collective-permute-done((bf16[32,512]{1,0:T(8,128)(2,1)S(1)}, bf16[32,512]{1,0:T(8,128)(2,1)S(1)}, u32[]{:S(2)}, u32[]{:S(2)}) %collective-permute-start.19) | collective-permute-done | bytes 32800 | tf_op jit(solution)/shard_map/ppermute | solution.py:28
  63.9 0.0 collective-permute-start.24
  64.0 1.4 %collective-permute-done.18.rest_4_ = bf16[32,512]{1,0:T(8,128)(2,1)S(1)} collective-permute-done((bf16[32,512]{1,0:T(8,128)(2,1)S(1)}, bf16[32,512]{1,0:T(8,128)(2,1)S(1)}, u32[]{:S(2)}, u32[]{:S(2)}) %collective-permute-start.18) | collective-permute-done | bytes 32800 | tf_op jit(solution)/shard_map/ppermute | solution.py:28
  65.3 0.5 collective-permute-start.16
  65.8 0.0 collective-permute-done.17.rest_3_
  65.8 0.6 add.104.total_ref
  66.4 2.8 %collective-permute-done.16.rest_2_ = bf16[32,512]{1,0:T(8,128)(2,1)S(1)} collective-permute-done((bf16[32,512]{1,0:T(8,128)(2,1)S(1)}, bf16[32,512]{1,0:T(8,128)(2,1)S(1)}, u32[]{:S(2)}, u32[]{:S(2)}) %collective-permute-start.16) | collective-permute-done | bytes 32800 | tf_op jit(solution)/shard_map/ppermute | solution.py:28
  69.4 0.5 copy-done.13
  69.8 0.0 copy-done.14
  69.9 0.0 copy-done.4
  69.9 0.0 copy-done.5
  69.9 0.0 copy-done.6
  69.9 4.1 %fisher_block.1 = f32[512,1024]{1,0:T(8,128)} custom-call(f32[8,128]{1,0:T(8,128)} %add.104.total_ref, bf16[32,512]{1,0:T(8,128)(2,1)} %get-tuple-element.25.rest_0_, bf16[32,512]{1,0:T(8,128)(2,1)} %copy-done.14, bf16[32,512]{1,0:T(8,128)(2,1)} %copy-done.13, bf16[32,512]{1,0:T(8,128)(2,1)} %copy-done.12, bf16[32,512]{1,0:T(8,128)(2,1)} %copy-done.11, ...), custom_call_target="tpu_custom_call" | custom-call | flops 268435456 | bytes 2097152 | tf_op jit(solution)/shard_map/fisher_block/pallas_call | solution.py:198
  (51 shorter events, 0.1 us)
Async XLA Ops:
  9.0 17.2 %collective-permute-start.3 = (bf16[64,512]{1,0:T(8,128)(2,1)}, bf16[64,512]{1,0:T(8,128)(2,1)S(1)}, u32[]{:S(2)}, u32[]{:S(2)}) collective-permute-start(bf16[64,512]{1,0:T(8,128)(2,1)} %get-tuple-element.14), channel_id=1, source_target_pairs={{0,1},{1,0},{2,3},{3,2},{4,5},{5,4},{6,7},{7,6},{8,9},{9,8},{10,11... | collective-permute-start | bytes 196616 | tf_op jit(solution)/shard_map/ppermute | solution.py:28
  11.9 14.2 %collective-permute-start.4 = (bf16[64,512]{1,0:T(8,128)(2,1)}, bf16[64,512]{1,0:T(8,128)(2,1)S(1)}, u32[]{:S(2)}, u32[]{:S(2)}) collective-permute-start(bf16[64,512]{1,0:T(8,128)(2,1)} %get-tuple-element.15), channel_id=1, source_target_pairs={{0,2},{1,3},{2,0},{3,1},{4,6},{5,7},{6,4},{7,5},{8,10},{9,11},{10,... | collective-permute-start | bytes 196616 | tf_op jit(solution)/shard_map/ppermute | solution.py:28
  13.4 12.7 %collective-permute-start.5 = (bf16[64,512]{1,0:T(8,128)(2,1)}, bf16[64,512]{1,0:T(8,128)(2,1)S(1)}, u32[]{:S(2)}, u32[]{:S(2)}) collective-permute-start(bf16[64,512]{1,0:T(8,128)(2,1)} %get-tuple-element.16), channel_id=1, source_target_pairs={{0,3},{1,2},{2,1},{3,0},{4,7},{5,6},{6,5},{7,4},{8,11},{9,10},{10,... | collective-permute-start | bytes 196616 | tf_op jit(solution)/shard_map/ppermute | solution.py:28
  19.0 11.6 %collective-permute-start = (bf16[16,2048]{1,0:T(8,128)(2,1)}, bf16[16,2048]{1,0:T(8,128)(2,1)S(1)}, u32[]{:S(2)}, u32[]{:S(2)}) collective-permute-start(bf16[16,2048]{1,0:T(8,128)(2,1)} %get-tuple-element.11), channel_id=1, source_target_pairs={{0,1},{1,0},{2,3},{3,2},{4,5},{5,4},{6,7},{7,6},{8,9},{9,8},{10,11... | collective-permute-start | bytes 196616 | tf_op jit(solution)/shard_map/ppermute | solution.py:28
  21.0 5.1 %copy-start.18 = (bf16[16,2048]{1,0:T(8,128)(2,1)S(1)}, bf16[16,2048]{1,0:T(8,128)(2,1)}, u32[]{:S(2)}) copy-start(bf16[16,2048]{1,0:T(8,128)(2,1)} %get-tuple-element.13) | copy-start | bytes 196612
  21.0 21.1 %copy-start.15 = (f32[8,128]{1,0:T(8,128)S(1)}, f32[8,128]{1,0:T(8,128)}, u32[]{:S(2)}) copy-start(f32[8,128]{1,0:T(8,128)} %get-tuple-element.17) | copy-start | bytes 12292
  21.0 9.7 %collective-permute-start.1 = (bf16[16,2048]{1,0:T(8,128)(2,1)}, bf16[16,2048]{1,0:T(8,128)(2,1)S(1)}, u32[]{:S(2)}, u32[]{:S(2)}) collective-permute-start(bf16[16,2048]{1,0:T(8,128)(2,1)} %get-tuple-element.12), channel_id=1, source_target_pairs={{0,2},{1,3},{2,0},{3,1},{4,6},{5,7},{6,4},{7,5},{8,10},{9,11},{10,... | collective-permute-start | bytes 196616 | tf_op jit(solution)/shard_map/ppermute | solution.py:28
  26.1 5.3 %collective-permute-start.2 = (bf16[16,2048]{1,0:T(8,128)(2,1)S(1)}, bf16[16,2048]{1,0:T(8,128)(2,1)S(1)}, u32[]{:S(2)}, u32[]{:S(2)}) collective-permute-start(bf16[16,2048]{1,0:T(8,128)(2,1)S(1)} %copy-done.18), channel_id=1, source_target_pairs={{0,3},{1,2},{2,1},{3,0},{4,7},{5,6},{6,5},{7,4},{8,11},{9,10},{10,... | collective-permute-start | bytes 196616 | tf_op jit(solution)/shard_map/ppermute | solution.py:28
  27.1 7.8 %copy-start.7 = (bf16[64,512]{1,0:T(8,128)(2,1)}, bf16[64,512]{1,0:T(8,128)(2,1)S(1)}, u32[]{:S(2)}) copy-start(bf16[64,512]{1,0:T(8,128)(2,1)S(1)} %add_convert_fusion.rest_4_) | copy-start | bytes 196612
  27.1 5.8 %collective-permute-start.8 = (bf16[64,512]{1,0:T(8,128)(2,1)S(1)}, bf16[64,512]{1,0:T(8,128)(2,1)S(1)}, u32[]{:S(2)}, u32[]{:S(2)}) collective-permute-start(bf16[64,512]{1,0:T(8,128)(2,1)S(1)} %add_convert_fusion.rest_4_), channel_id=1, source_target_pairs={{0,3},{1,2},{2,1},{3,0},{4,7},{5,6},{6,5},{7,4},{8,11},{9,10},{10,... | collective-permute-start | bytes 196616 | tf_op jit(solution)/shard_map/ppermute | solution.py:28
  30.1 4.3 %collective-permute-start.7 = (bf16[64,512]{1,0:T(8,128)(2,1)S(1)}, bf16[64,512]{1,0:T(8,128)(2,1)S(1)}, u32[]{:S(2)}, u32[]{:S(2)}) collective-permute-start(bf16[64,512]{1,0:T(8,128)(2,1)S(1)} %add_convert_fusion.rest_4_), channel_id=1, source_target_pairs={{0,2},{1,3},{2,0},{3,1},{4,6},{5,7},{6,4},{7,5},{8,10},{9,11},{10,... | collective-permute-start | bytes 196616 | tf_op jit(solution)/shard_map/ppermute | solution.py:28
  30.6 4.3 %copy-start.16 = (bf16[16,2048]{1,0:T(8,128)(2,1)}, bf16[16,2048]{1,0:T(8,128)(2,1)S(1)}, u32[]{:S(2)}) copy-start(bf16[16,2048]{1,0:T(8,128)(2,1)S(1)} %collective-permute-done.rest_1_) | copy-start | bytes 196612
  30.6 4.3 %collective-permute-start.6 = (bf16[64,512]{1,0:T(8,128)(2,1)S(1)}, bf16[64,512]{1,0:T(8,128)(2,1)S(1)}, u32[]{:S(2)}, u32[]{:S(2)}) collective-permute-start(bf16[64,512]{1,0:T(8,128)(2,1)S(1)} %add_convert_fusion.rest_4_), channel_id=1, source_target_pairs={{0,1},{1,0},{2,3},{3,2},{4,5},{5,4},{6,7},{7,6},{8,9},{9,8},{10,11... | collective-permute-start | bytes 196616 | tf_op jit(solution)/shard_map/ppermute | solution.py:28
  30.7 4.1 %copy-start.17 = (bf16[16,2048]{1,0:T(8,128)(2,1)}, bf16[16,2048]{1,0:T(8,128)(2,1)S(1)}, u32[]{:S(2)}) copy-start(bf16[16,2048]{1,0:T(8,128)(2,1)S(1)} %collective-permute-done.1.rest_2_) | copy-start | bytes 196612
  31.4 3.5 %copy-start.19 = (bf16[16,2048]{1,0:T(8,128)(2,1)}, bf16[16,2048]{1,0:T(8,128)(2,1)S(1)}, u32[]{:S(2)}) copy-start(bf16[16,2048]{1,0:T(8,128)(2,1)S(1)} %collective-permute-done.2.rest_3_) | copy-start | bytes 196612
  33.0 1.9 %copy-start.20 = (bf16[64,512]{1,0:T(8,128)(2,1)}, bf16[64,512]{1,0:T(8,128)(2,1)S(1)}, u32[]{:S(2)}) copy-start(bf16[64,512]{1,0:T(8,128)(2,1)S(1)} %collective-permute-done.8.rest_7_) | copy-start | bytes 196612
  34.3 0.6 copy-start.21
  34.9 0.6 copy-start.22
  38.6 12.2 %collective-permute-start.14 = (bf16[32,1024]{1,0:T(8,128)(2,1)}, bf16[32,1024]{1,0:T(8,128)(2,1)S(1)}, u32[]{:S(2)}, u32[]{:S(2)}) collective-permute-start(bf16[32,1024]{1,0:T(8,128)(2,1)} %doc_sums.1.rest_8_), channel_id=1, source_target_pairs={{0,3},{1,2},{2,1},{3,0},{4,7},{5,6},{6,5},{7,4},{8,11},{9,10},{10,... | collective-permute-start | bytes 196616 | tf_op jit(solution)/shard_map/ppermute | solution.py:28
  40.1 12.4 %collective-permute-start.13 = (bf16[32,1024]{1,0:T(8,128)(2,1)}, bf16[32,1024]{1,0:T(8,128)(2,1)S(1)}, u32[]{:S(2)}, u32[]{:S(2)}) collective-permute-start(bf16[32,1024]{1,0:T(8,128)(2,1)} %doc_sums.1.rest_8_), channel_id=1, source_target_pairs={{0,2},{1,3},{2,0},{3,1},{4,6},{5,7},{6,4},{7,5},{8,10},{9,11},{10,... | collective-permute-start | bytes 196616 | tf_op jit(solution)/shard_map/ppermute | solution.py:28
  40.3 13.6 %collective-permute-start.12 = (bf16[32,1024]{1,0:T(8,128)(2,1)}, bf16[32,1024]{1,0:T(8,128)(2,1)S(1)}, u32[]{:S(2)}, u32[]{:S(2)}) collective-permute-start(bf16[32,1024]{1,0:T(8,128)(2,1)} %doc_sums.1.rest_8_), channel_id=1, source_target_pairs={{0,1},{1,0},{2,3},{3,2},{4,5},{5,4},{6,7},{7,6},{8,9},{9,8},{10,11... | collective-permute-start | bytes 196616 | tf_op jit(solution)/shard_map/ppermute | solution.py:28
  42.1 1.2 %collective-permute-start.9 = (f32[8,128]{1,0:T(8,128)S(1)}, f32[8,128]{1,0:T(8,128)S(1)}, u32[]{:S(2)}, u32[]{:S(2)}) collective-permute-start(f32[8,128]{1,0:T(8,128)S(1)} %copy-done.15), channel_id=1, source_target_pairs={{0,4},{4,0},{8,12},{12,8},{16,20},{20,16},{24,28},{28,24},{1,5},{5... | collective-permute-start | bytes 12296 | tf_op jit(solution)/shard_map/ppermute | solution.py:28
  43.3 3.6 %collective-permute-start.10 = (f32[8,128]{1,0:T(8,128)S(1)}, f32[8,128]{1,0:T(8,128)S(1)}, u32[]{:S(2)}, u32[]{:S(2)}) collective-permute-start(f32[8,128]{1,0:T(8,128)S(1)} %add.102), channel_id=1, source_target_pairs={{0,8},{4,12},{8,0},{12,4},{16,24},{20,28},{24,16},{28,20},{1,9},{5... | collective-permute-start | bytes 12296 | tf_op jit(solution)/shard_map/ppermute | solution.py:28
  46.9 8.6 %collective-permute-start.11 = (f32[8,128]{1,0:T(8,128)S(1)}, f32[8,128]{1,0:T(8,128)S(1)}, u32[]{:S(2)}, u32[]{:S(2)}) collective-permute-start(f32[8,128]{1,0:T(8,128)S(1)} %add.103), channel_id=1, source_target_pairs={{0,16},{4,20},{8,24},{12,28},{16,0},{20,4},{24,8},{28,12},{1,17},{... | collective-permute-start | bytes 12296 | tf_op jit(solution)/shard_map/ppermute | solution.py:28
  49.5 7.4 %collective-permute-start.27 = (bf16[32,1024]{1,0:T(8,128)(2,1)}, bf16[32,1024]{1,0:T(8,128)(2,1)S(1)}, u32[]{:S(2)}, u32[]{:S(2)}) collective-permute-start(bf16[32,1024]{1,0:T(8,128)(2,1)} %doc_sums.1.rest_8_), channel_id=1, source_target_pairs={{0,24},{4,28},{8,16},{12,20},{16,8},{20,12},{24,0},{28,4},{1,25},{... | collective-permute-start | bytes 196616 | tf_op jit(solution)/shard_map/ppermute | solution.py:28
  50.8 8.5 %collective-permute-start.25 = (bf16[32,1024]{1,0:T(8,128)(2,1)}, bf16[32,1024]{1,0:T(8,128)(2,1)S(1)}, u32[]{:S(2)}, u32[]{:S(2)}) collective-permute-start(bf16[32,1024]{1,0:T(8,128)(2,1)} %doc_sums.1.rest_8_), channel_id=1, source_target_pairs={{0,16},{4,20},{8,24},{12,28},{16,0},{20,4},{24,8},{28,12},{1,17},{... | collective-permute-start | bytes 196616 | tf_op jit(solution)/shard_map/ppermute | solution.py:28
  52.5 6.9 %collective-permute-start.23 = (bf16[32,1024]{1,0:T(8,128)(2,1)}, bf16[32,1024]{1,0:T(8,128)(2,1)S(1)}, u32[]{:S(2)}, u32[]{:S(2)}) collective-permute-start(bf16[32,1024]{1,0:T(8,128)(2,1)} %doc_sums.1.rest_8_), channel_id=1, source_target_pairs={{0,8},{4,12},{8,0},{12,4},{16,24},{20,28},{24,16},{28,20},{1,9},{5... | collective-permute-start | bytes 196616 | tf_op jit(solution)/shard_map/ppermute | solution.py:28
  53.9 7.8 %collective-permute-start.22 = (bf16[32,1024]{1,0:T(8,128)(2,1)}, bf16[32,1024]{1,0:T(8,128)(2,1)S(1)}, u32[]{:S(2)}, u32[]{:S(2)}) collective-permute-start(bf16[32,1024]{1,0:T(8,128)(2,1)} %doc_sums.1.rest_8_), channel_id=1, source_target_pairs={{0,4},{4,0},{8,12},{12,8},{16,20},{20,16},{24,28},{28,24},{1,5},{5... | collective-permute-start | bytes 196616 | tf_op jit(solution)/shard_map/ppermute | solution.py:28
  55.5 6.2 %collective-permute-start.21 = (bf16[32,512]{1,0:T(8,128)(2,1)S(1)}, bf16[32,512]{1,0:T(8,128)(2,1)S(1)}, u32[]{:S(2)}, u32[]{:S(2)}) collective-permute-start(bf16[32,512]{1,0:T(8,128)(2,1)S(1)} %get-tuple-element.18), channel_id=1, source_target_pairs={{0,28},{4,24},{8,20},{12,16},{16,12},{20,8},{24,4},{28,0},{1,29},{... | collective-permute-start | bytes 98312 | tf_op jit(solution)/shard_map/ppermute | solution.py:28
  56.9 12.4 %copy-start = (bf16[32,1024]{1,0:T(8,128)(2,1)}, bf16[32,1024]{1,0:T(8,128)(2,1)S(1)}, u32[]{:S(2)}) copy-start(bf16[32,1024]{1,0:T(8,128)(2,1)S(1)} %collective-permute-done.27.rest_14_) | copy-start | bytes 196612
  56.9 5.7 %collective-permute-start.20 = (bf16[32,512]{1,0:T(8,128)(2,1)S(1)}, bf16[32,512]{1,0:T(8,128)(2,1)S(1)}, u32[]{:S(2)}, u32[]{:S(2)}) collective-permute-start(bf16[32,512]{1,0:T(8,128)(2,1)S(1)} %get-tuple-element.19), channel_id=1, source_target_pairs={{0,24},{4,28},{8,16},{12,20},{16,8},{20,12},{24,0},{28,4},{1,25},{... | collective-permute-start | bytes 98312 | tf_op jit(solution)/shard_map/ppermute | solution.py:28
  59.4 9.9 %copy-start.1 = (bf16[32,1024]{1,0:T(8,128)(2,1)}, bf16[32,1024]{1,0:T(8,128)(2,1)S(1)}, u32[]{:S(2)}) copy-start(bf16[32,1024]{1,0:T(8,128)(2,1)S(1)} %collective-permute-done.25.rest_12_) | copy-start | bytes 196612
  59.4 4.5 %collective-permute-start.19 = (bf16[32,512]{1,0:T(8,128)(2,1)S(1)}, bf16[32,512]{1,0:T(8,128)(2,1)S(1)}, u32[]{:S(2)}, u32[]{:S(2)}) collective-permute-start(bf16[32,512]{1,0:T(8,128)(2,1)S(1)} %get-tuple-element.20), channel_id=1, source_target_pairs={{0,20},{4,16},{8,28},{12,24},{16,4},{20,0},{24,12},{28,8},{1,21},{... | collective-permute-start | bytes 98312 | tf_op jit(solution)/shard_map/ppermute | solution.py:28
  59.4 9.9 %copy-start.2 = (bf16[32,1024]{1,0:T(8,128)(2,1)}, bf16[32,1024]{1,0:T(8,128)(2,1)S(1)}, u32[]{:S(2)}) copy-start(bf16[32,1024]{1,0:T(8,128)(2,1)S(1)} %collective-permute-done.23.rest_10_) | copy-start | bytes 196612
  59.4 5.9 %collective-permute-start.18 = (bf16[32,512]{1,0:T(8,128)(2,1)S(1)}, bf16[32,512]{1,0:T(8,128)(2,1)S(1)}, u32[]{:S(2)}, u32[]{:S(2)}) collective-permute-start(bf16[32,512]{1,0:T(8,128)(2,1)S(1)} %get-tuple-element.21), channel_id=1, source_target_pairs={{0,16},{4,20},{8,24},{12,28},{16,0},{20,4},{24,8},{28,12},{1,17},{... | collective-permute-start | bytes 98312 | tf_op jit(solution)/shard_map/ppermute | solution.py:28
  61.7 7.6 %copy-start.3 = (bf16[32,1024]{1,0:T(8,128)(2,1)}, bf16[32,1024]{1,0:T(8,128)(2,1)S(1)}, u32[]{:S(2)}) copy-start(bf16[32,1024]{1,0:T(8,128)(2,1)S(1)} %collective-permute-done.22.rest_9_) | copy-start | bytes 196612
  61.7 4.2 %collective-permute-start.17 = (bf16[32,512]{1,0:T(8,128)(2,1)S(1)}, bf16[32,512]{1,0:T(8,128)(2,1)S(1)}, u32[]{:S(2)}, u32[]{:S(2)}) collective-permute-start(bf16[32,512]{1,0:T(8,128)(2,1)S(1)} %get-tuple-element.22), channel_id=1, source_target_pairs={{0,12},{4,8},{8,4},{12,0},{16,28},{20,24},{24,20},{28,16},{1,13},{... | collective-permute-start | bytes 98312 | tf_op jit(solution)/shard_map/ppermute | solution.py:28
  61.7 7.6 %copy-start.8 = (bf16[32,512]{1,0:T(8,128)(2,1)}, bf16[32,512]{1,0:T(8,128)(2,1)S(1)}, u32[]{:S(2)}) copy-start(bf16[32,512]{1,0:T(8,128)(2,1)S(1)} %collective-permute-done.21.rest_7_) | copy-start | bytes 98308
  61.7 7.5 %collective-permute-start.28 = (bf16[32,1024]{1,0:T(8,128)(2,1)S(1)}, bf16[32,1024]{1,0:T(8,128)(2,1)S(1)}, u32[]{:S(2)}, u32[]{:S(2)}) collective-permute-start(bf16[32,1024]{1,0:T(8,128)(2,1)S(1)} %collective-permute-done.27.rest_14_), channel_id=1, source_target_pairs={{0,4},{4,0},{8,12},{12,8},{16,20},{20,16},{24,28},{28,24},{1,5},{5... | collective-permute-start | bytes 196616 | tf_op jit(solution)/shard_map/ppermute | solution.py:28
  62.6 6.7 %copy-start.9 = (bf16[32,512]{1,0:T(8,128)(2,1)}, bf16[32,512]{1,0:T(8,128)(2,1)S(1)}, u32[]{:S(2)}) copy-start(bf16[32,512]{1,0:T(8,128)(2,1)S(1)} %collective-permute-done.20.rest_6_) | copy-start | bytes 98308
  62.6 6.6 %collective-permute-start.26 = (bf16[32,1024]{1,0:T(8,128)(2,1)S(1)}, bf16[32,1024]{1,0:T(8,128)(2,1)S(1)}, u32[]{:S(2)}, u32[]{:S(2)}) collective-permute-start(bf16[32,1024]{1,0:T(8,128)(2,1)S(1)} %collective-permute-done.25.rest_12_), channel_id=1, source_target_pairs={{0,4},{4,0},{8,12},{12,8},{16,20},{20,16},{24,28},{28,24},{1,5},{5... | collective-permute-start | bytes 196616 | tf_op jit(solution)/shard_map/ppermute | solution.py:28
  63.9 5.4 %copy-start.10 = (bf16[32,512]{1,0:T(8,128)(2,1)}, bf16[32,512]{1,0:T(8,128)(2,1)S(1)}, u32[]{:S(2)}) copy-start(bf16[32,512]{1,0:T(8,128)(2,1)S(1)} %collective-permute-done.19.rest_5_) | copy-start | bytes 98308
  63.9 5.4 %collective-permute-start.24 = (bf16[32,1024]{1,0:T(8,128)(2,1)S(1)}, bf16[32,1024]{1,0:T(8,128)(2,1)S(1)}, u32[]{:S(2)}, u32[]{:S(2)}) collective-permute-start(bf16[32,1024]{1,0:T(8,128)(2,1)S(1)} %collective-permute-done.23.rest_10_), channel_id=1, source_target_pairs={{0,4},{4,0},{8,12},{12,8},{16,20},{20,16},{24,28},{28,24},{1,5},{5... | collective-permute-start | bytes 196616 | tf_op jit(solution)/shard_map/ppermute | solution.py:28
  65.3 4.1 %copy-start.11 = (bf16[32,512]{1,0:T(8,128)(2,1)}, bf16[32,512]{1,0:T(8,128)(2,1)S(1)}, u32[]{:S(2)}) copy-start(bf16[32,512]{1,0:T(8,128)(2,1)S(1)} %collective-permute-done.18.rest_4_) | copy-start | bytes 98308
  65.3 3.9 %collective-permute-start.16 = (bf16[32,512]{1,0:T(8,128)(2,1)S(1)}, bf16[32,512]{1,0:T(8,128)(2,1)S(1)}, u32[]{:S(2)}, u32[]{:S(2)}) collective-permute-start(bf16[32,512]{1,0:T(8,128)(2,1)S(1)} %get-tuple-element.23), channel_id=1, source_target_pairs={{0,8},{4,12},{8,0},{12,4},{16,24},{20,28},{24,16},{28,20},{1,9},{5... | collective-permute-start | bytes 98312 | tf_op jit(solution)/shard_map/ppermute | solution.py:28
  65.8 3.5 %copy-start.12 = (bf16[32,512]{1,0:T(8,128)(2,1)}, bf16[32,512]{1,0:T(8,128)(2,1)S(1)}, u32[]{:S(2)}) copy-start(bf16[32,512]{1,0:T(8,128)(2,1)S(1)} %collective-permute-done.17.rest_3_) | copy-start | bytes 98308
  65.8 3.4 %collective-permute-start.15 = (bf16[32,512]{1,0:T(8,128)(2,1)S(1)}, bf16[32,512]{1,0:T(8,128)(2,1)S(1)}, u32[]{:S(2)}, u32[]{:S(2)}) collective-permute-start(bf16[32,512]{1,0:T(8,128)(2,1)S(1)} %get-tuple-element.24), channel_id=1, source_target_pairs={{0,4},{4,0},{8,12},{12,8},{16,20},{20,16},{24,28},{28,24},{1,5},{5... | collective-permute-start | bytes 98312 | tf_op jit(solution)/shard_map/ppermute | solution.py:28
  69.2 0.6 copy-start.13
  69.2 0.6 copy-start.14
  69.2 0.6 copy-start.4
  69.3 0.7 copy-start.5
  69.3 0.7 copy-start.6

commit v2 on v0

v2 whole, which is shorter than its diff:
```python
import functools

import jax
import jax.numpy as jnp
from jax import lax
from jax.experimental import pallas as pl
from jax.experimental.pallas import tpu as pltpu
from jax.sharding import PartitionSpec as P

BF16 = jnp.bfloat16
F32 = jnp.float32
NT = (((1,), (1,)), ((), ()))
TN = (((0,), (0,)), ((), ()))
SMEM = pl.BlockSpec(memory_space=pltpu.SMEM)
VMEM = pl.BlockSpec(memory_space=pltpu.VMEM)
DIGITS = (65536, 256, 1)
DIGIT_ROWS = 8


def swap(value, axis, step):
    return lax.ppermute(value, axis, [(i, i ^ step) for i in range(lax.axis_size(axis))])


def peers_kernel(pos_ref, acts_ref, grads_ref, proj_in_ref, proj_out_ref, *rest):
    outs, own_ref, weights = rest[:-2], rest[-2], rest[-1]
    size = len(outs) + 1
    step = pl.program_id(0)
    rank = proj_out_ref.shape[0]
    part = rank // size

    @pl.when(step == 0)
    def _():
        row = lax.broadcasted_iota(jnp.int32, (rank, rank), 0)
        col = lax.broadcasted_iota(jnp.int32, (rank, rank), 1)
        source = (pos_ref[0] ^ (row // part)) * part + row % part
        pick = jnp.where(col == source, 1.0, 0.0).astype(BF16)
        weights[...] = jnp.dot(pick, proj_out_ref[...], preferred_element_type=F32).astype(BF16)

    dy = lax.dot_general(weights[...], grads_ref[...], NT, preferred_element_type=F32)
    for n in range(size):

        @pl.when(step == n)
        def _():
            lines = slice(n * part, (n + 1) * part)
            own_ref[lines, :] = dy[:part, :]
            for k in range(1, size):
                lines = slice(rank + n * part, rank + (n + 1) * part)
                outs[k - 1][lines, :] = dy[k * part : (k + 1) * part, :].astype(BF16)
            if n + 1 < size:
                x = lax.dot_general(
                    proj_in_ref[...], acts_ref[...], NT, preferred_element_type=F32
                )
                outs[n][:rank, :] = x.astype(BF16)


def peer_messages(pos, acts, grads, proj_in_t, proj_out_t, size):
    tokens, acts_width = acts.shape
    grads_width = grads.shape[1]
    rank = proj_in_t.shape[0]
    chunk = tokens // size
    whole = lambda n, p: (0, 0)
    outs = [jax.ShapeDtypeStruct((2 * rank, chunk), BF16)] * (size - 1)
    outs += [jax.ShapeDtypeStruct((rank, chunk), F32)]
    return pl.pallas_call(
        peers_kernel,
        grid_spec=pltpu.PrefetchScalarGridSpec(
            num_scalar_prefetch=1,
            grid=(size,),
            in_specs=[
                pl.BlockSpec(
                    (chunk, acts_width), lambda n, p: (p[0] ^ jnp.minimum(n + 1, size - 1), 0)
                ),
                pl.BlockSpec((chunk, grads_width), lambda n, p: (n, 0)),
                pl.BlockSpec((rank, acts_width), whole),
                pl.BlockSpec((rank, grads_width), whole),
            ],
            out_specs=[pl.BlockSpec(o.shape, whole) for o in outs],
            scratch_shapes=[pltpu.VMEM((rank, grads_width), BF16)],
        ),
        out_shape=outs,
        cost_estimate=pl.CostEstimate(
            flops=2 * tokens * rank * (acts_width + grads_width),
            bytes_accessed=2 * tokens * (acts_width + grads_width),
            transcendentals=0,
        ),
        name="peer_messages",
    )(pos, acts, grads, proj_in_t, proj_out_t)


def own_kernel(pos_ref, acts_ref, proj_ref, out_ref):
    out_ref[...] = lax.dot_general(proj_ref[...], acts_ref[...], NT, preferred_element_type=F32)


def own_partial(pos, acts, proj_t, size):
    tokens, width = acts.shape
    rank = proj_t.shape[0]
    chunk = tokens // size
    tile = min(256, chunk)
    tiles = chunk // tile
    return pl.pallas_call(
        own_kernel,
        grid_spec=pltpu.PrefetchScalarGridSpec(
            num_scalar_prefetch=1,
            grid=(tiles,),
            in_specs=[
                pl.BlockSpec((tile, width), lambda n, p: (p[0] * tiles + n, 0)),
                pl.BlockSpec((rank, width), lambda n, p: (0, 0)),
            ],
            out_specs=pl.BlockSpec((rank, tile), lambda n, p: (0, n)),
        ),
        out_shape=jax.ShapeDtypeStruct((rank, chunk), F32),
        cost_estimate=pl.CostEstimate(
            flops=2 * chunk * width * rank, bytes_accessed=2 * chunk * width, transcendentals=0
        ),
        name="own_partial",
    )(pos, acts, proj_t)


def docs_kernel(size, pos_ref, counts_ref, seg_ref, dy_own_ref, *rest):
    messages, xs = rest[: size - 1], rest[size - 1 : 2 * size - 1]
    grads_ref, shared_ref, dy_ref, sums_ref = rest[2 * size - 1 :]
    docs, tokens = seg_ref.shape
    rank, chunk = xs[0].shape
    part = rank // size
    rows = dy_ref.shape[0] // size
    total = dy_own_ref[...]
    for message in messages:
        total = total + message[rank:, :].astype(F32)
    for n in range(size):
        lines = total[n * part : (n + 1) * part, :]
        if rows > part:
            lines = jnp.concatenate([lines, jnp.zeros((rows - part, chunk), F32)], axis=0)
        dy_ref[n * rows : (n + 1) * rows, :] = lines
    sums = jnp.zeros((docs * rows, rank), F32)
    doc = lax.broadcasted_iota(jnp.int32, (docs, chunk), 0)
    live_tokens = jnp.zeros((docs, chunk), jnp.int32)
    for k in range(size):
        block = pos_ref[0] ^ k
        cols = pl.ds(pl.multiple_of(block * chunk, chunk), chunk)
        seg = jnp.where(doc < counts_ref[0], seg_ref[:, cols], 0)
        live_tokens = live_tokens + seg
        seg = seg.astype(F32).astype(BF16)
        dy = dy_ref[pl.ds(pl.multiple_of(block * rows, rows), rows), :]
        high = dy.astype(BF16)
        low = (dy - high.astype(F32)).astype(BF16)
        for piece in (high, low):
            masked = (seg[:, None, :] * piece[None, :, :]).reshape(docs * rows, chunk)
            sums = sums + lax.dot_general(masked, xs[k][...], NT, preferred_element_type=F32)
    sums_ref[...] = sums
    lanes = 128 // rank
    for a in range(0, part, lanes):
        pieces = [sums_ref[pl.ds(a + n, docs, stride=rows), :] for n in range(lanes)]
        wide = pieces[0] if lanes == 1 else jnp.concatenate(pieces, axis=1)
        wide = wide.astype(BF16)
        grads_ref[:, a * rank : (a + lanes) * rank] = wide
        shared_ref[:docs, a * rank : (a + lanes) * rank] = wide
    left = jnp.sum(live_tokens)
    row = lax.broadcasted_iota(jnp.int32, (DIGIT_ROWS, part * rank), 0)
    digits = jnp.zeros(row.shape, jnp.int32)
    for n, unit in enumerate(DIGITS):
        digit = left // unit
        left = left - digit * unit
        digits = jnp.where(row == n, digit, digits)
    shared_ref[docs:, :] = digits.astype(F32).astype(BF16)


def doc_sums(pos, counts, seg, dy_own, messages, xs):
    size = len(xs)
    docs, tokens = seg.shape
    rank, chunk = xs[0].shape
    part = rank // size
    rows = -(-part // 16) * 16
    return pl.pallas_call(
        functools.partial(docs_kernel, size),
        in_specs=[SMEM, SMEM] + [VMEM] * (1 + 2 * size),
        out_specs=[VMEM, VMEM],
        out_shape=[
            jax.ShapeDtypeStruct((docs, part * rank), BF16),
            jax.ShapeDtypeStruct((docs + DIGIT_ROWS, part * rank), BF16),
        ],
        scratch_shapes=[
            pltpu.VMEM((rows * size, chunk), F32),
            pltpu.VMEM((docs * rows, rank), F32),
        ],
        cost_estimate=pl.CostEstimate(
            flops=4 * docs * rows * tokens * rank, bytes_accessed=1 << 20, transcendentals=0
        ),
        name="doc_sums",
    )(pos, counts, seg, dy_own, *messages, *xs)


def fisher_kernel(shards, half_ref, *rest):
    rows, cols, out_ref = rest[:shards], rest[shards : 2 * shards], rest[2 * shards]
    docs = rows[0].shape[0]
    left = jnp.concatenate([r[...] for r in rows], axis=0)
    right = jnp.concatenate([c[:docs, :] for c in cols], axis=0)
    product = lax.dot_general(left, right, TN, preferred_element_type=F32)
    total = jnp.zeros((1, 1), F32)
    for c in cols:
        digits = c[docs:, 0:1].astype(F32)
        for n, unit in enumerate(DIGITS):
            total = total + digits[n : n + 1, :] * float(unit)
    out_ref[...] = product / total


def fisher_block(half, rows, cols):
    shards = len(rows)
    docs, width = rows[0].shape
    height = width // 2
    tile = min(128, height)
    tiles = height // tile
    return pl.pallas_call(
        functools.partial(fisher_kernel, shards),
        grid_spec=pltpu.PrefetchScalarGridSpec(
            num_scalar_prefetch=1,
            grid=(tiles,),
            in_specs=[pl.BlockSpec((docs, tile), lambda i, h: (0, h[0] * tiles + i))] * shards
            + [pl.BlockSpec((docs + DIGIT_ROWS, width), lambda i, h: (0, 0))] * shards,
            out_specs=pl.BlockSpec((tile, width), lambda i, h: (i, 0)),
        ),
        out_shape=jax.ShapeDtypeStruct((height, width), F32),
        cost_estimate=pl.CostEstimate(
            flops=2 * docs * shards * height * width,
            bytes_accessed=4 * height * width,
            transcendentals=0,
        ),
        name="fisher_block",
    )(half, *rows, *cols)


def per_device(hidden_acts, out_grads, proj_in, proj_out, segments, doc_counts):
    size, dp_size = lax.axis_size("tensor"), lax.axis_size("dp")
    assert dp_size == 2 * size
    pos = lax.axis_index("tensor").astype(jnp.int32)
    shard = lax.axis_index("dp").astype(jnp.int32)
    pair, half = shard // 2, shard % 2
    steps = range(1, size)
    pos1, half1 = pos.reshape(1), half.reshape(1)

    proj_in_t = proj_in.T
    *messages, dy_own = peer_messages(pos1, hidden_acts, out_grads, proj_in_t, proj_out.T, size)
    messages = [swap(messages[k - 1], "tensor", k) for k in steps]
    x = own_partial(pos1, hidden_acts, proj_in_t, size)
    rank = x.shape[0]
    for message in messages:
        x = x + message[:rank].astype(F32)
    x = x.astype(BF16)
    xs = [x] + [swap(x, "tensor", k) for k in steps]
    grads, shared = doc_sums(pos1, doc_counts, segments, dy_own, messages, xs)

    cols = {0: shared}
    for j in steps:
        low = j & -j
        cols[j] = swap(cols[j - low] if j != low else shared, "dp", 2 * low)
    blocks = [grads] + [swap(grads, "tensor", k) for k in steps]
    rows = []
    for j in range(size):
        where = pos ^ pair ^ j
        picked = blocks[0]
        for k in steps:
            picked = jnp.where(where == k, blocks[k], picked)
        rows.append(picked if j == 0 else swap(picked, "dp", 2 * j))
    cols = [cols[j] for j in range(size)]
    cols += [swap(c, "dp", 1) for c in cols]
    rows += [swap(r, "dp", 1) for r in rows]
    return grads, fisher_block(half1, rows, cols)


def solution(mesh):
    return jax.shard_map(
        per_device,
        mesh=mesh,
        in_specs=(
            P("dp", "tensor"),
            P("dp", "tensor"),
            P("tensor", None),
            P("tensor", None),
            P(None, "dp"),
            P("dp"),
        ),
        out_specs=(P("dp", "tensor"), P("dp", "tensor")),
        check_vma=False,
    )
```

time: 138 us -> 60.5 us (0.44)
  waiting for transfers between devices: 53.9 us -> 10.3 us
  blocking collectives: 32.7 us -> 0 us
  matrix products: 21 us -> 0 us
  Pallas kernels: 0 us -> 20.7 us
  starting transfers between devices: 4.65 us -> 24.5 us
  between operations: 15.4 us -> 1.53 us
  other arithmetic: 8.34 us -> 1.91 us
    psum x1 -> x0, waiting for transfers between devices: 53.9 us -> none  [per_device(): stacked = lax.psum(partial_proj, 'tensor')]
    ppermute x0 -> x23, starting transfers between devices: none -> 24.5 us  [swap(): lax.ppermute(value, axis, [(i, i ^ step) for i in range(lax.axis_size(axi...]
    dot_general x7 -> x0, matrix products: 21 us -> none  [the longest x1 9.71 us: per_device(): x_part = jnp.dot(hidden_acts, proj_in, preferred_element_type=jnp.float32)]
    pallas_call x0 -> x4, Pallas kernels: none -> 20.7 us  [the longest x1 9.58 us: peer_messages(): pl.pallas_call(peers_kernel, grid_spec=pltpu.PrefetchScalarGridSpec(num_s...]
    psum x1 -> x0, blocking collectives: 17.8 us -> none  [per_device(): total_tokens = lax.psum(local_tokens, 'dp')]
    all_gather x1 -> x0, blocking collectives: 14.9 us -> none  [per_device(): lax.all_gather(col_block, 'dp', axis=0, tiled=True)]
    ppermute x0 -> x23, waiting for transfers between devices: none -> 10.3 us  [swap(): lax.ppermute(value, axis, [(i, i ^ step) for i in range(lax.axis_size(axi...]
    convert_element_type x3 -> x1, other arithmetic: 6.53 us -> 1.03 us  [per_device(): x = x.astype(BF16)]
  transfers between devices with their start and end apart: 2 -> 23, of which waited for: 1 -> 10; matrix products, arithmetic and copies ran while one was open for 1% -> 1% of each run, Pallas kernels for 0% -> 6%
where the time goes in v2:
time: 60.5 us; the launch traced here: 60.1 us
  starting transfers between devices  24.5 us (40%)
  Pallas kernels  20.7 us (34%)
  waiting for transfers between devices  10.3 us (17%)
  other arithmetic  1.91 us (3%)
  between operations  1.53 us (3%)
  local copies, waits for them, and re-layouts  1.19 us (2%)
    ppermute x23, starting transfers between devices, swap(): lax.ppermute(value, axis, [(i, i ^ step) for i in range(lax.axis_size(axi...  24.5 us
    ppermute x23, waiting for transfers between devices, swap(): lax.ppermute(value, axis, [(i, i ^ step) for i in range(lax.axis_size(axi...  10.3 us
    pallas_call x1, Pallas kernels, peer_messages(): pl.pallas_call(peers_kernel, grid_spec=pltpu.PrefetchScalarGridSpec(num_s...  9.58 us
    pallas_call x1, Pallas kernels, fisher_block(): pl.pallas_call(functools.partial(fisher_kernel, shards), grid_spec=pltpu....  4.28 us
    pallas_call x1, Pallas kernels, own_partial(): pl.pallas_call(own_kernel, grid_spec=pltpu.PrefetchScalarGridSpec(num_sca...  3.57 us
    pallas_call x1, Pallas kernels, doc_sums(): pl.pallas_call(functools.partial(docs_kernel, size), in_specs=[SMEM, SMEM...  3.25 us
  transfers between devices with their start and end apart: 23, of which 10 were waited for; matrix products, arithmetic and copies ran while one was open for 1% of the time, Pallas kernels for 6%

profile of v2, /device:TPU:0, one launch (start us, length us, event | category | flops | bytes accessed | tf_op | source)
XLA Modules:
  0.0 60.1 jit_solution(9806088033847378925)
XLA Ops:
  0.6 9.6 %peer_messages.1 = (bf16[128,512]{1,0:T(8,128)(2,1)}, bf16[128,512]{1,0:T(8,128)(2,1)}, bf16[128,512]{1,0:T(8,128)(2,1)}, f32[64,512]{1,0:T(8,128)}) custom-call(s32[1]{0:T(128)} %bitcast.pos_ref, bf16[2048,3584]{1,0:T(8,128)(2,1)} %acts_ref.3, bf16[2048,1024]{1,0:T(8,128)(2,1)} %grads_ref.1, bf16[64,3584]{1,0:T(8,128)(2,1)} %bitcast.4, bf16[64,1024]{1,0:T(8,128)(2,1)} %bitcast.6), custom_call_target="tpu_custom_call" | custom-call | flops 1207959552 | bytes 18874368 | tf_op jit(solution)/shard_map/peer_messages/pallas_call | solution.py:64
  10.2 3.0 %collective-permute-start = (bf16[128,512]{1,0:T(8,128)(2,1)}, bf16[128,512]{1,0:T(8,128)(2,1)S(1)}, u32[]{:S(2)}, u32[]{:S(2)}) collective-permute-start(bf16[128,512]{1,0:T(8,128)(2,1)} %get-tuple-element.9), channel_id=1, source_target_pairs={{0,1},{1,0},{2,3},{3,2},{4,5},{5,4},{6,7},{7,6},{8,9},{9,8},{10,11... | collective-permute-start | bytes 393224 | tf_op jit(solution)/shard_map/ppermute | solution.py:21
  13.2 1.5 %collective-permute-start.1 = (bf16[128,512]{1,0:T(8,128)(2,1)}, bf16[128,512]{1,0:T(8,128)(2,1)S(1)}, u32[]{:S(2)}, u32[]{:S(2)}) collective-permute-start(bf16[128,512]{1,0:T(8,128)(2,1)} %get-tuple-element.10), channel_id=1, source_target_pairs={{0,2},{1,3},{2,0},{3,1},{4,6},{5,7},{6,4},{7,5},{8,10},{9,11},{10,... | collective-permute-start | bytes 393224 | tf_op jit(solution)/shard_map/ppermute | solution.py:21
  14.7 0.0 collective-permute-start.2
  14.7 3.6 %own_partial.1 = f32[64,512]{1,0:T(8,128)} custom-call(s32[1]{0:T(128)} %bitcast.pos_ref, bf16[2048,3584]{1,0:T(8,128)(2,1)} %acts_ref.3, bf16[64,3584]{1,0:T(8,128)(2,1)} %bitcast.5), custom_call_target="tpu_custom_call" | custom-call | flops 234881024 | bytes 3670016 | tf_op jit(solution)/shard_map/own_partial/pallas_call | solution.py:100
  18.3 0.0 collective-permute-done.rest_0_
  18.3 2.9 %collective-permute-done.1.rest_1_ = bf16[128,512]{1,0:T(8,128)(2,1)S(1)} collective-permute-done((bf16[128,512]{1,0:T(8,128)(2,1)}, bf16[128,512]{1,0:T(8,128)(2,1)S(1)}, u32[]{:S(2)}, u32[]{:S(2)}) %collective-permute-start.1) | collective-permute-done | bytes 131104 | tf_op jit(solution)/shard_map/ppermute | solution.py:21
  21.2 0.0 collective-permute-done.2.rest_2_
  21.2 1.0 %add_convert_fusion.rest_3_ = bf16[64,512]{1,0:T(8,128)(2,1)S(1)} fusion(f32[64,512]{1,0:T(8,128)} %own_partial.1, bf16[128,512]{1,0:T(8,128)(2,1)S(1)} %collective-permute-done.2.rest_2_, bf16[128,512]{1,0:T(8,128)(2,1)S(1)} %collective-permute-done.1.rest_1_, bf16[128,512]{1,0:T(8,128)(2,1)S(1)} %collective-permute-done.rest_0_), kind=kLoop, calls=%fused_computation | loop fusion | flops 229376 | bytes 393216 | tf_op jit(solution)/shard_map/convert_element_type | solution.py:247
  22.2 0.0 copy-start.3
  22.2 1.6 %collective-permute-start.5 = (bf16[64,512]{1,0:T(8,128)(2,1)S(1)}, bf16[64,512]{1,0:T(8,128)(2,1)S(1)}, u32[]{:S(2)}, u32[]{:S(2)}) collective-permute-start(bf16[64,512]{1,0:T(8,128)(2,1)S(1)} %add_convert_fusion.rest_3_), channel_id=1, source_target_pairs={{0,3},{1,2},{2,1},{3,0},{4,7},{5,6},{6,5},{7,4},{8,11},{9,10},{10,... | collective-permute-start | bytes 196616 | tf_op jit(solution)/shard_map/ppermute | solution.py:21
  23.8 1.1 %collective-permute-start.4 = (bf16[64,512]{1,0:T(8,128)(2,1)S(1)}, bf16[64,512]{1,0:T(8,128)(2,1)S(1)}, u32[]{:S(2)}, u32[]{:S(2)}) collective-permute-start(bf16[64,512]{1,0:T(8,128)(2,1)S(1)} %add_convert_fusion.rest_3_), channel_id=1, source_target_pairs={{0,2},{1,3},{2,0},{3,1},{4,6},{5,7},{6,4},{7,5},{8,10},{9,11},{10,... | collective-permute-start | bytes 196616 | tf_op jit(solution)/shard_map/ppermute | solution.py:21
  24.9 0.8 %collective-permute-start.3 = (bf16[64,512]{1,0:T(8,128)(2,1)S(1)}, bf16[64,512]{1,0:T(8,128)(2,1)S(1)}, u32[]{:S(2)}, u32[]{:S(2)}) collective-permute-start(bf16[64,512]{1,0:T(8,128)(2,1)S(1)} %add_convert_fusion.rest_3_), channel_id=1, source_target_pairs={{0,1},{1,0},{2,3},{3,2},{4,5},{5,4},{6,7},{7,6},{8,9},{9,8},{10,11... | collective-permute-start | bytes 196616 | tf_op jit(solution)/shard_map/ppermute | solution.py:21
  26.4 1.0 %collective-permute-done.5.rest_6_ = bf16[64,512]{1,0:T(8,128)(2,1)S(1)} collective-permute-done((bf16[64,512]{1,0:T(8,128)(2,1)S(1)}, bf16[64,512]{1,0:T(8,128)(2,1)S(1)}, u32[]{:S(2)}, u32[]{:S(2)}) %collective-permute-start.5) | collective-permute-done | bytes 65568 | tf_op jit(solution)/shard_map/ppermute | solution.py:21
  27.5 0.7 %collective-permute-done.4.rest_5_ = bf16[64,512]{1,0:T(8,128)(2,1)S(1)} collective-permute-done((bf16[64,512]{1,0:T(8,128)(2,1)S(1)}, bf16[64,512]{1,0:T(8,128)(2,1)S(1)}, u32[]{:S(2)}, u32[]{:S(2)}) %collective-permute-start.4) | collective-permute-done | bytes 65568 | tf_op jit(solution)/shard_map/ppermute | solution.py:21
  28.1 1.0 %collective-permute-done.3.rest_4_ = bf16[64,512]{1,0:T(8,128)(2,1)S(1)} collective-permute-done((bf16[64,512]{1,0:T(8,128)(2,1)S(1)}, bf16[64,512]{1,0:T(8,128)(2,1)S(1)}, u32[]{:S(2)}, u32[]{:S(2)}) %collective-permute-start.3) | collective-permute-done | bytes 65568 | tf_op jit(solution)/shard_map/ppermute | solution.py:21
  29.2 0.0 copy-done
  29.2 0.0 copy-done.1
  29.2 0.0 copy-done.3
  29.2 0.0 copy-done.19
  29.2 0.0 copy-done.20
  29.2 0.6 copy-done.21
  29.8 3.2 %doc_sums.1 = (bf16[32,1024]{1,0:T(8,128)(2,1)}, bf16[40,1024]{1,0:T(8,128)(2,1)}) custom-call(s32[1]{0:T(128)} %bitcast.pos_ref, s32[1]{0:T(128)S(6)} %copy.8.counts_ref, s32[32,2048]{1,0:T(8,128)} %seg_ref.1, f32[64,512]{1,0:T(8,128)} %get-tuple-element.8.dy_own_ref, bf16[128,512]{1,0:T(8,128)(2,1)} %copy-done, bf16[128,512]{1,0:T(8,128)(2,1)} %copy-done.1, ...), custom_call_target="tpu_custom_call" | custom-call | flops 268435456 | bytes 1048576 | tf_op jit(solution)/shard_map/doc_sums/pallas_call | solution.py:173
  33.1 0.8 %collective-permute-start.8 = (bf16[32,1024]{1,0:T(8,128)(2,1)}, bf16[32,1024]{1,0:T(8,128)(2,1)S(1)}, u32[]{:S(2)}, u32[]{:S(2)}) collective-permute-start(bf16[32,1024]{1,0:T(8,128)(2,1)} %get-tuple-element.6), channel_id=1, source_target_pairs={{0,1},{1,0},{2,3},{3,2},{4,5},{5,4},{6,7},{7,6},{8,9},{9,8},{10,11... | collective-permute-start | bytes 196616 | tf_op jit(solution)/shard_map/ppermute | solution.py:21
  33.9 1.5 %collective-permute-start.7 = (bf16[32,1024]{1,0:T(8,128)(2,1)}, bf16[32,1024]{1,0:T(8,128)(2,1)S(1)}, u32[]{:S(2)}, u32[]{:S(2)}) collective-permute-start(bf16[32,1024]{1,0:T(8,128)(2,1)} %get-tuple-element.6), channel_id=1, source_target_pairs={{0,2},{1,3},{2,0},{3,1},{4,6},{5,7},{6,4},{7,5},{8,10},{9,11},{10,... | collective-permute-start | bytes 196616 | tf_op jit(solution)/shard_map/ppermute | solution.py:21
  35.4 1.1 %collective-permute-start.6 = (bf16[32,1024]{1,0:T(8,128)(2,1)}, bf16[32,1024]{1,0:T(8,128)(2,1)S(1)}, u32[]{:S(2)}, u32[]{:S(2)}) collective-permute-start(bf16[32,1024]{1,0:T(8,128)(2,1)} %get-tuple-element.6), channel_id=1, source_target_pairs={{0,3},{1,2},{2,1},{3,0},{4,7},{5,6},{6,5},{7,4},{8,11},{9,10},{10,... | collective-permute-start | bytes 196616 | tf_op jit(solution)/shard_map/ppermute | solution.py:21
  36.5 0.0 collective-permute-start.19
  36.6 2.6 %collective-permute-start.17 = (bf16[40,1024]{1,0:T(8,128)(2,1)}, bf16[40,1024]{1,0:T(8,128)(2,1)S(1)}, u32[]{:S(2)}, u32[]{:S(2)}) collective-permute-start(bf16[40,1024]{1,0:T(8,128)(2,1)} %get-tuple-element.13.rest_8_), channel_id=1, source_target_pairs={{0,16},{4,20},{8,24},{12,28},{16,0},{20,4},{24,8},{28,12},{1,17},{... | collective-permute-start | bytes 245768 | tf_op jit(solution)/shard_map/ppermute | solution.py:21
  39.1 0.0 collective-permute-done.8
  39.1 1.6 %collective-permute-start.16 = (bf16[40,1024]{1,0:T(8,128)(2,1)}, bf16[40,1024]{1,0:T(8,128)(2,1)S(1)}, u32[]{:S(2)}, u32[]{:S(2)}) collective-permute-start(bf16[40,1024]{1,0:T(8,128)(2,1)} %get-tuple-element.13.rest_8_), channel_id=1, source_target_pairs={{0,8},{4,12},{8,0},{12,4},{16,24},{20,28},{24,16},{28,20},{1,9},{5... | collective-permute-start | bytes 245768 | tf_op jit(solution)/shard_map/ppermute | solution.py:21
  40.7 0.0 collective-permute-done.7
  40.7 0.1 collective-permute-done.6
  40.8 0.9 %select_select_fusion = (bf16[32,1024]{1,0:T(8,128)(2,1)S(1)}, bf16[32,1024]{1,0:T(8,128)(2,1)S(1)}, bf16[32,1024]{1,0:T(8,128)(2,1)S(1)}, bf16[32,1024]{1,0:T(8,128)(2,1)S(1)}) fusion(bf16[32,1024]{1,0:T(8,128)(2,1)S(1)} %collective-permute-done.6, bf16[32,1024]{1,0:T(8,128)(2,1)S(1)} %collective-permute-done.7, ...), kind=kLoop, calls=%fused_computation.1 | loop fusion | flops 393216 | bytes 524300 | tf_op jit(solution)/shard_map/jit(_where)/select_n | solution.py:261
  41.7 3.7 %collective-permute-start.11 = (bf16[32,1024]{1,0:T(8,128)(2,1)S(1)}, bf16[32,1024]{1,0:T(8,128)(2,1)S(1)}, u32[]{:S(2)}, u32[]{:S(2)}) collective-permute-start(bf16[32,1024]{1,0:T(8,128)(2,1)S(1)} %get-tuple-element.14), channel_id=1, source_target_pairs={{0,24},{4,28},{8,16},{12,20},{16,8},{20,12},{24,0},{28,4},{1,25},{... | collective-permute-start | bytes 196616 | tf_op jit(solution)/shard_map/ppermute | solution.py:21
  45.4 0.0 collective-permute-done.17.rest_10_
  45.4 0.0 collective-permute-start.18
  45.4 3.5 %collective-permute-start.10 = (bf16[32,1024]{1,0:T(8,128)(2,1)S(1)}, bf16[32,1024]{1,0:T(8,128)(2,1)S(1)}, u32[]{:S(2)}, u32[]{:S(2)}) collective-permute-start(bf16[32,1024]{1,0:T(8,128)(2,1)S(1)} %get-tuple-element.15), channel_id=1, source_target_pairs={{0,16},{4,20},{8,24},{12,28},{16,0},{20,4},{24,8},{28,12},{1,17},{... | collective-permute-start | bytes 196616 | tf_op jit(solution)/shard_map/ppermute | solution.py:21
  48.8 0.0 collective-permute-done.19.rest_12_
  48.8 0.0 collective-permute-start.21
  48.8 0.0 collective-permute-done.16.rest_9_
  48.8 0.0 copy-start.7
  48.9 0.1 collective-permute-start.9
  48.9 0.0 collective-permute-done.11.rest_3_
  49.0 0.5 collective-permute-start.12
  49.4 2.3 %collective-permute-done.10.rest_2_ = bf16[32,1024]{1,0:T(8,128)(2,1)S(1)} collective-permute-done((bf16[32,1024]{1,0:T(8,128)(2,1)S(1)}, bf16[32,1024]{1,0:T(8,128)(2,1)S(1)}, u32[]{:S(2)}, u32[]{:S(2)}) %collective-permute-start.10) | collective-permute-done | bytes 65568 | tf_op jit(solution)/shard_map/ppermute | solution.py:21
  51.7 0.0 collective-permute-start.20
  51.8 0.0 collective-permute-done.18.rest_11_
  51.8 0.5 collective-permute-start.22
  52.3 1.1 %collective-permute-done.9.rest_1_ = bf16[32,1024]{1,0:T(8,128)(2,1)S(1)} collective-permute-done((bf16[32,1024]{1,0:T(8,128)(2,1)S(1)}, bf16[32,1024]{1,0:T(8,128)(2,1)S(1)}, u32[]{:S(2)}, u32[]{:S(2)}) %collective-permute-start.9) | collective-permute-done | bytes 65568 | tf_op jit(solution)/shard_map/ppermute | solution.py:21
  53.3 0.0 collective-permute-start.15
  53.3 0.0 collective-permute-done.12.rest_4_
  53.4 0.0 copy-start.15
  53.4 0.5 collective-permute-start.14
  53.9 0.0 collective-permute-done.21.rest_14_
  53.9 0.1 collective-permute-start.13
  54.0 0.0 collective-permute-done.20.rest_13_
  54.0 0.6 %collective-permute-done.15.rest_7_ = bf16[32,1024]{1,0:T(8,128)(2,1)S(1)} collective-permute-done((bf16[32,1024]{1,0:T(8,128)(2,1)S(1)}, bf16[32,1024]{1,0:T(8,128)(2,1)S(1)}, u32[]{:S(2)}, u32[]{:S(2)}) %collective-permute-start.15) | collective-permute-done | bytes 65568 | tf_op jit(solution)/shard_map/ppermute | solution.py:21
  54.6 0.2 collective-permute-done.14.rest_6_
  54.8 0.4 collective-permute-done.13.rest_5_
  55.1 0.0 collective-permute-done.22.rest_15_
  55.2 0.1 copy-done.17
  55.4 0.4 copy-done.18
  55.7 0.0 copy-done.11
  55.8 4.3 %fisher_block.1 = f32[512,1024]{1,0:T(8,128)} custom-call(s32[1]{0:T(128)} %bitcast.3.half_ref, bf16[32,1024]{1,0:T(8,128)(2,1)} %copy-done.4, bf16[32,1024]{1,0:T(8,128)(2,1)} %copy-done.14, bf16[32,1024]{1,0:T(8,128)(2,1)} %copy-done.13, bf16[32,1024]{1,0:T(8,128)(2,1)} %copy-done.12, bf16[32,1024]{1,0:T(8,128)(2,1)} %copy-done.15, ...), custom_call_target="tpu_custom_call" | custom-call | flops 268435456 | bytes 2097152 | tf_op jit(solution)/shard_map/fisher_block/pallas_call | solution.py:212
  (32 shorter events, 0.1 us)
Async XLA Ops:
  10.2 8.1 %collective-permute-start = (bf16[128,512]{1,0:T(8,128)(2,1)}, bf16[128,512]{1,0:T(8,128)(2,1)S(1)}, u32[]{:S(2)}, u32[]{:S(2)}) collective-permute-start(bf16[128,512]{1,0:T(8,128)(2,1)} %get-tuple-element.9), channel_id=1, source_target_pairs={{0,1},{1,0},{2,3},{3,2},{4,5},{5,4},{6,7},{7,6},{8,9},{9,8},{10,11... | collective-permute-start | bytes 393224 | tf_op jit(solution)/shard_map/ppermute | solution.py:21
  13.2 8.0 %collective-permute-start.1 = (bf16[128,512]{1,0:T(8,128)(2,1)}, bf16[128,512]{1,0:T(8,128)(2,1)S(1)}, u32[]{:S(2)}, u32[]{:S(2)}) collective-permute-start(bf16[128,512]{1,0:T(8,128)(2,1)} %get-tuple-element.10), channel_id=1, source_target_pairs={{0,2},{1,3},{2,0},{3,1},{4,6},{5,7},{6,4},{7,5},{8,10},{9,11},{10,... | collective-permute-start | bytes 393224 | tf_op jit(solution)/shard_map/ppermute | solution.py:21
  14.7 6.5 %collective-permute-start.2 = (bf16[128,512]{1,0:T(8,128)(2,1)}, bf16[128,512]{1,0:T(8,128)(2,1)S(1)}, u32[]{:S(2)}, u32[]{:S(2)}) collective-permute-start(bf16[128,512]{1,0:T(8,128)(2,1)} %get-tuple-element.11), channel_id=1, source_target_pairs={{0,3},{1,2},{2,1},{3,0},{4,7},{5,6},{6,5},{7,4},{8,11},{9,10},{10,... | collective-permute-start | bytes 393224 | tf_op jit(solution)/shard_map/ppermute | solution.py:21
  18.3 10.9 %copy-start = (bf16[128,512]{1,0:T(8,128)(2,1)}, bf16[128,512]{1,0:T(8,128)(2,1)S(1)}, u32[]{:S(2)}) copy-start(bf16[128,512]{1,0:T(8,128)(2,1)S(1)} %collective-permute-done.rest_0_) | copy-start | bytes 393220
  21.2 8.0 %copy-start.1 = (bf16[128,512]{1,0:T(8,128)(2,1)}, bf16[128,512]{1,0:T(8,128)(2,1)S(1)}, u32[]{:S(2)}) copy-start(bf16[128,512]{1,0:T(8,128)(2,1)S(1)} %collective-permute-done.1.rest_1_) | copy-start | bytes 393220
  21.2 8.0 %copy-start.2 = (bf16[128,512]{1,0:T(8,128)(2,1)}, bf16[128,512]{1,0:T(8,128)(2,1)S(1)}, u32[]{:S(2)}) copy-start(bf16[128,512]{1,0:T(8,128)(2,1)S(1)} %collective-permute-done.2.rest_2_) | copy-start | bytes 393220
  22.2 7.0 %copy-start.3 = (bf16[64,512]{1,0:T(8,128)(2,1)}, bf16[64,512]{1,0:T(8,128)(2,1)S(1)}, u32[]{:S(2)}) copy-start(bf16[64,512]{1,0:T(8,128)(2,1)S(1)} %add_convert_fusion.rest_3_) | copy-start | bytes 196612
  22.2 5.2 %collective-permute-start.5 = (bf16[64,512]{1,0:T(8,128)(2,1)S(1)}, bf16[64,512]{1,0:T(8,128)(2,1)S(1)}, u32[]{:S(2)}, u32[]{:S(2)}) collective-permute-start(bf16[64,512]{1,0:T(8,128)(2,1)S(1)} %add_convert_fusion.rest_3_), channel_id=1, source_target_pairs={{0,3},{1,2},{2,1},{3,0},{4,7},{5,6},{6,5},{7,4},{8,11},{9,10},{10,... | collective-permute-start | bytes 196616 | tf_op jit(solution)/shard_map/ppermute | solution.py:21
  23.8 4.4 %collective-permute-start.4 = (bf16[64,512]{1,0:T(8,128)(2,1)S(1)}, bf16[64,512]{1,0:T(8,128)(2,1)S(1)}, u32[]{:S(2)}, u32[]{:S(2)}) collective-permute-start(bf16[64,512]{1,0:T(8,128)(2,1)S(1)} %add_convert_fusion.rest_3_), channel_id=1, source_target_pairs={{0,2},{1,3},{2,0},{3,1},{4,6},{5,7},{6,4},{7,5},{8,10},{9,11},{10,... | collective-permute-start | bytes 196616 | tf_op jit(solution)/shard_map/ppermute | solution.py:21
  24.9 4.3 %collective-permute-start.3 = (bf16[64,512]{1,0:T(8,128)(2,1)S(1)}, bf16[64,512]{1,0:T(8,128)(2,1)S(1)}, u32[]{:S(2)}, u32[]{:S(2)}) collective-permute-start(bf16[64,512]{1,0:T(8,128)(2,1)S(1)} %add_convert_fusion.rest_3_), channel_id=1, source_target_pairs={{0,1},{1,0},{2,3},{3,2},{4,5},{5,4},{6,7},{7,6},{8,9},{9,8},{10,11... | collective-permute-start | bytes 196616 | tf_op jit(solution)/shard_map/ppermute | solution.py:21
  27.5 1.8 %copy-start.19 = (bf16[64,512]{1,0:T(8,128)(2,1)}, bf16[64,512]{1,0:T(8,128)(2,1)S(1)}, u32[]{:S(2)}) copy-start(bf16[64,512]{1,0:T(8,128)(2,1)S(1)} %collective-permute-done.5.rest_6_) | copy-start | bytes 196612
  28.1 1.1 %copy-start.20 = (bf16[64,512]{1,0:T(8,128)(2,1)}, bf16[64,512]{1,0:T(8,128)(2,1)S(1)}, u32[]{:S(2)}) copy-start(bf16[64,512]{1,0:T(8,128)(2,1)S(1)} %collective-permute-done.4.rest_5_) | copy-start | bytes 196612
  29.2 0.6 %copy-start.21 = (bf16[64,512]{1,0:T(8,128)(2,1)}, bf16[64,512]{1,0:T(8,128)(2,1)S(1)}, u32[]{:S(2)}) copy-start(bf16[64,512]{1,0:T(8,128)(2,1)S(1)} %collective-permute-done.3.rest_4_) | copy-start | bytes 196612
  33.1 6.1 %collective-permute-start.8 = (bf16[32,1024]{1,0:T(8,128)(2,1)}, bf16[32,1024]{1,0:T(8,128)(2,1)S(1)}, u32[]{:S(2)}, u32[]{:S(2)}) collective-permute-start(bf16[32,1024]{1,0:T(8,128)(2,1)} %get-tuple-element.6), channel_id=1, source_target_pairs={{0,1},{1,0},{2,3},{3,2},{4,5},{5,4},{6,7},{7,6},{8,9},{9,8},{10,11... | collective-permute-start | bytes 196616 | tf_op jit(solution)/shard_map/ppermute | solution.py:21
  33.9 6.8 %collective-permute-start.7 = (bf16[32,1024]{1,0:T(8,128)(2,1)}, bf16[32,1024]{1,0:T(8,128)(2,1)S(1)}, u32[]{:S(2)}, u32[]{:S(2)}) collective-permute-start(bf16[32,1024]{1,0:T(8,128)(2,1)} %get-tuple-element.6), channel_id=1, source_target_pairs={{0,2},{1,3},{2,0},{3,1},{4,6},{5,7},{6,4},{7,5},{8,10},{9,11},{10,... | collective-permute-start | bytes 196616 | tf_op jit(solution)/shard_map/ppermute | solution.py:21
  35.4 5.4 %collective-permute-start.6 = (bf16[32,1024]{1,0:T(8,128)(2,1)}, bf16[32,1024]{1,0:T(8,128)(2,1)S(1)}, u32[]{:S(2)}, u32[]{:S(2)}) collective-permute-start(bf16[32,1024]{1,0:T(8,128)(2,1)} %get-tuple-element.6), channel_id=1, source_target_pairs={{0,3},{1,2},{2,1},{3,0},{4,7},{5,6},{6,5},{7,4},{8,11},{9,10},{10,... | collective-permute-start | bytes 196616 | tf_op jit(solution)/shard_map/ppermute | solution.py:21
  36.5 12.3 %collective-permute-start.19 = (bf16[40,1024]{1,0:T(8,128)(2,1)}, bf16[40,1024]{1,0:T(8,128)(2,1)S(1)}, u32[]{:S(2)}, u32[]{:S(2)}) collective-permute-start(bf16[40,1024]{1,0:T(8,128)(2,1)} %get-tuple-element.13.rest_8_), channel_id=1, source_target_pairs={{0,4},{4,0},{8,12},{12,8},{16,20},{20,16},{24,28},{28,24},{1,5},{5... | collective-permute-start | bytes 245768 | tf_op jit(solution)/shard_map/ppermute | solution.py:21
  36.6 8.8 %collective-permute-start.17 = (bf16[40,1024]{1,0:T(8,128)(2,1)}, bf16[40,1024]{1,0:T(8,128)(2,1)S(1)}, u32[]{:S(2)}, u32[]{:S(2)}) collective-permute-start(bf16[40,1024]{1,0:T(8,128)(2,1)} %get-tuple-element.13.rest_8_), channel_id=1, source_target_pairs={{0,16},{4,20},{8,24},{12,28},{16,0},{20,4},{24,8},{28,12},{1,17},{... | collective-permute-start | bytes 245768 | tf_op jit(solution)/shard_map/ppermute | solution.py:21
  39.1 9.7 %collective-permute-start.16 = (bf16[40,1024]{1,0:T(8,128)(2,1)}, bf16[40,1024]{1,0:T(8,128)(2,1)S(1)}, u32[]{:S(2)}, u32[]{:S(2)}) collective-permute-start(bf16[40,1024]{1,0:T(8,128)(2,1)} %get-tuple-element.13.rest_8_), channel_id=1, source_target_pairs={{0,8},{4,12},{8,0},{12,4},{16,24},{20,28},{24,16},{28,20},{1,9},{5... | collective-permute-start | bytes 245768 | tf_op jit(solution)/shard_map/ppermute | solution.py:21
  41.7 13.5 %copy-start.4 = (bf16[32,1024]{1,0:T(8,128)(2,1)}, bf16[32,1024]{1,0:T(8,128)(2,1)S(1)}, u32[]{:S(2)}) copy-start(bf16[32,1024]{1,0:T(8,128)(2,1)S(1)} %get-tuple-element.17.rest_0_) | copy-start | bytes 196612
  41.7 7.2 %collective-permute-start.11 = (bf16[32,1024]{1,0:T(8,128)(2,1)S(1)}, bf16[32,1024]{1,0:T(8,128)(2,1)S(1)}, u32[]{:S(2)}, u32[]{:S(2)}) collective-permute-start(bf16[32,1024]{1,0:T(8,128)(2,1)S(1)} %get-tuple-element.14), channel_id=1, source_target_pairs={{0,24},{4,28},{8,16},{12,20},{16,8},{20,12},{24,0},{28,4},{1,25},{... | collective-permute-start | bytes 196616 | tf_op jit(solution)/shard_map/ppermute | solution.py:21
  45.4 9.8 %copy-start.6 = (bf16[40,1024]{1,0:T(8,128)(2,1)}, bf16[40,1024]{1,0:T(8,128)(2,1)S(1)}, u32[]{:S(2)}) copy-start(bf16[40,1024]{1,0:T(8,128)(2,1)S(1)} %collective-permute-done.17.rest_10_) | copy-start | bytes 245764
  45.4 6.4 %collective-permute-start.18 = (bf16[40,1024]{1,0:T(8,128)(2,1)S(1)}, bf16[40,1024]{1,0:T(8,128)(2,1)S(1)}, u32[]{:S(2)}, u32[]{:S(2)}) collective-permute-start(bf16[40,1024]{1,0:T(8,128)(2,1)S(1)} %collective-permute-done.17.rest_10_), channel_id=1, source_target_pairs={{0,8},{4,12},{8,0},{12,4},{16,24},{20,28},{24,16},{28,20},{1,9},{5... | collective-permute-start | bytes 245768 | tf_op jit(solution)/shard_map/ppermute | solution.py:21
  45.4 6.4 %collective-permute-start.10 = (bf16[32,1024]{1,0:T(8,128)(2,1)S(1)}, bf16[32,1024]{1,0:T(8,128)(2,1)S(1)}, u32[]{:S(2)}, u32[]{:S(2)}) collective-permute-start(bf16[32,1024]{1,0:T(8,128)(2,1)S(1)} %get-tuple-element.15), channel_id=1, source_target_pairs={{0,16},{4,20},{8,24},{12,28},{16,0},{20,4},{24,8},{28,12},{1,17},{... | collective-permute-start | bytes 196616 | tf_op jit(solution)/shard_map/ppermute | solution.py:21
  48.8 6.3 %copy-start.5 = (bf16[40,1024]{1,0:T(8,128)(2,1)}, bf16[40,1024]{1,0:T(8,128)(2,1)S(1)}, u32[]{:S(2)}) copy-start(bf16[40,1024]{1,0:T(8,128)(2,1)S(1)} %collective-permute-done.19.rest_12_) | copy-start | bytes 245764
  48.8 5.0 %collective-permute-start.21 = (bf16[40,1024]{1,0:T(8,128)(2,1)S(1)}, bf16[40,1024]{1,0:T(8,128)(2,1)S(1)}, u32[]{:S(2)}, u32[]{:S(2)}) collective-permute-start(bf16[40,1024]{1,0:T(8,128)(2,1)S(1)} %collective-permute-done.17.rest_10_), channel_id=1, source_target_pairs={{0,4},{4,0},{8,12},{12,8},{16,20},{20,16},{24,28},{28,24},{1,5},{5... | collective-permute-start | bytes 245768 | tf_op jit(solution)/shard_map/ppermute | solution.py:21
  48.8 6.3 %copy-start.7 = (bf16[40,1024]{1,0:T(8,128)(2,1)}, bf16[40,1024]{1,0:T(8,128)(2,1)S(1)}, u32[]{:S(2)}) copy-start(bf16[40,1024]{1,0:T(8,128)(2,1)S(1)} %collective-permute-done.16.rest_9_) | copy-start | bytes 245764
  48.9 4.5 %collective-permute-start.9 = (bf16[32,1024]{1,0:T(8,128)(2,1)S(1)}, bf16[32,1024]{1,0:T(8,128)(2,1)S(1)}, u32[]{:S(2)}, u32[]{:S(2)}) collective-permute-start(bf16[32,1024]{1,0:T(8,128)(2,1)S(1)} %get-tuple-element.16), channel_id=1, source_target_pairs={{0,8},{4,12},{8,0},{12,4},{16,24},{20,28},{24,16},{28,20},{1,9},{5... | collective-permute-start | bytes 196616 | tf_op jit(solution)/shard_map/ppermute | solution.py:21
  48.9 6.2 %copy-start.12 = (bf16[32,1024]{1,0:T(8,128)(2,1)}, bf16[32,1024]{1,0:T(8,128)(2,1)S(1)}, u32[]{:S(2)}) copy-start(bf16[32,1024]{1,0:T(8,128)(2,1)S(1)} %collective-permute-done.11.rest_3_) | copy-start | bytes 196612
  49.0 4.4 %collective-permute-start.12 = (bf16[32,1024]{1,0:T(8,128)(2,1)S(1)}, bf16[32,1024]{1,0:T(8,128)(2,1)S(1)}, u32[]{:S(2)}, u32[]{:S(2)}) collective-permute-start(bf16[32,1024]{1,0:T(8,128)(2,1)S(1)} %get-tuple-element.17.rest_0_), channel_id=1, source_target_pairs={{0,4},{4,0},{8,12},{12,8},{16,20},{20,16},{24,28},{28,24},{1,5},{5... | collective-permute-start | bytes 196616 | tf_op jit(solution)/shard_map/ppermute | solution.py:21
  51.7 3.4 %copy-start.13 = (bf16[32,1024]{1,0:T(8,128)(2,1)}, bf16[32,1024]{1,0:T(8,128)(2,1)S(1)}, u32[]{:S(2)}) copy-start(bf16[32,1024]{1,0:T(8,128)(2,1)S(1)} %collective-permute-done.10.rest_2_) | copy-start | bytes 196612
  51.7 2.2 %collective-permute-start.20 = (bf16[40,1024]{1,0:T(8,128)(2,1)S(1)}, bf16[40,1024]{1,0:T(8,128)(2,1)S(1)}, u32[]{:S(2)}, u32[]{:S(2)}) collective-permute-start(bf16[40,1024]{1,0:T(8,128)(2,1)S(1)} %collective-permute-done.16.rest_9_), channel_id=1, source_target_pairs={{0,4},{4,0},{8,12},{12,8},{16,20},{20,16},{24,28},{28,24},{1,5},{5... | collective-permute-start | bytes 245768 | tf_op jit(solution)/shard_map/ppermute | solution.py:21
  51.8 3.4 %copy-start.8 = (bf16[40,1024]{1,0:T(8,128)(2,1)}, bf16[40,1024]{1,0:T(8,128)(2,1)S(1)}, u32[]{:S(2)}) copy-start(bf16[40,1024]{1,0:T(8,128)(2,1)S(1)} %collective-permute-done.18.rest_11_) | copy-start | bytes 245764
  51.8 3.4 %collective-permute-start.22 = (bf16[40,1024]{1,0:T(8,128)(2,1)S(1)}, bf16[40,1024]{1,0:T(8,128)(2,1)S(1)}, u32[]{:S(2)}, u32[]{:S(2)}) collective-permute-start(bf16[40,1024]{1,0:T(8,128)(2,1)S(1)} %collective-permute-done.18.rest_11_), channel_id=1, source_target_pairs={{0,4},{4,0},{8,12},{12,8},{16,20},{20,16},{24,28},{28,24},{1,5},{5... | collective-permute-start | bytes 245768 | tf_op jit(solution)/shard_map/ppermute | solution.py:21
  53.3 1.9 %copy-start.14 = (bf16[32,1024]{1,0:T(8,128)(2,1)}, bf16[32,1024]{1,0:T(8,128)(2,1)S(1)}, u32[]{:S(2)}) copy-start(bf16[32,1024]{1,0:T(8,128)(2,1)S(1)} %collective-permute-done.9.rest_1_) | copy-start | bytes 196612
  53.3 1.3 %collective-permute-start.15 = (bf16[32,1024]{1,0:T(8,128)(2,1)S(1)}, bf16[32,1024]{1,0:T(8,128)(2,1)S(1)}, u32[]{:S(2)}, u32[]{:S(2)}) collective-permute-start(bf16[32,1024]{1,0:T(8,128)(2,1)S(1)} %collective-permute-done.11.rest_3_), channel_id=1, source_target_pairs={{0,4},{4,0},{8,12},{12,8},{16,20},{20,16},{24,28},{28,24},{1,5},{5... | collective-permute-start | bytes 196616 | tf_op jit(solution)/shard_map/ppermute | solution.py:21
  53.4 1.9 %copy-start.15 = (bf16[32,1024]{1,0:T(8,128)(2,1)}, bf16[32,1024]{1,0:T(8,128)(2,1)S(1)}, u32[]{:S(2)}) copy-start(bf16[32,1024]{1,0:T(8,128)(2,1)S(1)} %collective-permute-done.12.rest_4_) | copy-start | bytes 196612
  53.4 1.4 %collective-permute-start.14 = (bf16[32,1024]{1,0:T(8,128)(2,1)S(1)}, bf16[32,1024]{1,0:T(8,128)(2,1)S(1)}, u32[]{:S(2)}, u32[]{:S(2)}) collective-permute-start(bf16[32,1024]{1,0:T(8,128)(2,1)S(1)} %collective-permute-done.10.rest_2_), channel_id=1, source_target_pairs={{0,4},{4,0},{8,12},{12,8},{16,20},{20,16},{24,28},{28,24},{1,5},{5... | collective-permute-start | bytes 196616 | tf_op jit(solution)/shard_map/ppermute | solution.py:21
  53.9 1.4 %copy-start.9 = (bf16[40,1024]{1,0:T(8,128)(2,1)}, bf16[40,1024]{1,0:T(8,128)(2,1)S(1)}, u32[]{:S(2)}) copy-start(bf16[40,1024]{1,0:T(8,128)(2,1)S(1)} %collective-permute-done.21.rest_14_) | copy-start | bytes 245764
  53.9 1.3 %collective-permute-start.13 = (bf16[32,1024]{1,0:T(8,128)(2,1)S(1)}, bf16[32,1024]{1,0:T(8,128)(2,1)S(1)}, u32[]{:S(2)}, u32[]{:S(2)}) collective-permute-start(bf16[32,1024]{1,0:T(8,128)(2,1)S(1)} %collective-permute-done.9.rest_1_), channel_id=1, source_target_pairs={{0,4},{4,0},{8,12},{12,8},{16,20},{20,16},{24,28},{28,24},{1,5},{5... | collective-permute-start | bytes 196616 | tf_op jit(solution)/shard_map/ppermute | solution.py:21
  54.0 1.3 %copy-start.10 = (bf16[40,1024]{1,0:T(8,128)(2,1)}, bf16[40,1024]{1,0:T(8,128)(2,1)S(1)}, u32[]{:S(2)}) copy-start(bf16[40,1024]{1,0:T(8,128)(2,1)S(1)} %collective-permute-done.20.rest_13_) | copy-start | bytes 245764
  54.6 0.6 %copy-start.16 = (bf16[32,1024]{1,0:T(8,128)(2,1)}, bf16[32,1024]{1,0:T(8,128)(2,1)S(1)}, u32[]{:S(2)}) copy-start(bf16[32,1024]{1,0:T(8,128)(2,1)S(1)} %collective-permute-done.15.rest_7_) | copy-start | bytes 196612
  54.8 0.6 %copy-start.17 = (bf16[32,1024]{1,0:T(8,128)(2,1)}, bf16[32,1024]{1,0:T(8,128)(2,1)S(1)}, u32[]{:S(2)}) copy-start(bf16[32,1024]{1,0:T(8,128)(2,1)S(1)} %collective-permute-done.14.rest_6_) | copy-start | bytes 196612
  55.1 0.6 %copy-start.18 = (bf16[32,1024]{1,0:T(8,128)(2,1)}, bf16[32,1024]{1,0:T(8,128)(2,1)S(1)}, u32[]{:S(2)}) copy-start(bf16[32,1024]{1,0:T(8,128)(2,1)S(1)} %collective-permute-done.13.rest_5_) | copy-start | bytes 196612
  55.1 0.7 %copy-start.11 = (bf16[40,1024]{1,0:T(8,128)(2,1)}, bf16[40,1024]{1,0:T(8,128)(2,1)S(1)}, u32[]{:S(2)}) copy-start(bf16[40,1024]{1,0:T(8,128)(2,1)S(1)} %collective-permute-done.22.rest_15_) | copy-start | bytes 245764

commit v3 on v2

--- a/solution.py
+++ b/solution.py
@@ -6,6 +6,7 @@
 from jax.experimental import pallas as pl
 from jax.experimental.pallas import tpu as pltpu
 from jax.sharding import PartitionSpec as P
+
 
 BF16 = jnp.bfloat16
 F32 = jnp.float32
@@ -83,6 +84,7 @@
             bytes_accessed=2 * tokens * (acts_width + grads_width),
             transcendentals=0,
         ),
+        compiler_params=pltpu.CompilerParams(vmem_limit_bytes=58 << 20),
         name="peer_messages",
     )(pos, acts, grads, proj_in_t, proj_out_t)
 
@@ -112,14 +114,15 @@
         cost_estimate=pl.CostEstimate(
             flops=2 * chunk * width * rank, bytes_accessed=2 * chunk * width, transcendentals=0
         ),
+        compiler_params=pltpu.CompilerParams(vmem_limit_bytes=48 << 20),
         name="own_partial",
     )(pos, acts, proj_t)
 
 
 def docs_kernel(size, pos_ref, counts_ref, seg_ref, dy_own_ref, *rest):
     messages, xs = rest[: size - 1], rest[size - 1 : 2 * size - 1]
-    grads_ref, shared_ref, dy_ref, sums_ref = rest[2 * size - 1 :]
-    docs, tokens = seg_ref.shape
+    grads_ref, inner_ref, shared_ref, dy_ref, sums_ref = rest[2 * size - 1 :]
+    docs, _ = seg_ref.shape
     rank, chunk = xs[0].shape
     part = rank // size
     rows = dy_ref.shape[0] // size
@@ -152,8 +155,10 @@
         pieces = [sums_ref[pl.ds(a + n, docs, stride=rows), :] for n in range(lanes)]
         wide = pieces[0] if lanes == 1 else jnp.concatenate(pieces, axis=1)
         wide = wide.astype(BF16)
-        grads_ref[:, a * rank : (a + lanes) * rank] = wide
-        shared_ref[:docs, a * rank : (a + lanes) * rank] = wide
+        span = slice(a * rank, (a + lanes) * rank)
+        grads_ref[:, span] = wide
+        inner_ref[:, span] = wide
+        shared_ref[:docs, span] = wide
     left = jnp.sum(live_tokens)
     row = lax.broadcasted_iota(jnp.int32, (DIGIT_ROWS, part * rank), 0)
     digits = jnp.zeros(row.shape, jnp.int32)
@@ -173,8 +178,9 @@
     return pl.pallas_call(
         functools.partial(docs_kernel, size),
         in_specs=[SMEM, SMEM] + [VMEM] * (1 + 2 * size),
-        out_specs=[VMEM, VMEM],
+        out_specs=[VMEM, VMEM, VMEM],
         out_shape=[
+            jax.ShapeDtypeStruct((docs, part * rank), BF16),
             jax.ShapeDtypeStruct((docs, part * rank), BF16),
             jax.ShapeDtypeStruct((docs + DIGIT_ROWS, part * rank), BF16),
         ],
@@ -185,6 +191,7 @@
         cost_estimate=pl.CostEstimate(
             flops=4 * docs * rows * tokens * rank, bytes_accessed=1 << 20, transcendentals=0
         ),
+        compiler_params=pltpu.CompilerParams(vmem_limit_bytes=16 << 20),
         name="doc_sums",
     )(pos, counts, seg, dy_own, *messages, *xs)
 
@@ -200,14 +207,14 @@
         digits = c[docs:, 0:1].astype(F32)
         for n, unit in enumerate(DIGITS):
             total = total + digits[n : n + 1, :] * float(unit)
-    out_ref[...] = product / total
+    out_ref[...] = product * (1.0 / total)
 
 
 def fisher_block(half, rows, cols):
     shards = len(rows)
     docs, width = rows[0].shape
     height = width // 2
-    tile = min(128, height)
+    tile = min(256, height)
     tiles = height // tile
     return pl.pallas_call(
         functools.partial(fisher_kernel, shards),
@@ -224,6 +231,7 @@
             bytes_accessed=4 * height * width,
             transcendentals=0,
         ),
+        compiler_params=pltpu.CompilerParams(vmem_limit_bytes=16 << 20),
         name="fisher_block",
     )(half, *rows, *cols)
 
@@ -246,13 +254,13 @@
         x = x + message[:rank].astype(F32)
     x = x.astype(BF16)
     xs = [x] + [swap(x, "tensor", k) for k in steps]
-    grads, shared = doc_sums(pos1, doc_counts, segments, dy_own, messages, xs)
+    grads, inner, shared = doc_sums(pos1, doc_counts, segments, dy_own, messages, xs)
 
     cols = {0: shared}
     for j in steps:
         low = j & -j
         cols[j] = swap(cols[j - low] if j != low else shared, "dp", 2 * low)
-    blocks = [grads] + [swap(grads, "tensor", k) for k in steps]
+    blocks = [inner] + [swap(inner, "tensor", k) for k in steps]
     rows = []
     for j in range(size):
         where = pos ^ pair ^ j

time: 60.5 us -> 54.1 us (0.89)
  Pallas kernels: 20.7 us -> 16.4 us
  other arithmetic: 1.91 us -> 0.07 us
  local copies, waits for them, and re-layouts: 1.19 us -> 0.01 us
  waiting for transfers between devices: 10.3 us -> 11.2 us
    pallas_call x1, Pallas kernels: 4.28 us -> 1.83 us  [fisher_block(): pl.pallas_call(functools.partial(fisher_kernel, shards), grid_spec=pltpu....]
    pallas_call x1, Pallas kernels: 3.25 us -> 2.01 us  [doc_sums(): pl.pallas_call(functools.partial(docs_kernel, size), in_specs=[SMEM, SMEM...]
    unnamed x44 -> x6, local copies, waits for them, and re-layouts: 1.19 us -> 0.01 us
    convert_element_type x1, other arithmetic: 1.03 us -> 0.03 us  [per_device(): x = x.astype(BF16)]
    ppermute x23, waiting for transfers between devices: 10.3 us -> 11.2 us  [swap(): lax.ppermute(value, axis, [(i, i ^ step) for i in range(lax.axis_size(axi...]
    select_n x1, other arithmetic: 0.88 us -> 0.04 us  [per_device(): picked = jnp.where(where == k, blocks[k], picked)]
    pallas_call x1, Pallas kernels: 3.57 us -> 2.94 us  [own_partial(): pl.pallas_call(own_kernel, grid_spec=pltpu.PrefetchScalarGridSpec(num_sca...]
  transfers between devices with their start and end apart: 23 -> 23, of which waited for: 10 -> 10; matrix products, arithmetic and copies ran while one was open for 1% -> 0% of each run, Pallas kernels for 6% -> 5%
where the time goes in v3:
time: 54.1 us; the launch traced here: 54 us
  starting transfers between devices  24.9 us (46%)
  Pallas kernels  16.4 us (30%)
  waiting for transfers between devices  11.2 us (21%)
  between operations  1.37 us (3%)
    ppermute x23, starting transfers between devices, swap(): lax.ppermute(value, axis, [(i, i ^ step) for i in range(lax.axis_size(axi...  24.9 us
    ppermute x23, waiting for transfers between devices, swap(): lax.ppermute(value, axis, [(i, i ^ step) for i in range(lax.axis_size(axi...  11.2 us
    pallas_call x1, Pallas kernels, peer_messages(): pl.pallas_call(peers_kernel, grid_spec=pltpu.PrefetchScalarGridSpec(num_s...  9.63 us
    pallas_call x1, Pallas kernels, own_partial(): pl.pallas_call(own_kernel, grid_spec=pltpu.PrefetchScalarGridSpec(num_sca...  2.94 us
    pallas_call x1, Pallas kernels, doc_sums(): pl.pallas_call(functools.partial(docs_kernel, size), in_specs=[SMEM, SMEM...  2.01 us
    pallas_call x1, Pallas kernels, fisher_block(): pl.pallas_call(functools.partial(fisher_kernel, shards), grid_spec=pltpu....  1.83 us
  transfers between devices with their start and end apart: 23, of which 10 were waited for; matrix products, arithmetic and copies ran while one was open for 0% of the time, Pallas kernels for 5%

profile of v3, /device:TPU:0, one launch (start us, length us, event | category | flops | bytes accessed | tf_op | source)
XLA Modules:
  0.0 54.0 jit_solution(17628627856312314320)
XLA Ops:
  0.6 0.0 copy-start
  0.6 9.6 %peer_messages.1 = (bf16[128,512]{1,0:T(8,128)(2,1)}, bf16[128,512]{1,0:T(8,128)(2,1)}, bf16[128,512]{1,0:T(8,128)(2,1)}, f32[64,512]{1,0:T(8,128)}) custom-call(s32[1]{0:T(128)} %bitcast.pos_ref, bf16[2048,3584]{1,0:T(8,128)(2,1)} %acts_ref.3, bf16[2048,1024]{1,0:T(8,128)(2,1)} %grads_ref.1, bf16[64,3584]{1,0:T(8,128)(2,1)} %bitcast.4, bf16[64,1024]{1,0:T(8,128)(2,1)} %bitcast.6), custom_call_target="tpu_custom_call" | custom-call | flops 1207959552 | bytes 18874368 | tf_op jit(solution)/shard_map/peer_messages/pallas_call | solution.py:65
  10.3 3.0 %collective-permute-start = (bf16[128,512]{1,0:T(8,128)(2,1)}, bf16[128,512]{1,0:T(8,128)(2,1)S(1)}, u32[]{:S(2)}, u32[]{:S(2)}) collective-permute-start(bf16[128,512]{1,0:T(8,128)(2,1)} %get-tuple-element.10), channel_id=1, source_target_pairs={{0,1},{1,0},{2,3},{3,2},{4,5},{5,4},{6,7},{7,6},{8,9},{9,8},{10,11... | collective-permute-start | bytes 393224 | tf_op jit(solution)/shard_map/ppermute | solution.py:22
  13.2 1.5 %collective-permute-start.1 = (bf16[128,512]{1,0:T(8,128)(2,1)}, bf16[128,512]{1,0:T(8,128)(2,1)S(1)}, u32[]{:S(2)}, u32[]{:S(2)}) collective-permute-start(bf16[128,512]{1,0:T(8,128)(2,1)} %get-tuple-element.11), channel_id=1, source_target_pairs={{0,2},{1,3},{2,0},{3,1},{4,6},{5,7},{6,4},{7,5},{8,10},{9,11},{10,... | collective-permute-start | bytes 393224 | tf_op jit(solution)/shard_map/ppermute | solution.py:22
  14.8 0.0 copy-start.1
  14.8 0.0 copy-start.2
  14.8 0.0 collective-permute-start.2
  14.8 0.0 copy-done
  14.8 2.9 %own_partial.1 = f32[64,512]{1,0:T(8,128)S(1)} custom-call(s32[1]{0:T(128)} %bitcast.pos_ref, bf16[2048,3584]{1,0:T(8,128)(2,1)} %acts_ref.3, bf16[64,3584]{1,0:T(8,128)(2,1)S(1)} %bitcast.5), custom_call_target="tpu_custom_call" | custom-call | flops 234881024 | bytes 3670016 | tf_op jit(solution)/shard_map/own_partial/pallas_call | solution.py:102
  17.7 0.0 collective-permute-done.rest_0_
  17.7 3.5 %collective-permute-done.1.rest_1_ = bf16[128,512]{1,0:T(8,128)(2,1)S(1)} collective-permute-done((bf16[128,512]{1,0:T(8,128)(2,1)}, bf16[128,512]{1,0:T(8,128)(2,1)S(1)}, u32[]{:S(2)}, u32[]{:S(2)}) %collective-permute-start.1) | collective-permute-done | bytes 131104 | tf_op jit(solution)/shard_map/ppermute | solution.py:22
  21.2 0.0 collective-permute-done.2.rest_2_
  21.3 1.6 %collective-permute-start.5 = (bf16[64,512]{1,0:T(8,128)(2,1)S(1)}, bf16[64,512]{1,0:T(8,128)(2,1)S(1)}, u32[]{:S(2)}, u32[]{:S(2)}) collective-permute-start(bf16[64,512]{1,0:T(8,128)(2,1)S(1)} %add_convert_fusion.rest_3_), channel_id=1, source_target_pairs={{0,3},{1,2},{2,1},{3,0},{4,7},{5,6},{6,5},{7,4},{8,11},{9,10},{10,... | collective-permute-start | bytes 196616 | tf_op jit(solution)/shard_map/ppermute | solution.py:22
  22.8 1.2 %collective-permute-start.4 = (bf16[64,512]{1,0:T(8,128)(2,1)S(1)}, bf16[64,512]{1,0:T(8,128)(2,1)S(1)}, u32[]{:S(2)}, u32[]{:S(2)}) collective-permute-start(bf16[64,512]{1,0:T(8,128)(2,1)S(1)} %add_convert_fusion.rest_3_), channel_id=1, source_target_pairs={{0,2},{1,3},{2,0},{3,1},{4,6},{5,7},{6,4},{7,5},{8,10},{9,11},{10,... | collective-permute-start | bytes 196616 | tf_op jit(solution)/shard_map/ppermute | solution.py:22
  24.0 0.8 %collective-permute-start.3 = (bf16[64,512]{1,0:T(8,128)(2,1)S(1)}, bf16[64,512]{1,0:T(8,128)(2,1)S(1)}, u32[]{:S(2)}, u32[]{:S(2)}) collective-permute-start(bf16[64,512]{1,0:T(8,128)(2,1)S(1)} %add_convert_fusion.rest_3_), channel_id=1, source_target_pairs={{0,1},{1,0},{2,3},{3,2},{4,5},{5,4},{6,7},{7,6},{8,9},{9,8},{10,11... | collective-permute-start | bytes 196616 | tf_op jit(solution)/shard_map/ppermute | solution.py:22
  25.5 1.0 %collective-permute-done.5.rest_6_ = bf16[64,512]{1,0:T(8,128)(2,1)S(1)} collective-permute-done((bf16[64,512]{1,0:T(8,128)(2,1)S(1)}, bf16[64,512]{1,0:T(8,128)(2,1)S(1)}, u32[]{:S(2)}, u32[]{:S(2)}) %collective-permute-start.5) | collective-permute-done | bytes 65568 | tf_op jit(solution)/shard_map/ppermute | solution.py:22
  26.5 0.7 %collective-permute-done.4.rest_5_ = bf16[64,512]{1,0:T(8,128)(2,1)S(1)} collective-permute-done((bf16[64,512]{1,0:T(8,128)(2,1)S(1)}, bf16[64,512]{1,0:T(8,128)(2,1)S(1)}, u32[]{:S(2)}, u32[]{:S(2)}) %collective-permute-start.4) | collective-permute-done | bytes 65568 | tf_op jit(solution)/shard_map/ppermute | solution.py:22
  27.2 1.1 %collective-permute-done.3.rest_4_ = bf16[64,512]{1,0:T(8,128)(2,1)S(1)} collective-permute-done((bf16[64,512]{1,0:T(8,128)(2,1)S(1)}, bf16[64,512]{1,0:T(8,128)(2,1)S(1)}, u32[]{:S(2)}, u32[]{:S(2)}) %collective-permute-start.3) | collective-permute-done | bytes 65568 | tf_op jit(solution)/shard_map/ppermute | solution.py:22
  28.3 0.0 copy-done.1
  28.3 0.0 copy-done.2
  28.3 2.0 %doc_sums.1 = (bf16[32,1024]{1,0:T(8,128)(2,1)}, bf16[32,1024]{1,0:T(8,128)(2,1)S(1)}, bf16[40,1024]{1,0:T(8,128)(2,1)S(1)}) custom-call(s32[1]{0:T(128)} %bitcast.pos_ref, s32[1]{0:T(128)S(6)} %copy.8.counts_ref, s32[32,2048]{1,0:T(8,128)S(1)} %copy-done.1, f32[64,512]{1,0:T(8,128)S(1)} %copy-done.2, bf16[128,512]{1,0:T(8,128)(2,1)S(1)} %collective-permute-done.rest_0_, ...), custom_call_target="tpu_custom_call" | custom-call | flops 268435456 | bytes 1048576 | tf_op jit(solution)/shard_map/doc_sums/pallas_call | solution.py:178
  30.3 0.8 %collective-permute-start.8 = (bf16[32,1024]{1,0:T(8,128)(2,1)S(1)}, bf16[32,1024]{1,0:T(8,128)(2,1)S(1)}, u32[]{:S(2)}, u32[]{:S(2)}) collective-permute-start(bf16[32,1024]{1,0:T(8,128)(2,1)S(1)} %get-tuple-element.14), channel_id=1, source_target_pairs={{0,1},{1,0},{2,3},{3,2},{4,5},{5,4},{6,7},{7,6},{8,9},{9,8},{10,11... | collective-permute-start | bytes 196616 | tf_op jit(solution)/shard_map/ppermute | solution.py:22
  31.1 1.5 %collective-permute-start.7 = (bf16[32,1024]{1,0:T(8,128)(2,1)S(1)}, bf16[32,1024]{1,0:T(8,128)(2,1)S(1)}, u32[]{:S(2)}, u32[]{:S(2)}) collective-permute-start(bf16[32,1024]{1,0:T(8,128)(2,1)S(1)} %get-tuple-element.14), channel_id=1, source_target_pairs={{0,2},{1,3},{2,0},{3,1},{4,6},{5,7},{6,4},{7,5},{8,10},{9,11},{10,... | collective-permute-start | bytes 196616 | tf_op jit(solution)/shard_map/ppermute | solution.py:22
  32.6 1.2 %collective-permute-start.6 = (bf16[32,1024]{1,0:T(8,128)(2,1)S(1)}, bf16[32,1024]{1,0:T(8,128)(2,1)S(1)}, u32[]{:S(2)}, u32[]{:S(2)}) collective-permute-start(bf16[32,1024]{1,0:T(8,128)(2,1)S(1)} %get-tuple-element.14), channel_id=1, source_target_pairs={{0,3},{1,2},{2,1},{3,0},{4,7},{5,6},{6,5},{7,4},{8,11},{9,10},{10,... | collective-permute-start | bytes 196616 | tf_op jit(solution)/shard_map/ppermute | solution.py:22
  33.8 0.0 collective-permute-start.19
  33.8 2.6 %collective-permute-start.17 = (bf16[40,1024]{1,0:T(8,128)(2,1)S(1)}, bf16[40,1024]{1,0:T(8,128)(2,1)S(1)}, u32[]{:S(2)}, u32[]{:S(2)}) collective-permute-start(bf16[40,1024]{1,0:T(8,128)(2,1)S(1)} %get-tuple-element.15.rest_8_), channel_id=1, source_target_pairs={{0,16},{4,20},{8,24},{12,28},{16,0},{20,4},{24,8},{28,12},{1,17},{... | collective-permute-start | bytes 245768 | tf_op jit(solution)/shard_map/ppermute | solution.py:22
  36.4 0.0 collective-permute-done.8
  36.4 1.6 %collective-permute-start.16 = (bf16[40,1024]{1,0:T(8,128)(2,1)S(1)}, bf16[40,1024]{1,0:T(8,128)(2,1)S(1)}, u32[]{:S(2)}, u32[]{:S(2)}) collective-permute-start(bf16[40,1024]{1,0:T(8,128)(2,1)S(1)} %get-tuple-element.15.rest_8_), channel_id=1, source_target_pairs={{0,8},{4,12},{8,0},{12,4},{16,24},{20,28},{24,16},{28,20},{1,9},{5... | collective-permute-start | bytes 245768 | tf_op jit(solution)/shard_map/ppermute | solution.py:22
  38.0 0.0 collective-permute-done.7
  38.0 0.0 collective-permute-done.6
  38.0 3.5 %collective-permute-start.11 = (bf16[32,1024]{1,0:T(8,128)(2,1)S(1)}, bf16[32,1024]{1,0:T(8,128)(2,1)S(1)}, u32[]{:S(2)}, u32[]{:S(2)}) collective-permute-start(bf16[32,1024]{1,0:T(8,128)(2,1)S(1)} %get-tuple-element.16), channel_id=1, source_target_pairs={{0,24},{4,28},{8,16},{12,20},{16,8},{20,12},{24,0},{28,4},{1,25},{... | collective-permute-start | bytes 196616 | tf_op jit(solution)/shard_map/ppermute | solution.py:22
  41.5 0.3 collective-permute-done.17.rest_10_
  41.8 0.5 collective-permute-start.18
  42.3 3.6 %collective-permute-start.10 = (bf16[32,1024]{1,0:T(8,128)(2,1)S(1)}, bf16[32,1024]{1,0:T(8,128)(2,1)S(1)}, u32[]{:S(2)}, u32[]{:S(2)}) collective-permute-start(bf16[32,1024]{1,0:T(8,128)(2,1)S(1)} %get-tuple-element.17), channel_id=1, source_target_pairs={{0,16},{4,20},{8,24},{12,28},{16,0},{20,4},{24,8},{28,12},{1,17},{... | collective-permute-start | bytes 196616 | tf_op jit(solution)/shard_map/ppermute | solution.py:22
  45.9 0.0 collective-permute-done.19.rest_12_
  45.9 0.0 collective-permute-start.21
  45.9 0.0 collective-permute-done.16.rest_9_
  45.9 0.1 collective-permute-start.9
  45.9 0.0 collective-permute-done.11.rest_3_
  46.0 0.5 collective-permute-start.12
  46.4 2.3 %collective-permute-done.10.rest_2_ = bf16[32,1024]{1,0:T(8,128)(2,1)S(1)} collective-permute-done((bf16[32,1024]{1,0:T(8,128)(2,1)S(1)}, bf16[32,1024]{1,0:T(8,128)(2,1)S(1)}, u32[]{:S(2)}, u32[]{:S(2)}) %collective-permute-start.10) | collective-permute-done | bytes 65568 | tf_op jit(solution)/shard_map/ppermute | solution.py:22
  48.8 0.0 collective-permute-start.20
  48.8 0.0 collective-permute-done.18.rest_11_
  48.8 0.5 collective-permute-start.22
  49.3 1.1 %collective-permute-done.9.rest_1_ = bf16[32,1024]{1,0:T(8,128)(2,1)S(1)} collective-permute-done((bf16[32,1024]{1,0:T(8,128)(2,1)S(1)}, bf16[32,1024]{1,0:T(8,128)(2,1)S(1)}, u32[]{:S(2)}, u32[]{:S(2)}) %collective-permute-start.9) | collective-permute-done | bytes 65568 | tf_op jit(solution)/shard_map/ppermute | solution.py:22
  50.4 0.0 collective-permute-start.15
  50.4 0.0 collective-permute-done.12.rest_4_
  50.4 0.5 collective-permute-start.14
  50.9 0.0 collective-permute-done.21.rest_14_
  50.9 0.1 collective-permute-start.13
  51.0 0.0 collective-permute-done.20.rest_13_
  51.0 0.7 %collective-permute-done.15.rest_7_ = bf16[32,1024]{1,0:T(8,128)(2,1)S(1)} collective-permute-done((bf16[32,1024]{1,0:T(8,128)(2,1)S(1)}, bf16[32,1024]{1,0:T(8,128)(2,1)S(1)}, u32[]{:S(2)}, u32[]{:S(2)}) %collective-permute-start.15) | collective-permute-done | bytes 65568 | tf_op jit(solution)/shard_map/ppermute | solution.py:22
  51.6 0.2 collective-permute-done.14.rest_6_
  51.8 0.4 collective-permute-done.13.rest_5_
  52.1 0.0 collective-permute-done.22.rest_15_
  52.1 1.8 %fisher_block.1 = f32[512,1024]{1,0:T(8,128)} custom-call(s32[1]{0:T(128)} %bitcast.3.half_ref, bf16[32,1024]{1,0:T(8,128)(2,1)S(1)} %get-tuple-element.19.rest_0_, bf16[32,1024]{1,0:T(8,128)(2,1)S(1)} %collective-permute-done.9.rest_1_, bf16[32,1024]{1,0:T(8,128)(2,1)S(1)} %collective-permute-done.10.rest_2_, ...), custom_call_target="tpu_custom_call" | custom-call | flops 268435456 | bytes 2097152 | tf_op jit(solution)/shard_map/fisher_block/pallas_call | solution.py:219
  (2 shorter events, 0.1 us)
Async XLA Ops:
  0.6 14.1 %copy-start = (bf16[3584,64]{0,1:T(8,128)(2,1)S(1)}, bf16[3584,64]{0,1:T(8,128)(2,1)}, u32[]{:S(2)}) copy-start(bf16[3584,64]{0,1:T(8,128)(2,1)} %param.8) | copy-start | bytes 1376260
  10.3 7.5 %collective-permute-start = (bf16[128,512]{1,0:T(8,128)(2,1)}, bf16[128,512]{1,0:T(8,128)(2,1)S(1)}, u32[]{:S(2)}, u32[]{:S(2)}) collective-permute-start(bf16[128,512]{1,0:T(8,128)(2,1)} %get-tuple-element.10), channel_id=1, source_target_pairs={{0,1},{1,0},{2,3},{3,2},{4,5},{5,4},{6,7},{7,6},{8,9},{9,8},{10,11... | collective-permute-start | bytes 393224 | tf_op jit(solution)/shard_map/ppermute | solution.py:22
  13.2 8.0 %collective-permute-start.1 = (bf16[128,512]{1,0:T(8,128)(2,1)}, bf16[128,512]{1,0:T(8,128)(2,1)S(1)}, u32[]{:S(2)}, u32[]{:S(2)}) collective-permute-start(bf16[128,512]{1,0:T(8,128)(2,1)} %get-tuple-element.11), channel_id=1, source_target_pairs={{0,2},{1,3},{2,0},{3,1},{4,6},{5,7},{6,4},{7,5},{8,10},{9,11},{10,... | collective-permute-start | bytes 393224 | tf_op jit(solution)/shard_map/ppermute | solution.py:22
  14.8 13.5 %copy-start.1 = (s32[32,2048]{1,0:T(8,128)S(1)}, s32[32,2048]{1,0:T(8,128)}, u32[]{:S(2)}) copy-start(s32[32,2048]{1,0:T(8,128)} %seg_ref.1) | copy-start | bytes 786436
  14.8 13.5 %copy-start.2 = (f32[64,512]{1,0:T(8,128)S(1)}, f32[64,512]{1,0:T(8,128)}, u32[]{:S(2)}) copy-start(f32[64,512]{1,0:T(8,128)} %get-tuple-element.9.dy_own_ref) | copy-start | bytes 393220
  14.8 6.5 %collective-permute-start.2 = (bf16[128,512]{1,0:T(8,128)(2,1)}, bf16[128,512]{1,0:T(8,128)(2,1)S(1)}, u32[]{:S(2)}, u32[]{:S(2)}) collective-permute-start(bf16[128,512]{1,0:T(8,128)(2,1)} %get-tuple-element.12), channel_id=1, source_target_pairs={{0,3},{1,2},{2,1},{3,0},{4,7},{5,6},{6,5},{7,4},{8,11},{9,10},{10,... | collective-permute-start | bytes 393224 | tf_op jit(solution)/shard_map/ppermute | solution.py:22
  21.3 5.2 %collective-permute-start.5 = (bf16[64,512]{1,0:T(8,128)(2,1)S(1)}, bf16[64,512]{1,0:T(8,128)(2,1)S(1)}, u32[]{:S(2)}, u32[]{:S(2)}) collective-permute-start(bf16[64,512]{1,0:T(8,128)(2,1)S(1)} %add_convert_fusion.rest_3_), channel_id=1, source_target_pairs={{0,3},{1,2},{2,1},{3,0},{4,7},{5,6},{6,5},{7,4},{8,11},{9,10},{10,... | collective-permute-start | bytes 196616 | tf_op jit(solution)/shard_map/ppermute | solution.py:22
  22.8 4.4 %collective-permute-start.4 = (bf16[64,512]{1,0:T(8,128)(2,1)S(1)}, bf16[64,512]{1,0:T(8,128)(2,1)S(1)}, u32[]{:S(2)}, u32[]{:S(2)}) collective-permute-start(bf16[64,512]{1,0:T(8,128)(2,1)S(1)} %add_convert_fusion.rest_3_), channel_id=1, source_target_pairs={{0,2},{1,3},{2,0},{3,1},{4,6},{5,7},{6,4},{7,5},{8,10},{9,11},{10,... | collective-permute-start | bytes 196616 | tf_op jit(solution)/shard_map/ppermute | solution.py:22
  24.0 4.3 %collective-permute-start.3 = (bf16[64,512]{1,0:T(8,128)(2,1)S(1)}, bf16[64,512]{1,0:T(8,128)(2,1)S(1)}, u32[]{:S(2)}, u32[]{:S(2)}) collective-permute-start(bf16[64,512]{1,0:T(8,128)(2,1)S(1)} %add_convert_fusion.rest_3_), channel_id=1, source_target_pairs={{0,1},{1,0},{2,3},{3,2},{4,5},{5,4},{6,7},{7,6},{8,9},{9,8},{10,11... | collective-permute-start | bytes 196616 | tf_op jit(solution)/shard_map/ppermute | solution.py:22
  30.3 6.1 %collective-permute-start.8 = (bf16[32,1024]{1,0:T(8,128)(2,1)S(1)}, bf16[32,1024]{1,0:T(8,128)(2,1)S(1)}, u32[]{:S(2)}, u32[]{:S(2)}) collective-permute-start(bf16[32,1024]{1,0:T(8,128)(2,1)S(1)} %get-tuple-element.14), channel_id=1, source_target_pairs={{0,1},{1,0},{2,3},{3,2},{4,5},{5,4},{6,7},{7,6},{8,9},{9,8},{10,11... | collective-permute-start | bytes 196616 | tf_op jit(solution)/shard_map/ppermute | solution.py:22
  31.1 6.9 %collective-permute-start.7 = (bf16[32,1024]{1,0:T(8,128)(2,1)S(1)}, bf16[32,1024]{1,0:T(8,128)(2,1)S(1)}, u32[]{:S(2)}, u32[]{:S(2)}) collective-permute-start(bf16[32,1024]{1,0:T(8,128)(2,1)S(1)} %get-tuple-element.14), channel_id=1, source_target_pairs={{0,2},{1,3},{2,0},{3,1},{4,6},{5,7},{6,4},{7,5},{8,10},{9,11},{10,... | collective-permute-start | bytes 196616 | tf_op jit(solution)/shard_map/ppermute | solution.py:22
  32.6 5.3 %collective-permute-start.6 = (bf16[32,1024]{1,0:T(8,128)(2,1)S(1)}, bf16[32,1024]{1,0:T(8,128)(2,1)S(1)}, u32[]{:S(2)}, u32[]{:S(2)}) collective-permute-start(bf16[32,1024]{1,0:T(8,128)(2,1)S(1)} %get-tuple-element.14), channel_id=1, source_target_pairs={{0,3},{1,2},{2,1},{3,0},{4,7},{5,6},{6,5},{7,4},{8,11},{9,10},{10,... | collective-permute-start | bytes 196616 | tf_op jit(solution)/shard_map/ppermute | solution.py:22
  33.8 12.1 %collective-permute-start.19 = (bf16[40,1024]{1,0:T(8,128)(2,1)S(1)}, bf16[40,1024]{1,0:T(8,128)(2,1)S(1)}, u32[]{:S(2)}, u32[]{:S(2)}) collective-permute-start(bf16[40,1024]{1,0:T(8,128)(2,1)S(1)} %get-tuple-element.15.rest_8_), channel_id=1, source_target_pairs={{0,4},{4,0},{8,12},{12,8},{16,20},{20,16},{24,28},{28,24},{1,5},{5... | collective-permute-start | bytes 245768 | tf_op jit(solution)/shard_map/ppermute | solution.py:22
  33.8 8.0 %collective-permute-start.17 = (bf16[40,1024]{1,0:T(8,128)(2,1)S(1)}, bf16[40,1024]{1,0:T(8,128)(2,1)S(1)}, u32[]{:S(2)}, u32[]{:S(2)}) collective-permute-start(bf16[40,1024]{1,0:T(8,128)(2,1)S(1)} %get-tuple-element.15.rest_8_), channel_id=1, source_target_pairs={{0,16},{4,20},{8,24},{12,28},{16,0},{20,4},{24,8},{28,12},{1,17},{... | collective-permute-start | bytes 245768 | tf_op jit(solution)/shard_map/ppermute | solution.py:22
  36.4 9.5 %collective-permute-start.16 = (bf16[40,1024]{1,0:T(8,128)(2,1)S(1)}, bf16[40,1024]{1,0:T(8,128)(2,1)S(1)}, u32[]{:S(2)}, u32[]{:S(2)}) collective-permute-start(bf16[40,1024]{1,0:T(8,128)(2,1)S(1)} %get-tuple-element.15.rest_8_), channel_id=1, source_target_pairs={{0,8},{4,12},{8,0},{12,4},{16,24},{20,28},{24,16},{28,20},{1,9},{5... | collective-permute-start | bytes 245768 | tf_op jit(solution)/shard_map/ppermute | solution.py:22
  38.0 7.9 %collective-permute-start.11 = (bf16[32,1024]{1,0:T(8,128)(2,1)S(1)}, bf16[32,1024]{1,0:T(8,128)(2,1)S(1)}, u32[]{:S(2)}, u32[]{:S(2)}) collective-permute-start(bf16[32,1024]{1,0:T(8,128)(2,1)S(1)} %get-tuple-element.16), channel_id=1, source_target_pairs={{0,24},{4,28},{8,16},{12,20},{16,8},{20,12},{24,0},{28,4},{1,25},{... | collective-permute-start | bytes 196616 | tf_op jit(solution)/shard_map/ppermute | solution.py:22
  41.8 7.0 %collective-permute-start.18 = (bf16[40,1024]{1,0:T(8,128)(2,1)S(1)}, bf16[40,1024]{1,0:T(8,128)(2,1)S(1)}, u32[]{:S(2)}, u32[]{:S(2)}) collective-permute-start(bf16[40,1024]{1,0:T(8,128)(2,1)S(1)} %collective-permute-done.17.rest_10_), channel_id=1, source_target_pairs={{0,8},{4,12},{8,0},{12,4},{16,24},{20,28},{24,16},{28,20},{1,9},{5... | collective-permute-start | bytes 245768 | tf_op jit(solution)/shard_map/ppermute | solution.py:22
  42.3 6.5 %collective-permute-start.10 = (bf16[32,1024]{1,0:T(8,128)(2,1)S(1)}, bf16[32,1024]{1,0:T(8,128)(2,1)S(1)}, u32[]{:S(2)}, u32[]{:S(2)}) collective-permute-start(bf16[32,1024]{1,0:T(8,128)(2,1)S(1)} %get-tuple-element.17), channel_id=1, source_target_pairs={{0,16},{4,20},{8,24},{12,28},{16,0},{20,4},{24,8},{28,12},{1,17},{... | collective-permute-start | bytes 196616 | tf_op jit(solution)/shard_map/ppermute | solution.py:22
  45.9 5.0 %collective-permute-start.21 = (bf16[40,1024]{1,0:T(8,128)(2,1)S(1)}, bf16[40,1024]{1,0:T(8,128)(2,1)S(1)}, u32[]{:S(2)}, u32[]{:S(2)}) collective-permute-start(bf16[40,1024]{1,0:T(8,128)(2,1)S(1)} %collective-permute-done.17.rest_10_), channel_id=1, source_target_pairs={{0,4},{4,0},{8,12},{12,8},{16,20},{20,16},{24,28},{28,24},{1,5},{5... | collective-permute-start | bytes 245768 | tf_op jit(solution)/shard_map/ppermute | solution.py:22
  45.9 4.5 %collective-permute-start.9 = (bf16[32,1024]{1,0:T(8,128)(2,1)S(1)}, bf16[32,1024]{1,0:T(8,128)(2,1)S(1)}, u32[]{:S(2)}, u32[]{:S(2)}) collective-permute-start(bf16[32,1024]{1,0:T(8,128)(2,1)S(1)} %get-tuple-element.18), channel_id=1, source_target_pairs={{0,8},{4,12},{8,0},{12,4},{16,24},{20,28},{24,16},{28,20},{1,9},{5... | collective-permute-start | bytes 196616 | tf_op jit(solution)/shard_map/ppermute | solution.py:22
  46.0 4.4 %collective-permute-start.12 = (bf16[32,1024]{1,0:T(8,128)(2,1)S(1)}, bf16[32,1024]{1,0:T(8,128)(2,1)S(1)}, u32[]{:S(2)}, u32[]{:S(2)}) collective-permute-start(bf16[32,1024]{1,0:T(8,128)(2,1)S(1)} %get-tuple-element.19.rest_0_), channel_id=1, source_target_pairs={{0,4},{4,0},{8,12},{12,8},{16,20},{20,16},{24,28},{28,24},{1,5},{5... | collective-permute-start | bytes 196616 | tf_op jit(solution)/shard_map/ppermute | solution.py:22
  48.8 2.2 %collective-permute-start.20 = (bf16[40,1024]{1,0:T(8,128)(2,1)S(1)}, bf16[40,1024]{1,0:T(8,128)(2,1)S(1)}, u32[]{:S(2)}, u32[]{:S(2)}) collective-permute-start(bf16[40,1024]{1,0:T(8,128)(2,1)S(1)} %collective-permute-done.16.rest_9_), channel_id=1, source_target_pairs={{0,4},{4,0},{8,12},{12,8},{16,20},{20,16},{24,28},{28,24},{1,5},{5... | collective-permute-start | bytes 245768 | tf_op jit(solution)/shard_map/ppermute | solution.py:22
  48.8 3.4 %collective-permute-start.22 = (bf16[40,1024]{1,0:T(8,128)(2,1)S(1)}, bf16[40,1024]{1,0:T(8,128)(2,1)S(1)}, u32[]{:S(2)}, u32[]{:S(2)}) collective-permute-start(bf16[40,1024]{1,0:T(8,128)(2,1)S(1)} %collective-permute-done.18.rest_11_), channel_id=1, source_target_pairs={{0,4},{4,0},{8,12},{12,8},{16,20},{20,16},{24,28},{28,24},{1,5},{5... | collective-permute-start | bytes 245768 | tf_op jit(solution)/shard_map/ppermute | solution.py:22
  50.4 1.3 %collective-permute-start.15 = (bf16[32,1024]{1,0:T(8,128)(2,1)S(1)}, bf16[32,1024]{1,0:T(8,128)(2,1)S(1)}, u32[]{:S(2)}, u32[]{:S(2)}) collective-permute-start(bf16[32,1024]{1,0:T(8,128)(2,1)S(1)} %collective-permute-done.11.rest_3_), channel_id=1, source_target_pairs={{0,4},{4,0},{8,12},{12,8},{16,20},{20,16},{24,28},{28,24},{1,5},{5... | collective-permute-start | bytes 196616 | tf_op jit(solution)/shard_map/ppermute | solution.py:22
  50.4 1.4 %collective-permute-start.14 = (bf16[32,1024]{1,0:T(8,128)(2,1)S(1)}, bf16[32,1024]{1,0:T(8,128)(2,1)S(1)}, u32[]{:S(2)}, u32[]{:S(2)}) collective-permute-start(bf16[32,1024]{1,0:T(8,128)(2,1)S(1)} %collective-permute-done.10.rest_2_), channel_id=1, source_target_pairs={{0,4},{4,0},{8,12},{12,8},{16,20},{20,16},{24,28},{28,24},{1,5},{5... | collective-permute-start | bytes 196616 | tf_op jit(solution)/shard_map/ppermute | solution.py:22
  50.9 1.3 %collective-permute-start.13 = (bf16[32,1024]{1,0:T(8,128)(2,1)S(1)}, bf16[32,1024]{1,0:T(8,128)(2,1)S(1)}, u32[]{:S(2)}, u32[]{:S(2)}) collective-permute-start(bf16[32,1024]{1,0:T(8,128)(2,1)S(1)} %collective-permute-done.9.rest_1_), channel_id=1, source_target_pairs={{0,4},{4,0},{8,12},{12,8},{16,20},{20,16},{24,28},{28,24},{1,5},{5... | collective-permute-start | bytes 196616 | tf_op jit(solution)/shard_map/ppermute | solution.py:22

commit v4 on v3

--- a/solution.py
+++ b/solution.py
@@ -14,116 +14,182 @@
 TN = (((0,), (0,)), ((), ()))
 SMEM = pl.BlockSpec(memory_space=pltpu.SMEM)
 VMEM = pl.BlockSpec(memory_space=pltpu.VMEM)
+HBM = pl.BlockSpec(memory_space=pltpu.HBM)
 DIGITS = (65536, 256, 1)
 DIGIT_ROWS = 8
+FIRST_GRANT = 58 << 20
+SECOND_GRANT = 48 << 20
 
 
 def swap(value, axis, step):
     return lax.ppermute(value, axis, [(i, i ^ step) for i in range(lax.axis_size(axis))])
 
 
-def peers_kernel(pos_ref, acts_ref, grads_ref, proj_in_ref, proj_out_ref, *rest):
-    outs, own_ref, weights = rest[:-2], rest[-2], rest[-1]
-    size = len(outs) + 1
-    step = pl.program_id(0)
+def stream(copies, depth, work):
+    for copy in copies[:depth]:
+        copy.start()
+    for n, copy in enumerate(copies):
+        copy.wait()
+        if n + depth < len(copies):
+            copies[n + depth].start()
+        work(n)
+
+
+def project(proj_ref, piece_ref, start, sums_ref, done):
+    stop = start + piece_ref.shape[1]
+    partial = lax.dot_general(
+        proj_ref[:, start:stop], piece_ref[...], NT, preferred_element_type=F32
+    )
+    if start > 0:
+        partial = sums_ref[...] + partial
+    if stop < proj_ref.shape[1]:
+        sums_ref[...] = partial
+    else:
+        done(partial)
+
+
+def chunk_copies(acts_ref, block, chunk, buffers, sems, first):
+    width = buffers.shape[2]
+    rows = pl.ds(pl.multiple_of(block * chunk, chunk), chunk)
+    return [
+        pltpu.make_async_copy(
+            acts_ref.at[rows, n * width : (n + 1) * width],
+            buffers.at[first + n],
+            sems.at[first + n],
+        )
+        for n in range(acts_ref.shape[1] // width)
+    ]
+
+
+def pieces_of(width, most):
+    return max(n for n in range(1, most + 1) if width % (128 * n) == 0)
+
+
+def peers_kernel(size, pos_ref, acts_ref, proj_ref, *rest):
+    outs, (buffers, sums_ref, sems) = rest[: size - 1], rest[size - 1 :]
+    chunk = buffers.shape[1]
+    pieces = buffers.shape[0] // (size - 1)
+    copies = []
+    for k in range(1, size):
+        block = pos_ref[0] ^ k
+        copies += chunk_copies(acts_ref, block, chunk, buffers, sems, (k - 1) * pieces)
+
+    def work(n):
+        def done(x):
+            outs[n // pieces][...] = x.astype(BF16)
+
+        piece = buffers.at[n]
+        project(proj_ref, piece, n % pieces * piece.shape[1], sums_ref, done)
+
+    stream(copies, 3, work)
+
+
+def peer_partials(pos, acts, proj_t, size):
+    tokens, width = acts.shape
+    rank = proj_t.shape[0]
+    chunk = tokens // size
+    pieces = pieces_of(width, 2)
+    count = (size - 1) * pieces
+    outs = [jax.ShapeDtypeStruct((rank, chunk), BF16)] * (size - 1)
+    return pl.pallas_call(
+        functools.partial(peers_kernel, size),
+        in_specs=[SMEM, HBM, VMEM],
+        out_specs=[VMEM] * len(outs),
+        out_shape=outs,
+        scratch_shapes=[
+            pltpu.VMEM((count, chunk, width // pieces), BF16),
+            pltpu.VMEM((rank, chunk), F32),
+            pltpu.SemaphoreType.DMA((count,)),
+        ],
+        cost_estimate=pl.CostEstimate(
+            flops=2 * chunk * (size - 1) * rank * width,
+            bytes_accessed=2 * chunk * (size - 1) * width,
+            transcendentals=0,
+        ),
+        compiler_params=pltpu.CompilerParams(vmem_limit_bytes=FIRST_GRANT),
+        name="peer_partials",
+    )(pos, acts, proj_t)
+
+
+def own_kernel(size, pos_ref, acts_ref, grads_ref, proj_in_ref, proj_out_ref, *rest):
+    own_ref, dy_refs = rest[0], rest[1 : size + 1]
+    weights, acts_buf, grads_buf, sums_ref, acts_sem, grads_sem = rest[size + 1 :]
+    pos = pos_ref[0]
     rank = proj_out_ref.shape[0]
     part = rank // size
-
-    @pl.when(step == 0)
-    def _():
-        row = lax.broadcasted_iota(jnp.int32, (rank, rank), 0)
-        col = lax.broadcasted_iota(jnp.int32, (rank, rank), 1)
-        source = (pos_ref[0] ^ (row // part)) * part + row % part
-        pick = jnp.where(col == source, 1.0, 0.0).astype(BF16)
-        weights[...] = jnp.dot(pick, proj_out_ref[...], preferred_element_type=F32).astype(BF16)
-
-    dy = lax.dot_general(weights[...], grads_ref[...], NT, preferred_element_type=F32)
-    for n in range(size):
-
-        @pl.when(step == n)
-        def _():
-            lines = slice(n * part, (n + 1) * part)
-            own_ref[lines, :] = dy[:part, :]
-            for k in range(1, size):
-                lines = slice(rank + n * part, rank + (n + 1) * part)
-                outs[k - 1][lines, :] = dy[k * part : (k + 1) * part, :].astype(BF16)
-            if n + 1 < size:
-                x = lax.dot_general(
-                    proj_in_ref[...], acts_ref[...], NT, preferred_element_type=F32
-                )
-                outs[n][:rank, :] = x.astype(BF16)
-
-
-def peer_messages(pos, acts, grads, proj_in_t, proj_out_t, size):
+    chunk = acts_buf.shape[1]
+    parts, span, _ = grads_buf.shape
+    copies = [
+        pltpu.make_async_copy(
+            grads_ref.at[n * span : (n + 1) * span], grads_buf.at[n], grads_sem.at[n]
+        )
+        for n in range(parts)
+    ]
+    copies += chunk_copies(acts_ref, pos, chunk, acts_buf, acts_sem, 0)
+
+    def work(n):
+        if n == 0:
+            row = lax.broadcasted_iota(jnp.int32, (rank, rank), 0)
+            col = lax.broadcasted_iota(jnp.int32, (rank, rank), 1)
+            source = (pos ^ (row // part)) * part + row % part
+            pick = jnp.where(col == source, 1.0, 0.0).astype(BF16)
+            weights[...] = jnp.dot(
+                pick, proj_out_ref[...], preferred_element_type=F32
+            ).astype(BF16)
+        if n < parts:
+            dy = lax.dot_general(weights[...], grads_buf[n], NT, preferred_element_type=F32)
+            for m in range(span // chunk):
+                block = dy[:, m * chunk : (m + 1) * chunk]
+                first = (n * (span // chunk) + m) * part
+                for k in range(size):
+                    lines = block[k * part : (k + 1) * part, :]
+                    dy_refs[k][first : first + part, :] = lines.astype(dy_refs[k].dtype)
+        else:
+
+            def done(x):
+                own_ref[...] = x
+
+            piece = acts_buf.at[n - parts]
+            project(proj_in_ref, piece, (n - parts) * piece.shape[1], sums_ref, done)
+
+    stream(copies, 4, work)
+
+
+def own_partials(pos, acts, grads, proj_in_t, proj_out_t, size):
     tokens, acts_width = acts.shape
     grads_width = grads.shape[1]
     rank = proj_in_t.shape[0]
     chunk = tokens // size
-    whole = lambda n, p: (0, 0)
-    outs = [jax.ShapeDtypeStruct((2 * rank, chunk), BF16)] * (size - 1)
-    outs += [jax.ShapeDtypeStruct((rank, chunk), F32)]
+    pieces = pieces_of(acts_width, 2)
     return pl.pallas_call(
-        peers_kernel,
-        grid_spec=pltpu.PrefetchScalarGridSpec(
-            num_scalar_prefetch=1,
-            grid=(size,),
-            in_specs=[
-                pl.BlockSpec(
-                    (chunk, acts_width), lambda n, p: (p[0] ^ jnp.minimum(n + 1, size - 1), 0)
-                ),
-                pl.BlockSpec((chunk, grads_width), lambda n, p: (n, 0)),
-                pl.BlockSpec((rank, acts_width), whole),
-                pl.BlockSpec((rank, grads_width), whole),
-            ],
-            out_specs=[pl.BlockSpec(o.shape, whole) for o in outs],
-            scratch_shapes=[pltpu.VMEM((rank, grads_width), BF16)],
-        ),
-        out_shape=outs,
+        functools.partial(own_kernel, size),
+        in_specs=[SMEM, HBM, HBM, VMEM, VMEM],
+        out_specs=[VMEM] * (size + 1),
+        out_shape=[jax.ShapeDtypeStruct((rank, chunk), F32)] * 2
+        + [jax.ShapeDtypeStruct((rank, chunk), BF16)] * (size - 1),
+        scratch_shapes=[
+            pltpu.VMEM((rank, grads_width), BF16),
+            pltpu.VMEM((pieces, chunk, acts_width // pieces), BF16),
+            pltpu.VMEM((2, tokens // 2, grads_width), BF16),
+            pltpu.VMEM((rank, chunk), F32),
+            pltpu.SemaphoreType.DMA((pieces,)),
+            pltpu.SemaphoreType.DMA((2,)),
+        ],
         cost_estimate=pl.CostEstimate(
-            flops=2 * tokens * rank * (acts_width + grads_width),
-            bytes_accessed=2 * tokens * (acts_width + grads_width),
+            flops=2 * rank * (chunk * acts_width + tokens * grads_width),
+            bytes_accessed=2 * (chunk * acts_width + tokens * grads_width),
             transcendentals=0,
         ),
-        compiler_params=pltpu.CompilerParams(vmem_limit_bytes=58 << 20),
-        name="peer_messages",
+        compiler_params=pltpu.CompilerParams(vmem_limit_bytes=SECOND_GRANT),
+        name="own_partials",
     )(pos, acts, grads, proj_in_t, proj_out_t)
 
 
-def own_kernel(pos_ref, acts_ref, proj_ref, out_ref):
-    out_ref[...] = lax.dot_general(proj_ref[...], acts_ref[...], NT, preferred_element_type=F32)
-
-
-def own_partial(pos, acts, proj_t, size):
-    tokens, width = acts.shape
-    rank = proj_t.shape[0]
-    chunk = tokens // size
-    tile = min(256, chunk)
-    tiles = chunk // tile
-    return pl.pallas_call(
-        own_kernel,
-        grid_spec=pltpu.PrefetchScalarGridSpec(
-            num_scalar_prefetch=1,
-            grid=(tiles,),
-            in_specs=[
-                pl.BlockSpec((tile, width), lambda n, p: (p[0] * tiles + n, 0)),
-                pl.BlockSpec((rank, width), lambda n, p: (0, 0)),
-            ],
-            out_specs=pl.BlockSpec((rank, tile), lambda n, p: (0, n)),
-        ),
-        out_shape=jax.ShapeDtypeStruct((rank, chunk), F32),
-        cost_estimate=pl.CostEstimate(
-            flops=2 * chunk * width * rank, bytes_accessed=2 * chunk * width, transcendentals=0
-        ),
-        compiler_params=pltpu.CompilerParams(vmem_limit_bytes=48 << 20),
-        name="own_partial",
-    )(pos, acts, proj_t)
-
-
-def docs_kernel(size, pos_ref, counts_ref, seg_ref, dy_own_ref, *rest):
-    messages, xs = rest[: size - 1], rest[size - 1 : 2 * size - 1]
-    grads_ref, inner_ref, shared_ref, dy_ref, sums_ref = rest[2 * size - 1 :]
+def docs_kernel(size, pos_ref, counts_ref, seg_ref, dy_own_ref, x_own_ref, *rest):
+    messages = rest[: size - 1]
+    grads_ref, inner_ref, shared_ref, dy_ref, sums_ref = rest[size - 1 :]
     docs, _ = seg_ref.shape
-    rank, chunk = xs[0].shape
+    rank, chunk = x_own_ref.shape
     part = rank // size
     rows = dy_ref.shape[0] // size
     total = dy_own_ref[...]
@@ -146,9 +212,10 @@
         dy = dy_ref[pl.ds(pl.multiple_of(block * rows, rows), rows), :]
         high = dy.astype(BF16)
         low = (dy - high.astype(F32)).astype(BF16)
+        x = x_own_ref[...] if k == 0 else messages[k - 1][:rank, :]
         for piece in (high, low):
             masked = (seg[:, None, :] * piece[None, :, :]).reshape(docs * rows, chunk)
-            sums = sums + lax.dot_general(masked, xs[k][...], NT, preferred_element_type=F32)
+            sums = sums + lax.dot_general(masked, x, NT, preferred_element_type=F32)
     sums_ref[...] = sums
     lanes = 128 // rank
     for a in range(0, part, lanes):
@@ -169,15 +236,15 @@
     shared_ref[docs:, :] = digits.astype(F32).astype(BF16)
 
 
-def doc_sums(pos, counts, seg, dy_own, messages, xs):
-    size = len(xs)
+def doc_sums(pos, counts, seg, dy_own, x_own, messages):
+    size = len(messages) + 1
     docs, tokens = seg.shape
-    rank, chunk = xs[0].shape
+    rank, chunk = x_own.shape
     part = rank // size
     rows = -(-part // 16) * 16
     return pl.pallas_call(
         functools.partial(docs_kernel, size),
-        in_specs=[SMEM, SMEM] + [VMEM] * (1 + 2 * size),
+        in_specs=[SMEM, SMEM] + [VMEM] * (2 + size),
         out_specs=[VMEM, VMEM, VMEM],
         out_shape=[
             jax.ShapeDtypeStruct((docs, part * rank), BF16),
@@ -193,7 +260,7 @@
         ),
         compiler_params=pltpu.CompilerParams(vmem_limit_bytes=16 << 20),
         name="doc_sums",
-    )(pos, counts, seg, dy_own, *messages, *xs)
+    )(pos, counts, seg, dy_own, x_own, *messages)
 
 
 def fisher_kernel(shards, half_ref, *rest):
@@ -246,15 +313,16 @@
     pos1, half1 = pos.reshape(1), half.reshape(1)
 
     proj_in_t = proj_in.T
-    *messages, dy_own = peer_messages(pos1, hidden_acts, out_grads, proj_in_t, proj_out.T, size)
-    messages = [swap(messages[k - 1], "tensor", k) for k in steps]
-    x = own_partial(pos1, hidden_acts, proj_in_t, size)
-    rank = x.shape[0]
-    for message in messages:
-        x = x + message[:rank].astype(F32)
+    partials = peer_partials(pos1, hidden_acts, proj_in_t, size)
+    partials = [swap(partials[k - 1], "tensor", k) for k in steps]
+    x, dy_own, *dys = own_partials(
+        pos1, hidden_acts, out_grads, proj_in_t, proj_out.T, size
+    )
+    for partial in partials:
+        x = x + partial.astype(F32)
     x = x.astype(BF16)
-    xs = [x] + [swap(x, "tensor", k) for k in steps]
-    grads, inner, shared = doc_sums(pos1, doc_counts, segments, dy_own, messages, xs)
+    messages = [swap(jnp.concatenate([x, dys[k - 1]]), "tensor", k) for k in steps]
+    grads, inner, shared = doc_sums(pos1, doc_counts, segments, dy_own, x, messages)
 
     cols = {0: shared}
     for j in steps:

time: 54.1 us -> 51.4 us (0.950)
  Pallas kernels: 16.4 us -> 14.5 us
  waiting for transfers between devices: 11.2 us -> 10.3 us
    pallas_call x2, Pallas kernels: 12.6 us -> 10.7 us  [the longest x1 7.52 us: peer_partials(): pl.pallas_call(functools.partial(peers_kernel, size), in_specs=[SMEM, HBM...]
    ppermute x23, waiting for transfers between devices: 11.2 us -> 10.3 us  [swap(): lax.ppermute(value, axis, [(i, i ^ step) for i in range(lax.axis_size(axi...]
  transfers between devices with their start and end apart: 23 -> 23, of which waited for: 10 -> 9; matrix products, arithmetic and copies ran while one was open for 0% -> 0% of each run, Pallas kernels for 5% -> 6%
where the time goes in v4:
time: 51.4 us; the launch traced here: 51.2 us
  starting transfers between devices  24.9 us (48%)
  Pallas kernels  14.5 us (28%)
  waiting for transfers between devices  10.3 us (20%)
  between operations  1.41 us (3%)
    ppermute x23, starting transfers between devices, swap(): lax.ppermute(value, axis, [(i, i ^ step) for i in range(lax.axis_size(axi...  24.9 us
    ppermute x23, waiting for transfers between devices, swap(): lax.ppermute(value, axis, [(i, i ^ step) for i in range(lax.axis_size(axi...  10.3 us
    pallas_call x1, Pallas kernels, peer_partials(): pl.pallas_call(functools.partial(peers_kernel, size), in_specs=[SMEM, HBM...  7.52 us
    pallas_call x1, Pallas kernels, own_partials(): pl.pallas_call(functools.partial(own_kernel, size), in_specs=[SMEM, HBM,...  3.14 us
    pallas_call x1, Pallas kernels, doc_sums(): pl.pallas_call(functools.partial(docs_kernel, size), in_specs=[SMEM, SMEM...  2.01 us
    pallas_call x1, Pallas kernels, fisher_block(): pl.pallas_call(functools.partial(fisher_kernel, shards), grid_spec=pltpu....  1.83 us
  transfers between devices with their start and end apart: 23, of which 9 were waited for; matrix products, arithmetic and copies ran while one was open for 0% of the time, Pallas kernels for 6%

profile of v4, /device:TPU:0, one launch (start us, length us, event | category | flops | bytes accessed | tf_op | source)
XLA Modules:
  0.0 51.2 jit_solution(995202352126732989)
XLA Ops:
  0.6 0.0 copy-start
  0.6 0.0 copy-start.1
  0.7 0.0 copy-start.2
  0.7 7.5 %peer_partials.1 = (bf16[64,512]{1,0:T(8,128)(2,1)}, bf16[64,512]{1,0:T(8,128)(2,1)}, bf16[64,512]{1,0:T(8,128)(2,1)}) custom-call(s32[1]{0:T(128)} %bitcast.pos_ref, bf16[2048,3584]{1,0:T(8,128)(2,1)} %acts_ref.3, bf16[64,3584]{1,0:T(8,128)(2,1)} %bitcast.4), custom_call_target="tpu_custom_call" | custom-call | flops 704643072 | bytes 11010048 | tf_op jit(solution)/shard_map/peer_partials/pallas_call | solution.py:94
  8.2 3.0 %collective-permute-start = (bf16[64,512]{1,0:T(8,128)(2,1)}, bf16[64,512]{1,0:T(8,128)(2,1)S(1)}, u32[]{:S(2)}, u32[]{:S(2)}) collective-permute-start(bf16[64,512]{1,0:T(8,128)(2,1)} %get-tuple-element.15), channel_id=1, source_target_pairs={{0,1},{1,0},{2,3},{3,2},{4,5},{5,4},{6,7},{7,6},{8,9},{9,8},{10,11... | collective-permute-start | bytes 196616 | tf_op jit(solution)/shard_map/ppermute | solution.py:25
  11.2 1.5 %collective-permute-start.1 = (bf16[64,512]{1,0:T(8,128)(2,1)}, bf16[64,512]{1,0:T(8,128)(2,1)S(1)}, u32[]{:S(2)}, u32[]{:S(2)}) collective-permute-start(bf16[64,512]{1,0:T(8,128)(2,1)} %get-tuple-element.16), channel_id=1, source_target_pairs={{0,2},{1,3},{2,0},{3,1},{4,6},{5,7},{6,4},{7,5},{8,10},{9,11},{10,... | collective-permute-start | bytes 196616 | tf_op jit(solution)/shard_map/ppermute | solution.py:25
  12.7 0.0 collective-permute-start.2
  12.8 0.0 copy-done
  12.8 0.0 copy-done.1
  12.8 0.0 copy-done.2
  12.8 0.0 copy-start.3
  12.8 3.1 %own_partials.1 = (f32[64,512]{1,0:T(8,128)S(1)}, f32[64,512]{1,0:T(8,128)S(1)}, bf16[64,512]{1,0:T(8,128)(2,1)S(1)}, bf16[64,512]{1,0:T(8,128)(2,1)S(1)}, bf16[64,512]{1,0:T(8,128)(2,1)S(1)}) custom-call(s32[1]{0:T(128)} %bitcast.pos_ref, bf16[2048,3584]{1,0:T(8,128)(2,1)} %acts_ref.3, bf16[2048,1024]{1,0:T(8,128)(2,1)S(1)} %copy-done, ...), custom_call_target="tpu_custom_call" | custom-call | flops 503316480 | bytes 7864320 | tf_op jit(solution)/shard_map/own_partials/pallas_call | solution.py:164
  15.9 0.0 collective-permute-done
  15.9 0.0 collective-permute-done.1
  15.9 2.2 %collective-permute-done.2 = bf16[64,512]{1,0:T(8,128)(2,1)S(1)} collective-permute-done((bf16[64,512]{1,0:T(8,128)(2,1)}, bf16[64,512]{1,0:T(8,128)(2,1)S(1)}, u32[]{:S(2)}, u32[]{:S(2)}) %collective-permute-start.2) | collective-permute-done | bytes 65568 | tf_op jit(solution)/shard_map/ppermute | solution.py:25
  18.2 0.8 %collective-permute-start.5 = (bf16[128,512]{1,0:T(8,128)(2,1)S(1)}, bf16[128,512]{1,0:T(8,128)(2,1)S(1)}, u32[]{:S(2)}, u32[]{:S(2)}) collective-permute-start(bf16[128,512]{1,0:T(8,128)(2,1)S(1)} %get-tuple-element.28), channel_id=1, source_target_pairs={{0,3},{1,2},{2,1},{3,0},{4,7},{5,6},{6,5},{7,4},{8,11},{9,10},{10,... | collective-permute-start | bytes 393224 | tf_op jit(solution)/shard_map/ppermute | solution.py:25
  19.0 1.3 %collective-permute-start.4 = (bf16[128,512]{1,0:T(8,128)(2,1)S(1)}, bf16[128,512]{1,0:T(8,128)(2,1)S(1)}, u32[]{:S(2)}, u32[]{:S(2)}) collective-permute-start(bf16[128,512]{1,0:T(8,128)(2,1)S(1)} %get-tuple-element.29), channel_id=1, source_target_pairs={{0,2},{1,3},{2,0},{3,1},{4,6},{5,7},{6,4},{7,5},{8,10},{9,11},{10,... | collective-permute-start | bytes 393224 | tf_op jit(solution)/shard_map/ppermute | solution.py:25
  20.2 1.5 %collective-permute-start.3 = (bf16[128,512]{1,0:T(8,128)(2,1)S(1)}, bf16[128,512]{1,0:T(8,128)(2,1)S(1)}, u32[]{:S(2)}, u32[]{:S(2)}) collective-permute-start(bf16[128,512]{1,0:T(8,128)(2,1)S(1)} %get-tuple-element.30), channel_id=1, source_target_pairs={{0,1},{1,0},{2,3},{3,2},{4,5},{5,4},{6,7},{7,6},{8,9},{9,8},{10,11... | collective-permute-start | bytes 393224 | tf_op jit(solution)/shard_map/ppermute | solution.py:25
  22.4 2.0 %collective-permute-done.5.rest_2_ = bf16[128,512]{1,0:T(8,128)(2,1)S(1)} collective-permute-done((bf16[128,512]{1,0:T(8,128)(2,1)S(1)}, bf16[128,512]{1,0:T(8,128)(2,1)S(1)}, u32[]{:S(2)}, u32[]{:S(2)}) %collective-permute-start.5) | collective-permute-done | bytes 131104 | tf_op jit(solution)/shard_map/ppermute | solution.py:25
  24.4 1.1 %collective-permute-done.4.rest_1_ = bf16[128,512]{1,0:T(8,128)(2,1)S(1)} collective-permute-done((bf16[128,512]{1,0:T(8,128)(2,1)S(1)}, bf16[128,512]{1,0:T(8,128)(2,1)S(1)}, u32[]{:S(2)}, u32[]{:S(2)}) %collective-permute-start.4) | collective-permute-done | bytes 131104 | tf_op jit(solution)/shard_map/ppermute | solution.py:25
  25.5 0.0 collective-permute-done.3.rest_0_
  25.5 0.0 copy-done.3
  25.5 2.0 %doc_sums.1 = (bf16[32,1024]{1,0:T(8,128)(2,1)}, bf16[32,1024]{1,0:T(8,128)(2,1)S(1)}, bf16[40,1024]{1,0:T(8,128)(2,1)S(1)}) custom-call(s32[1]{0:T(128)} %bitcast.pos_ref, s32[1]{0:T(128)S(6)} %copy.8.counts_ref, s32[32,2048]{1,0:T(8,128)S(1)} %copy-done.3, f32[64,512]{1,0:T(8,128)S(1)} %get-tuple-element.13.dy_own_ref, ...), custom_call_target="tpu_custom_call" | custom-call | flops 268435456 | bytes 1048576 | tf_op jit(solution)/shard_map/doc_sums/pallas_call | solution.py:245
  27.5 1.2 %collective-permute-start.8 = (bf16[32,1024]{1,0:T(8,128)(2,1)S(1)}, bf16[32,1024]{1,0:T(8,128)(2,1)S(1)}, u32[]{:S(2)}, u32[]{:S(2)}) collective-permute-start(bf16[32,1024]{1,0:T(8,128)(2,1)S(1)} %get-tuple-element.22), channel_id=1, source_target_pairs={{0,1},{1,0},{2,3},{3,2},{4,5},{5,4},{6,7},{7,6},{8,9},{9,8},{10,11... | collective-permute-start | bytes 196616 | tf_op jit(solution)/shard_map/ppermute | solution.py:25
  28.7 1.0 %collective-permute-start.7 = (bf16[32,1024]{1,0:T(8,128)(2,1)S(1)}, bf16[32,1024]{1,0:T(8,128)(2,1)S(1)}, u32[]{:S(2)}, u32[]{:S(2)}) collective-permute-start(bf16[32,1024]{1,0:T(8,128)(2,1)S(1)} %get-tuple-element.22), channel_id=1, source_target_pairs={{0,2},{1,3},{2,0},{3,1},{4,6},{5,7},{6,4},{7,5},{8,10},{9,11},{10,... | collective-permute-start | bytes 196616 | tf_op jit(solution)/shard_map/ppermute | solution.py:25
  29.7 1.3 %collective-permute-start.6 = (bf16[32,1024]{1,0:T(8,128)(2,1)S(1)}, bf16[32,1024]{1,0:T(8,128)(2,1)S(1)}, u32[]{:S(2)}, u32[]{:S(2)}) collective-permute-start(bf16[32,1024]{1,0:T(8,128)(2,1)S(1)} %get-tuple-element.22), channel_id=1, source_target_pairs={{0,3},{1,2},{2,1},{3,0},{4,7},{5,6},{6,5},{7,4},{8,11},{9,10},{10,... | collective-permute-start | bytes 196616 | tf_op jit(solution)/shard_map/ppermute | solution.py:25
  31.0 0.0 collective-permute-start.19
  31.0 2.6 %collective-permute-start.17 = (bf16[40,1024]{1,0:T(8,128)(2,1)S(1)}, bf16[40,1024]{1,0:T(8,128)(2,1)S(1)}, u32[]{:S(2)}, u32[]{:S(2)}) collective-permute-start(bf16[40,1024]{1,0:T(8,128)(2,1)S(1)} %get-tuple-element.23.rest_8_), channel_id=1, source_target_pairs={{0,16},{4,20},{8,24},{12,28},{16,0},{20,4},{24,8},{28,12},{1,17},{... | collective-permute-start | bytes 245768 | tf_op jit(solution)/shard_map/ppermute | solution.py:25
  33.6 0.0 collective-permute-done.8
  33.6 1.6 %collective-permute-start.16 = (bf16[40,1024]{1,0:T(8,128)(2,1)S(1)}, bf16[40,1024]{1,0:T(8,128)(2,1)S(1)}, u32[]{:S(2)}, u32[]{:S(2)}) collective-permute-start(bf16[40,1024]{1,0:T(8,128)(2,1)S(1)} %get-tuple-element.23.rest_8_), channel_id=1, source_target_pairs={{0,8},{4,12},{8,0},{12,4},{16,24},{20,28},{24,16},{28,20},{1,9},{5... | collective-permute-start | bytes 245768 | tf_op jit(solution)/shard_map/ppermute | solution.py:25
  35.2 0.0 collective-permute-done.7
  35.2 0.0 collective-permute-done.6
  35.2 3.4 %collective-permute-start.11 = (bf16[32,1024]{1,0:T(8,128)(2,1)S(1)}, bf16[32,1024]{1,0:T(8,128)(2,1)S(1)}, u32[]{:S(2)}, u32[]{:S(2)}) collective-permute-start(bf16[32,1024]{1,0:T(8,128)(2,1)S(1)} %get-tuple-element.24), channel_id=1, source_target_pairs={{0,24},{4,28},{8,16},{12,20},{16,8},{20,12},{24,0},{28,4},{1,25},{... | collective-permute-start | bytes 196616 | tf_op jit(solution)/shard_map/ppermute | solution.py:25
  38.6 0.4 collective-permute-done.17.rest_10_
  39.0 0.5 %collective-permute-start.18 = (bf16[40,1024]{1,0:T(8,128)(2,1)S(1)}, bf16[40,1024]{1,0:T(8,128)(2,1)S(1)}, u32[]{:S(2)}, u32[]{:S(2)}) collective-permute-start(bf16[40,1024]{1,0:T(8,128)(2,1)S(1)} %collective-permute-done.17.rest_10_), channel_id=1, source_target_pairs={{0,8},{4,12},{8,0},{12,4},{16,24},{20,28},{24,16},{28,20},{1,9},{5... | collective-permute-start | bytes 245768 | tf_op jit(solution)/shard_map/ppermute | solution.py:25
  39.5 3.6 %collective-permute-start.10 = (bf16[32,1024]{1,0:T(8,128)(2,1)S(1)}, bf16[32,1024]{1,0:T(8,128)(2,1)S(1)}, u32[]{:S(2)}, u32[]{:S(2)}) collective-permute-start(bf16[32,1024]{1,0:T(8,128)(2,1)S(1)} %get-tuple-element.25), channel_id=1, source_target_pairs={{0,16},{4,20},{8,24},{12,28},{16,0},{20,4},{24,8},{28,12},{1,17},{... | collective-permute-start | bytes 196616 | tf_op jit(solution)/shard_map/ppermute | solution.py:25
  43.1 0.0 collective-permute-done.19.rest_12_
  43.1 0.0 collective-permute-start.21
  43.1 0.0 collective-permute-done.16.rest_9_
  43.1 0.1 collective-permute-start.9
  43.2 0.0 collective-permute-done.11.rest_3_
  43.2 0.5 collective-permute-start.12
  43.7 2.3 %collective-permute-done.10.rest_2_ = bf16[32,1024]{1,0:T(8,128)(2,1)S(1)} collective-permute-done((bf16[32,1024]{1,0:T(8,128)(2,1)S(1)}, bf16[32,1024]{1,0:T(8,128)(2,1)S(1)}, u32[]{:S(2)}, u32[]{:S(2)}) %collective-permute-start.10) | collective-permute-done | bytes 65568 | tf_op jit(solution)/shard_map/ppermute | solution.py:25
  46.0 0.0 collective-permute-start.20
  46.0 0.0 collective-permute-done.18.rest_11_
  46.0 0.5 collective-permute-start.22
  46.5 1.1 %collective-permute-done.9.rest_1_ = bf16[32,1024]{1,0:T(8,128)(2,1)S(1)} collective-permute-done((bf16[32,1024]{1,0:T(8,128)(2,1)S(1)}, bf16[32,1024]{1,0:T(8,128)(2,1)S(1)}, u32[]{:S(2)}, u32[]{:S(2)}) %collective-permute-start.9) | collective-permute-done | bytes 65568 | tf_op jit(solution)/shard_map/ppermute | solution.py:25
  47.6 0.0 collective-permute-start.15
  47.6 0.0 collective-permute-done.12.rest_4_
  47.6 0.5 collective-permute-start.14
  48.1 0.0 collective-permute-done.21.rest_14_
  48.1 0.1 collective-permute-start.13
  48.2 0.0 collective-permute-done.20.rest_13_
  48.2 0.7 %collective-permute-done.15.rest_7_ = bf16[32,1024]{1,0:T(8,128)(2,1)S(1)} collective-permute-done((bf16[32,1024]{1,0:T(8,128)(2,1)S(1)}, bf16[32,1024]{1,0:T(8,128)(2,1)S(1)}, u32[]{:S(2)}, u32[]{:S(2)}) %collective-permute-start.15) | collective-permute-done | bytes 65568 | tf_op jit(solution)/shard_map/ppermute | solution.py:25
  48.8 0.2 collective-permute-done.14.rest_6_
  49.0 0.4 collective-permute-done.13.rest_5_
  49.4 0.0 collective-permute-done.22.rest_15_
  49.4 1.8 %fisher_block.1 = f32[512,1024]{1,0:T(8,128)} custom-call(s32[1]{0:T(128)} %bitcast.3.half_ref, bf16[32,1024]{1,0:T(8,128)(2,1)S(1)} %get-tuple-element.27.rest_0_, bf16[32,1024]{1,0:T(8,128)(2,1)S(1)} %collective-permute-done.9.rest_1_, bf16[32,1024]{1,0:T(8,128)(2,1)S(1)} %collective-permute-done.10.rest_2_, ...), custom_call_target="tpu_custom_call" | custom-call | flops 268435456 | bytes 2097152 | tf_op jit(solution)/shard_map/fisher_block/pallas_call | solution.py:286
  (3 shorter events, 0.1 us)
Async XLA Ops:
  0.6 12.1 %copy-start = (bf16[2048,1024]{1,0:T(8,128)(2,1)S(1)}, bf16[2048,1024]{1,0:T(8,128)(2,1)}, u32[]{:S(2)}) copy-start(bf16[2048,1024]{1,0:T(8,128)(2,1)} %grads_ref.1) | copy-start | bytes 12582916
  0.6 12.1 %copy-start.1 = (bf16[3584,64]{0,1:T(8,128)(2,1)S(1)}, bf16[3584,64]{0,1:T(8,128)(2,1)}, u32[]{:S(2)}) copy-start(bf16[3584,64]{0,1:T(8,128)(2,1)} %param.8) | copy-start | bytes 1376260
  0.7 12.1 %copy-start.2 = (bf16[1024,64]{0,1:T(8,128)(2,1)S(1)}, bf16[1024,64]{0,1:T(8,128)(2,1)}, u32[]{:S(2)}) copy-start(bf16[1024,64]{0,1:T(8,128)(2,1)} %param.9) | copy-start | bytes 393220
  8.2 7.7 %collective-permute-start = (bf16[64,512]{1,0:T(8,128)(2,1)}, bf16[64,512]{1,0:T(8,128)(2,1)S(1)}, u32[]{:S(2)}, u32[]{:S(2)}) collective-permute-start(bf16[64,512]{1,0:T(8,128)(2,1)} %get-tuple-element.15), channel_id=1, source_target_pairs={{0,1},{1,0},{2,3},{3,2},{4,5},{5,4},{6,7},{7,6},{8,9},{9,8},{10,11... | collective-permute-start | bytes 196616 | tf_op jit(solution)/shard_map/ppermute | solution.py:25
  11.2 4.7 %collective-permute-start.1 = (bf16[64,512]{1,0:T(8,128)(2,1)}, bf16[64,512]{1,0:T(8,128)(2,1)S(1)}, u32[]{:S(2)}, u32[]{:S(2)}) collective-permute-start(bf16[64,512]{1,0:T(8,128)(2,1)} %get-tuple-element.16), channel_id=1, source_target_pairs={{0,2},{1,3},{2,0},{3,1},{4,6},{5,7},{6,4},{7,5},{8,10},{9,11},{10,... | collective-permute-start | bytes 196616 | tf_op jit(solution)/shard_map/ppermute | solution.py:25
  12.7 5.4 %collective-permute-start.2 = (bf16[64,512]{1,0:T(8,128)(2,1)}, bf16[64,512]{1,0:T(8,128)(2,1)S(1)}, u32[]{:S(2)}, u32[]{:S(2)}) collective-permute-start(bf16[64,512]{1,0:T(8,128)(2,1)} %get-tuple-element.17), channel_id=1, source_target_pairs={{0,3},{1,2},{2,1},{3,0},{4,7},{5,6},{6,5},{7,4},{8,11},{9,10},{10,... | collective-permute-start | bytes 196616 | tf_op jit(solution)/shard_map/ppermute | solution.py:25
  12.8 12.7 %copy-start.3 = (s32[32,2048]{1,0:T(8,128)S(1)}, s32[32,2048]{1,0:T(8,128)}, u32[]{:S(2)}) copy-start(s32[32,2048]{1,0:T(8,128)} %seg_ref.1) | copy-start | bytes 786436
  18.2 6.2 %collective-permute-start.5 = (bf16[128,512]{1,0:T(8,128)(2,1)S(1)}, bf16[128,512]{1,0:T(8,128)(2,1)S(1)}, u32[]{:S(2)}, u32[]{:S(2)}) collective-permute-start(bf16[128,512]{1,0:T(8,128)(2,1)S(1)} %get-tuple-element.28), channel_id=1, source_target_pairs={{0,3},{1,2},{2,1},{3,0},{4,7},{5,6},{6,5},{7,4},{8,11},{9,10},{10,... | collective-permute-start | bytes 393224 | tf_op jit(solution)/shard_map/ppermute | solution.py:25
  19.0 6.5 %collective-permute-start.4 = (bf16[128,512]{1,0:T(8,128)(2,1)S(1)}, bf16[128,512]{1,0:T(8,128)(2,1)S(1)}, u32[]{:S(2)}, u32[]{:S(2)}) collective-permute-start(bf16[128,512]{1,0:T(8,128)(2,1)S(1)} %get-tuple-element.29), channel_id=1, source_target_pairs={{0,2},{1,3},{2,0},{3,1},{4,6},{5,7},{6,4},{7,5},{8,10},{9,11},{10,... | collective-permute-start | bytes 393224 | tf_op jit(solution)/shard_map/ppermute | solution.py:25
  20.2 5.2 %collective-permute-start.3 = (bf16[128,512]{1,0:T(8,128)(2,1)S(1)}, bf16[128,512]{1,0:T(8,128)(2,1)S(1)}, u32[]{:S(2)}, u32[]{:S(2)}) collective-permute-start(bf16[128,512]{1,0:T(8,128)(2,1)S(1)} %get-tuple-element.30), channel_id=1, source_target_pairs={{0,1},{1,0},{2,3},{3,2},{4,5},{5,4},{6,7},{7,6},{8,9},{9,8},{10,11... | collective-permute-start | bytes 393224 | tf_op jit(solution)/shard_map/ppermute | solution.py:25
  27.5 6.1 %collective-permute-start.8 = (bf16[32,1024]{1,0:T(8,128)(2,1)S(1)}, bf16[32,1024]{1,0:T(8,128)(2,1)S(1)}, u32[]{:S(2)}, u32[]{:S(2)}) collective-permute-start(bf16[32,1024]{1,0:T(8,128)(2,1)S(1)} %get-tuple-element.22), channel_id=1, source_target_pairs={{0,1},{1,0},{2,3},{3,2},{4,5},{5,4},{6,7},{7,6},{8,9},{9,8},{10,11... | collective-permute-start | bytes 196616 | tf_op jit(solution)/shard_map/ppermute | solution.py:25
  28.7 6.5 %collective-permute-start.7 = (bf16[32,1024]{1,0:T(8,128)(2,1)S(1)}, bf16[32,1024]{1,0:T(8,128)(2,1)S(1)}, u32[]{:S(2)}, u32[]{:S(2)}) collective-permute-start(bf16[32,1024]{1,0:T(8,128)(2,1)S(1)} %get-tuple-element.22), channel_id=1, source_target_pairs={{0,2},{1,3},{2,0},{3,1},{4,6},{5,7},{6,4},{7,5},{8,10},{9,11},{10,... | collective-permute-start | bytes 196616 | tf_op jit(solution)/shard_map/ppermute | solution.py:25
  29.7 5.5 %collective-permute-start.6 = (bf16[32,1024]{1,0:T(8,128)(2,1)S(1)}, bf16[32,1024]{1,0:T(8,128)(2,1)S(1)}, u32[]{:S(2)}, u32[]{:S(2)}) collective-permute-start(bf16[32,1024]{1,0:T(8,128)(2,1)S(1)} %get-tuple-element.22), channel_id=1, source_target_pairs={{0,3},{1,2},{2,1},{3,0},{4,7},{5,6},{6,5},{7,4},{8,11},{9,10},{10,... | collective-permute-start | bytes 196616 | tf_op jit(solution)/shard_map/ppermute | solution.py:25
  31.0 12.1 %collective-permute-start.19 = (bf16[40,1024]{1,0:T(8,128)(2,1)S(1)}, bf16[40,1024]{1,0:T(8,128)(2,1)S(1)}, u32[]{:S(2)}, u32[]{:S(2)}) collective-permute-start(bf16[40,1024]{1,0:T(8,128)(2,1)S(1)} %get-tuple-element.23.rest_8_), channel_id=1, source_target_pairs={{0,4},{4,0},{8,12},{12,8},{16,20},{20,16},{24,28},{28,24},{1,5},{5... | collective-permute-start | bytes 245768 | tf_op jit(solution)/shard_map/ppermute | solution.py:25
  31.0 8.0 %collective-permute-start.17 = (bf16[40,1024]{1,0:T(8,128)(2,1)S(1)}, bf16[40,1024]{1,0:T(8,128)(2,1)S(1)}, u32[]{:S(2)}, u32[]{:S(2)}) collective-permute-start(bf16[40,1024]{1,0:T(8,128)(2,1)S(1)} %get-tuple-element.23.rest_8_), channel_id=1, source_target_pairs={{0,16},{4,20},{8,24},{12,28},{16,0},{20,4},{24,8},{28,12},{1,17},{... | collective-permute-start | bytes 245768 | tf_op jit(solution)/shard_map/ppermute | solution.py:25
  33.6 9.5 %collective-permute-start.16 = (bf16[40,1024]{1,0:T(8,128)(2,1)S(1)}, bf16[40,1024]{1,0:T(8,128)(2,1)S(1)}, u32[]{:S(2)}, u32[]{:S(2)}) collective-permute-start(bf16[40,1024]{1,0:T(8,128)(2,1)S(1)} %get-tuple-element.23.rest_8_), channel_id=1, source_target_pairs={{0,8},{4,12},{8,0},{12,4},{16,24},{20,28},{24,16},{28,20},{1,9},{5... | collective-permute-start | bytes 245768 | tf_op jit(solution)/shard_map/ppermute | solution.py:25
  35.2 8.0 %collective-permute-start.11 = (bf16[32,1024]{1,0:T(8,128)(2,1)S(1)}, bf16[32,1024]{1,0:T(8,128)(2,1)S(1)}, u32[]{:S(2)}, u32[]{:S(2)}) collective-permute-start(bf16[32,1024]{1,0:T(8,128)(2,1)S(1)} %get-tuple-element.24), channel_id=1, source_target_pairs={{0,24},{4,28},{8,16},{12,20},{16,8},{20,12},{24,0},{28,4},{1,25},{... | collective-permute-start | bytes 196616 | tf_op jit(solution)/shard_map/ppermute | solution.py:25
  39.0 7.0 %collective-permute-start.18 = (bf16[40,1024]{1,0:T(8,128)(2,1)S(1)}, bf16[40,1024]{1,0:T(8,128)(2,1)S(1)}, u32[]{:S(2)}, u32[]{:S(2)}) collective-permute-start(bf16[40,1024]{1,0:T(8,128)(2,1)S(1)} %collective-permute-done.17.rest_10_), channel_id=1, source_target_pairs={{0,8},{4,12},{8,0},{12,4},{16,24},{20,28},{24,16},{28,20},{1,9},{5... | collective-permute-start | bytes 245768 | tf_op jit(solution)/shard_map/ppermute | solution.py:25
  39.5 6.5 %collective-permute-start.10 = (bf16[32,1024]{1,0:T(8,128)(2,1)S(1)}, bf16[32,1024]{1,0:T(8,128)(2,1)S(1)}, u32[]{:S(2)}, u32[]{:S(2)}) collective-permute-start(bf16[32,1024]{1,0:T(8,128)(2,1)S(1)} %get-tuple-element.25), channel_id=1, source_target_pairs={{0,16},{4,20},{8,24},{12,28},{16,0},{20,4},{24,8},{28,12},{1,17},{... | collective-permute-start | bytes 196616 | tf_op jit(solution)/shard_map/ppermute | solution.py:25
  43.1 5.0 %collective-permute-start.21 = (bf16[40,1024]{1,0:T(8,128)(2,1)S(1)}, bf16[40,1024]{1,0:T(8,128)(2,1)S(1)}, u32[]{:S(2)}, u32[]{:S(2)}) collective-permute-start(bf16[40,1024]{1,0:T(8,128)(2,1)S(1)} %collective-permute-done.17.rest_10_), channel_id=1, source_target_pairs={{0,4},{4,0},{8,12},{12,8},{16,20},{20,16},{24,28},{28,24},{1,5},{5... | collective-permute-start | bytes 245768 | tf_op jit(solution)/shard_map/ppermute | solution.py:25
  43.1 4.5 %collective-permute-start.9 = (bf16[32,1024]{1,0:T(8,128)(2,1)S(1)}, bf16[32,1024]{1,0:T(8,128)(2,1)S(1)}, u32[]{:S(2)}, u32[]{:S(2)}) collective-permute-start(bf16[32,1024]{1,0:T(8,128)(2,1)S(1)} %get-tuple-element.26), channel_id=1, source_target_pairs={{0,8},{4,12},{8,0},{12,4},{16,24},{20,28},{24,16},{28,20},{1,9},{5... | collective-permute-start | bytes 196616 | tf_op jit(solution)/shard_map/ppermute | solution.py:25
  43.2 4.4 %collective-permute-start.12 = (bf16[32,1024]{1,0:T(8,128)(2,1)S(1)}, bf16[32,1024]{1,0:T(8,128)(2,1)S(1)}, u32[]{:S(2)}, u32[]{:S(2)}) collective-permute-start(bf16[32,1024]{1,0:T(8,128)(2,1)S(1)} %get-tuple-element.27.rest_0_), channel_id=1, source_target_pairs={{0,4},{4,0},{8,12},{12,8},{16,20},{20,16},{24,28},{28,24},{1,5},{5... | collective-permute-start | bytes 196616 | tf_op jit(solution)/shard_map/ppermute | solution.py:25
  46.0 2.2 %collective-permute-start.20 = (bf16[40,1024]{1,0:T(8,128)(2,1)S(1)}, bf16[40,1024]{1,0:T(8,128)(2,1)S(1)}, u32[]{:S(2)}, u32[]{:S(2)}) collective-permute-start(bf16[40,1024]{1,0:T(8,128)(2,1)S(1)} %collective-permute-done.16.rest_9_), channel_id=1, source_target_pairs={{0,4},{4,0},{8,12},{12,8},{16,20},{20,16},{24,28},{28,24},{1,5},{5... | collective-permute-start | bytes 245768 | tf_op jit(solution)/shard_map/ppermute | solution.py:25
  46.0 3.4 %collective-permute-start.22 = (bf16[40,1024]{1,0:T(8,128)(2,1)S(1)}, bf16[40,1024]{1,0:T(8,128)(2,1)S(1)}, u32[]{:S(2)}, u32[]{:S(2)}) collective-permute-start(bf16[40,1024]{1,0:T(8,128)(2,1)S(1)} %collective-permute-done.18.rest_11_), channel_id=1, source_target_pairs={{0,4},{4,0},{8,12},{12,8},{16,20},{20,16},{24,28},{28,24},{1,5},{5... | collective-permute-start | bytes 245768 | tf_op jit(solution)/shard_map/ppermute | solution.py:25
  47.6 1.3 %collective-permute-start.15 = (bf16[32,1024]{1,0:T(8,128)(2,1)S(1)}, bf16[32,1024]{1,0:T(8,128)(2,1)S(1)}, u32[]{:S(2)}, u32[]{:S(2)}) collective-permute-start(bf16[32,1024]{1,0:T(8,128)(2,1)S(1)} %collective-permute-done.11.rest_3_), channel_id=1, source_target_pairs={{0,4},{4,0},{8,12},{12,8},{16,20},{20,16},{24,28},{28,24},{1,5},{5... | collective-permute-start | bytes 196616 | tf_op jit(solution)/shard_map/ppermute | solution.py:25
  47.6 1.4 %collective-permute-start.14 = (bf16[32,1024]{1,0:T(8,128)(2,1)S(1)}, bf16[32,1024]{1,0:T(8,128)(2,1)S(1)}, u32[]{:S(2)}, u32[]{:S(2)}) collective-permute-start(bf16[32,1024]{1,0:T(8,128)(2,1)S(1)} %collective-permute-done.10.rest_2_), channel_id=1, source_target_pairs={{0,4},{4,0},{8,12},{12,8},{16,20},{20,16},{24,28},{28,24},{1,5},{5... | collective-permute-start | bytes 196616 | tf_op jit(solution)/shard_map/ppermute | solution.py:25
  48.1 1.3 %collective-permute-start.13 = (bf16[32,1024]{1,0:T(8,128)(2,1)S(1)}, bf16[32,1024]{1,0:T(8,128)(2,1)S(1)}, u32[]{:S(2)}, u32[]{:S(2)}) collective-permute-start(bf16[32,1024]{1,0:T(8,128)(2,1)S(1)} %collective-permute-done.9.rest_1_), channel_id=1, source_target_pairs={{0,4},{4,0},{8,12},{12,8},{16,20},{20,16},{24,28},{28,24},{1,5},{5... | collective-permute-start | bytes 196616 | tf_op jit(solution)/shard_map/ppermute | solution.py:25

commit v5 on v4

--- a/solution.py
+++ b/solution.py
@@ -17,7 +17,8 @@
 HBM = pl.BlockSpec(memory_space=pltpu.HBM)
 DIGITS = (65536, 256, 1)
 DIGIT_ROWS = 8
-FIRST_GRANT = 58 << 20
+TILE = 128
+FIRST_GRANT = 48 << 20
 SECOND_GRANT = 48 << 20
 
 
@@ -66,8 +67,10 @@
 
 
 def peers_kernel(size, pos_ref, acts_ref, proj_ref, *rest):
-    outs, (buffers, sums_ref, sems) = rest[: size - 1], rest[size - 1 :]
+    outs, (proj_buf, buffers, sums_ref, sems, proj_sem) = rest[: size - 1], rest[size - 1 :]
     chunk = buffers.shape[1]
+    load = pltpu.make_async_copy(proj_ref, proj_buf, proj_sem)
+    load.start()
     pieces = buffers.shape[0] // (size - 1)
     copies = []
     for k in range(1, size):
@@ -75,11 +78,14 @@
         copies += chunk_copies(acts_ref, block, chunk, buffers, sems, (k - 1) * pieces)
 
     def work(n):
+        if n == 0:
+            load.wait()
+
         def done(x):
             outs[n // pieces][...] = x.astype(BF16)
 
         piece = buffers.at[n]
-        project(proj_ref, piece, n % pieces * piece.shape[1], sums_ref, done)
+        project(proj_buf, piece, n % pieces * piece.shape[1], sums_ref, done)
 
     stream(copies, 3, work)
 
@@ -93,13 +99,15 @@
     outs = [jax.ShapeDtypeStruct((rank, chunk), BF16)] * (size - 1)
     return pl.pallas_call(
         functools.partial(peers_kernel, size),
-        in_specs=[SMEM, HBM, VMEM],
+        in_specs=[SMEM, HBM, HBM],
         out_specs=[VMEM] * len(outs),
         out_shape=outs,
         scratch_shapes=[
+            pltpu.VMEM((rank, width), BF16),
             pltpu.VMEM((count, chunk, width // pieces), BF16),
             pltpu.VMEM((rank, chunk), F32),
             pltpu.SemaphoreType.DMA((count,)),
+            pltpu.SemaphoreType.DMA,
         ],
         cost_estimate=pl.CostEstimate(
             flops=2 * chunk * (size - 1) * rank * width,
@@ -108,51 +116,38 @@
         ),
         compiler_params=pltpu.CompilerParams(vmem_limit_bytes=FIRST_GRANT),
         name="peer_partials",
-    )(pos, acts, proj_t)
+    )(pos, acts, pltpu.with_memory_space_constraint(proj_t, pltpu.HBM))
 
 
 def own_kernel(size, pos_ref, acts_ref, grads_ref, proj_in_ref, proj_out_ref, *rest):
     own_ref, dy_refs = rest[0], rest[1 : size + 1]
-    weights, acts_buf, grads_buf, sums_ref, acts_sem, grads_sem = rest[size + 1 :]
+    weights, acts_buf, sums_ref, acts_sem = rest[size + 1 :]
     pos = pos_ref[0]
     rank = proj_out_ref.shape[0]
     part = rank // size
     chunk = acts_buf.shape[1]
-    parts, span, _ = grads_buf.shape
-    copies = [
-        pltpu.make_async_copy(
-            grads_ref.at[n * span : (n + 1) * span], grads_buf.at[n], grads_sem.at[n]
-        )
-        for n in range(parts)
-    ]
-    copies += chunk_copies(acts_ref, pos, chunk, acts_buf, acts_sem, 0)
-
-    def work(n):
-        if n == 0:
-            row = lax.broadcasted_iota(jnp.int32, (rank, rank), 0)
-            col = lax.broadcasted_iota(jnp.int32, (rank, rank), 1)
-            source = (pos ^ (row // part)) * part + row % part
-            pick = jnp.where(col == source, 1.0, 0.0).astype(BF16)
-            weights[...] = jnp.dot(
-                pick, proj_out_ref[...], preferred_element_type=F32
-            ).astype(BF16)
-        if n < parts:
-            dy = lax.dot_general(weights[...], grads_buf[n], NT, preferred_element_type=F32)
-            for m in range(span // chunk):
-                block = dy[:, m * chunk : (m + 1) * chunk]
-                first = (n * (span // chunk) + m) * part
-                for k in range(size):
-                    lines = block[k * part : (k + 1) * part, :]
-                    dy_refs[k][first : first + part, :] = lines.astype(dy_refs[k].dtype)
-        else:
-
-            def done(x):
-                own_ref[...] = x
-
-            piece = acts_buf.at[n - parts]
-            project(proj_in_ref, piece, (n - parts) * piece.shape[1], sums_ref, done)
-
-    stream(copies, 4, work)
+    copies = chunk_copies(acts_ref, pos, chunk, acts_buf, acts_sem, 0)
+    for copy in copies:
+        copy.start()
+
+    row = lax.broadcasted_iota(jnp.int32, (rank, rank), 0)
+    col = lax.broadcasted_iota(jnp.int32, (rank, rank), 1)
+    source = (pos ^ (row // part)) * part + row % part
+    pick = jnp.where(col == source, 1.0, 0.0).astype(BF16)
+    weights[...] = jnp.dot(pick, proj_out_ref[...], preferred_element_type=F32).astype(BF16)
+    dy = lax.dot_general(weights[...], grads_ref[...], NT, preferred_element_type=F32)
+    for m in range(size):
+        for k in range(size):
+            lines = dy[k * part : (k + 1) * part, m * chunk : (m + 1) * chunk]
+            dy_refs[k][m * part : (m + 1) * part, :] = lines.astype(dy_refs[k].dtype)
+
+    def done(x):
+        own_ref[...] = x
+
+    for n, copy in enumerate(copies):
+        copy.wait()
+        piece = acts_buf.at[n]
+        project(proj_in_ref, piece, n * piece.shape[1], sums_ref, done)
 
 
 def own_partials(pos, acts, grads, proj_in_t, proj_out_t, size):
@@ -163,17 +158,15 @@
     pieces = pieces_of(acts_width, 2)
     return pl.pallas_call(
         functools.partial(own_kernel, size),
-        in_specs=[SMEM, HBM, HBM, VMEM, VMEM],
+        in_specs=[SMEM, HBM, VMEM, VMEM, VMEM],
         out_specs=[VMEM] * (size + 1),
         out_shape=[jax.ShapeDtypeStruct((rank, chunk), F32)] * 2
         + [jax.ShapeDtypeStruct((rank, chunk), BF16)] * (size - 1),
         scratch_shapes=[
             pltpu.VMEM((rank, grads_width), BF16),
             pltpu.VMEM((pieces, chunk, acts_width // pieces), BF16),
-            pltpu.VMEM((2, tokens // 2, grads_width), BF16),
             pltpu.VMEM((rank, chunk), F32),
             pltpu.SemaphoreType.DMA((pieces,)),
-            pltpu.SemaphoreType.DMA((2,)),
         ],
         cost_estimate=pl.CostEstimate(
             flops=2 * rank * (chunk * acts_width + tokens * grads_width),
@@ -187,7 +180,7 @@
 
 def docs_kernel(size, pos_ref, counts_ref, seg_ref, dy_own_ref, x_own_ref, *rest):
     messages = rest[: size - 1]
-    grads_ref, inner_ref, shared_ref, dy_ref, sums_ref = rest[size - 1 :]
+    inner_ref, shared_ref, dy_ref, sums_ref = rest[size - 1 :]
     docs, _ = seg_ref.shape
     rank, chunk = x_own_ref.shape
     part = rank // size
@@ -223,7 +216,6 @@
         wide = pieces[0] if lanes == 1 else jnp.concatenate(pieces, axis=1)
         wide = wide.astype(BF16)
         span = slice(a * rank, (a + lanes) * rank)
-        grads_ref[:, span] = wide
         inner_ref[:, span] = wide
         shared_ref[:docs, span] = wide
     left = jnp.sum(live_tokens)
@@ -245,9 +237,8 @@
     return pl.pallas_call(
         functools.partial(docs_kernel, size),
         in_specs=[SMEM, SMEM] + [VMEM] * (2 + size),
-        out_specs=[VMEM, VMEM, VMEM],
+        out_specs=[VMEM, VMEM],
         out_shape=[
-            jax.ShapeDtypeStruct((docs, part * rank), BF16),
             jax.ShapeDtypeStruct((docs, part * rank), BF16),
             jax.ShapeDtypeStruct((docs + DIGIT_ROWS, part * rank), BF16),
         ],
@@ -264,35 +255,48 @@
 
 
 def fisher_kernel(shards, half_ref, *rest):
-    rows, cols, out_ref = rest[:shards], rest[shards : 2 * shards], rest[2 * shards]
-    docs = rows[0].shape[0]
-    left = jnp.concatenate([r[...] for r in rows], axis=0)
-    right = jnp.concatenate([c[:docs, :] for c in cols], axis=0)
-    product = lax.dot_general(left, right, TN, preferred_element_type=F32)
+    rows, cols = rest[:shards], rest[shards : 2 * shards]
+    out_ref, right_ref, tiles_ref, sems = rest[2 * shards :]
+    docs, _ = rows[0].shape
+    count, tile, _ = tiles_ref.shape
     total = jnp.zeros((1, 1), F32)
-    for c in cols:
+    for n, c in enumerate(cols):
+        right_ref[n * docs : (n + 1) * docs, :] = c[:docs, :]
         digits = c[docs:, 0:1].astype(F32)
-        for n, unit in enumerate(DIGITS):
-            total = total + digits[n : n + 1, :] * float(unit)
-    out_ref[...] = product * (1.0 / total)
+        for d, unit in enumerate(DIGITS):
+            total = total + digits[d : d + 1, :] * float(unit)
+    scale = 1.0 / total
+    copies = []
+    for t in range(count):
+        lanes = pl.ds(pl.multiple_of((half_ref[0] * count + t) * tile, tile), tile)
+        left = jnp.concatenate([r[:, lanes] for r in rows], axis=0)
+        product = lax.dot_general(left, right_ref[...], TN, preferred_element_type=F32)
+        tiles_ref[t] = product * scale
+        copy = pltpu.make_async_copy(
+            tiles_ref.at[t], out_ref.at[t * tile : (t + 1) * tile], sems.at[t]
+        )
+        copy.start()
+        copies.append(copy)
+    for copy in copies:
+        copy.wait()
 
 
 def fisher_block(half, rows, cols):
     shards = len(rows)
     docs, width = rows[0].shape
     height = width // 2
-    tile = min(256, height)
-    tiles = height // tile
+    tile = min(TILE, height)
+    count = height // tile
     return pl.pallas_call(
         functools.partial(fisher_kernel, shards),
-        grid_spec=pltpu.PrefetchScalarGridSpec(
-            num_scalar_prefetch=1,
-            grid=(tiles,),
-            in_specs=[pl.BlockSpec((docs, tile), lambda i, h: (0, h[0] * tiles + i))] * shards
-            + [pl.BlockSpec((docs + DIGIT_ROWS, width), lambda i, h: (0, 0))] * shards,
-            out_specs=pl.BlockSpec((tile, width), lambda i, h: (i, 0)),
-        ),
+        in_specs=[SMEM] + [VMEM] * (2 * shards),
+        out_specs=HBM,
         out_shape=jax.ShapeDtypeStruct((height, width), F32),
+        scratch_shapes=[
+            pltpu.VMEM((shards * docs, width), BF16),
+            pltpu.VMEM((count, tile, width), F32),
+            pltpu.SemaphoreType.DMA((count,)),
+        ],
         cost_estimate=pl.CostEstimate(
             flops=2 * docs * shards * height * width,
             bytes_accessed=4 * height * width,
@@ -322,7 +326,7 @@
         x = x + partial.astype(F32)
     x = x.astype(BF16)
     messages = [swap(jnp.concatenate([x, dys[k - 1]]), "tensor", k) for k in steps]
-    grads, inner, shared = doc_sums(pos1, doc_counts, segments, dy_own, x, messages)
+    inner, shared = doc_sums(pos1, doc_counts, segments, dy_own, x, messages)
 
     cols = {0: shared}
     for j in steps:
@@ -339,7 +343,7 @@
     cols = [cols[j] for j in range(size)]
     cols += [swap(c, "dp", 1) for c in cols]
     rows += [swap(r, "dp", 1) for r in rows]
-    return grads, fisher_block(half1, rows, cols)
+    return shared[: inner.shape[0]], fisher_block(half1, rows, cols)
 
 
 def solution(mesh):

time: 51.4 us -> 50 us (0.973)
  Pallas kernels: 14.5 us -> 12.5 us
  waiting for transfers between devices: 10.3 us -> 12.1 us
  starting transfers between devices: 24.9 us -> 23.1 us
  local copies, waits for them, and re-layouts: 0.02 us -> 0.65 us
    ppermute x23, waiting for transfers between devices: 10.3 us -> 12.1 us  [swap(): lax.ppermute(value, axis, [(i, i ^ step) for i in range(lax.axis_size(axi...]
    ppermute x23, starting transfers between devices: 24.9 us -> 23.1 us  [swap(): lax.ppermute(value, axis, [(i, i ^ step) for i in range(lax.axis_size(axi...]
    pallas_call x1, Pallas kernels: 7.52 us -> 6.63 us  [peer_partials(): pl.pallas_call(functools.partial(peers_kernel, size), in_specs=[SMEM, HBM...]
    slice x0 -> x1, local copies, waits for them, and re-layouts: none -> 0.63 us  [per_device(): return (shared[:inner.shape[0]], fisher_block(half1, rows, cols))]
    pallas_call x1, Pallas kernels: 2.01 us -> 1.38 us  [doc_sums(): pl.pallas_call(functools.partial(docs_kernel, size), in_specs=[SMEM, SMEM...]
  transfers between devices with their start and end apart: 23 -> 23, of which waited for: 9 -> 8; matrix products, arithmetic and copies ran while one was open for 0% -> 1% of each run, Pallas kernels for 6% -> 6%
where the time goes in v5:
time: 50 us; the launch traced here: 49.8 us
  starting transfers between devices  23.1 us (46%)
  Pallas kernels  12.5 us (25%)
  waiting for transfers between devices  12.1 us (24%)
  between operations  1.42 us (3%)
  local copies, waits for them, and re-layouts  0.65 us (1%)
    ppermute x23, starting transfers between devices, swap(): lax.ppermute(value, axis, [(i, i ^ step) for i in range(lax.axis_size(axi...  23.1 us
    ppermute x23, waiting for transfers between devices, swap(): lax.ppermute(value, axis, [(i, i ^ step) for i in range(lax.axis_size(axi...  12.1 us
    pallas_call x1, Pallas kernels, peer_partials(): pl.pallas_call(functools.partial(peers_kernel, size), in_specs=[SMEM, HBM...  6.63 us
    pallas_call x1, Pallas kernels, own_partials(): pl.pallas_call(functools.partial(own_kernel, size), in_specs=[SMEM, HBM,...  2.83 us
    pallas_call x1, Pallas kernels, fisher_block(): pl.pallas_call(functools.partial(fisher_kernel, shards), in_specs=[SMEM]...  1.62 us
    pallas_call x1, Pallas kernels, doc_sums(): pl.pallas_call(functools.partial(docs_kernel, size), in_specs=[SMEM, SMEM...  1.38 us
  transfers between devices with their start and end apart: 23, of which 8 were waited for; matrix products, arithmetic and copies ran while one was open for 1% of the time, Pallas kernels for 6%

profile of v5, /device:TPU:0, one launch (start us, length us, event | category | flops | bytes accessed | tf_op | source)
XLA Modules:
  0.0 49.8 jit_solution(5806220734639706005)
XLA Ops:
  0.6 0.0 copy-start
  0.6 0.0 copy-start.1
  0.7 0.0 copy-start.2
  0.7 6.6 %peer_partials.1 = (bf16[64,512]{1,0:T(8,128)(2,1)S(1)}, bf16[64,512]{1,0:T(8,128)(2,1)S(1)}, bf16[64,512]{1,0:T(8,128)(2,1)S(1)}) custom-call(s32[1]{0:T(128)} %bitcast.pos_ref, bf16[2048,3584]{1,0:T(8,128)(2,1)} %acts_ref.3, bf16[64,3584]{1,0:T(8,128)(2,1)} %bitcast.4), custom_call_target="tpu_custom_call" | custom-call | flops 704643072 | bytes 11010048 | tf_op jit(solution)/shard_map/peer_partials/pallas_call | solution.py:100
  7.3 3.0 %collective-permute-start = (bf16[64,512]{1,0:T(8,128)(2,1)S(1)}, bf16[64,512]{1,0:T(8,128)(2,1)S(1)}, u32[]{:S(2)}, u32[]{:S(2)}) collective-permute-start(bf16[64,512]{1,0:T(8,128)(2,1)S(1)} %get-tuple-element.14), channel_id=1, source_target_pairs={{0,1},{1,0},{2,3},{3,2},{4,5},{5,4},{6,7},{7,6},{8,9},{9,8},{10,11... | collective-permute-start | bytes 196616 | tf_op jit(solution)/shard_map/ppermute | solution.py:26
  10.3 1.5 %collective-permute-start.1 = (bf16[64,512]{1,0:T(8,128)(2,1)S(1)}, bf16[64,512]{1,0:T(8,128)(2,1)S(1)}, u32[]{:S(2)}, u32[]{:S(2)}) collective-permute-start(bf16[64,512]{1,0:T(8,128)(2,1)S(1)} %get-tuple-element.15), channel_id=1, source_target_pairs={{0,2},{1,3},{2,0},{3,1},{4,6},{5,7},{6,4},{7,5},{8,10},{9,11},{10,... | collective-permute-start | bytes 196616 | tf_op jit(solution)/shard_map/ppermute | solution.py:26
  11.8 0.0 collective-permute-start.2
  11.9 0.0 copy-done
  11.9 0.0 copy-done.1
  11.9 0.0 copy-done.2
  11.9 0.0 copy-start.3
  11.9 2.8 %own_partials.1 = (f32[64,512]{1,0:T(8,128)S(1)}, f32[64,512]{1,0:T(8,128)S(1)}, bf16[64,512]{1,0:T(8,128)(2,1)S(1)}, bf16[64,512]{1,0:T(8,128)(2,1)S(1)}, bf16[64,512]{1,0:T(8,128)(2,1)S(1)}) custom-call(s32[1]{0:T(128)} %bitcast.pos_ref, bf16[2048,3584]{1,0:T(8,128)(2,1)} %acts_ref.3, bf16[2048,1024]{1,0:T(8,128)(2,1)S(1)} %copy-done, ...), custom_call_target="tpu_custom_call" | custom-call | flops 503316480 | bytes 7864320 | tf_op jit(solution)/shard_map/own_partials/pallas_call | solution.py:159
  14.7 0.0 collective-permute-done
  14.7 0.0 collective-permute-done.1
  14.7 2.3 %collective-permute-done.2 = bf16[64,512]{1,0:T(8,128)(2,1)S(1)} collective-permute-done((bf16[64,512]{1,0:T(8,128)(2,1)S(1)}, bf16[64,512]{1,0:T(8,128)(2,1)S(1)}, u32[]{:S(2)}, u32[]{:S(2)}) %collective-permute-start.2) | collective-permute-done | bytes 65568 | tf_op jit(solution)/shard_map/ppermute | solution.py:26
  17.1 0.6 %collective-permute-start.3 = (bf16[128,512]{1,0:T(8,128)(2,1)S(1)}, bf16[128,512]{1,0:T(8,128)(2,1)S(1)}, u32[]{:S(2)}, u32[]{:S(2)}) collective-permute-start(bf16[128,512]{1,0:T(8,128)(2,1)S(1)} %get-tuple-element.28), channel_id=1, source_target_pairs={{0,1},{1,0},{2,3},{3,2},{4,5},{5,4},{6,7},{7,6},{8,9},{9,8},{10,11... | collective-permute-start | bytes 393224 | tf_op jit(solution)/shard_map/ppermute | solution.py:26
  17.7 0.7 %collective-permute-start.4 = (bf16[128,512]{1,0:T(8,128)(2,1)S(1)}, bf16[128,512]{1,0:T(8,128)(2,1)S(1)}, u32[]{:S(2)}, u32[]{:S(2)}) collective-permute-start(bf16[128,512]{1,0:T(8,128)(2,1)S(1)} %get-tuple-element.27), channel_id=1, source_target_pairs={{0,2},{1,3},{2,0},{3,1},{4,6},{5,7},{6,4},{7,5},{8,10},{9,11},{10,... | collective-permute-start | bytes 393224 | tf_op jit(solution)/shard_map/ppermute | solution.py:26
  18.4 2.3 %collective-permute-start.5 = (bf16[128,512]{1,0:T(8,128)(2,1)S(1)}, bf16[128,512]{1,0:T(8,128)(2,1)S(1)}, u32[]{:S(2)}, u32[]{:S(2)}) collective-permute-start(bf16[128,512]{1,0:T(8,128)(2,1)S(1)} %get-tuple-element.26), channel_id=1, source_target_pairs={{0,3},{1,2},{2,1},{3,0},{4,7},{5,6},{6,5},{7,4},{8,11},{9,10},{10,... | collective-permute-start | bytes 393224 | tf_op jit(solution)/shard_map/ppermute | solution.py:26
  21.3 1.2 %collective-permute-done.3.rest_0_ = bf16[128,512]{1,0:T(8,128)(2,1)S(1)} collective-permute-done((bf16[128,512]{1,0:T(8,128)(2,1)S(1)}, bf16[128,512]{1,0:T(8,128)(2,1)S(1)}, u32[]{:S(2)}, u32[]{:S(2)}) %collective-permute-start.3) | collective-permute-done | bytes 131104 | tf_op jit(solution)/shard_map/ppermute | solution.py:26
  22.5 2.3 %collective-permute-done.4.rest_1_ = bf16[128,512]{1,0:T(8,128)(2,1)S(1)} collective-permute-done((bf16[128,512]{1,0:T(8,128)(2,1)S(1)}, bf16[128,512]{1,0:T(8,128)(2,1)S(1)}, u32[]{:S(2)}, u32[]{:S(2)}) %collective-permute-start.4) | collective-permute-done | bytes 131104 | tf_op jit(solution)/shard_map/ppermute | solution.py:26
  24.8 0.0 collective-permute-done.5.rest_2_
  24.8 0.0 copy-done.3
  24.8 1.4 %doc_sums.1 = (bf16[32,1024]{1,0:T(8,128)(2,1)S(1)}, bf16[40,1024]{1,0:T(8,128)(2,1)S(1)}) custom-call(s32[1]{0:T(128)} %bitcast.pos_ref, s32[1]{0:T(128)S(6)} %copy.8.counts_ref, s32[32,2048]{1,0:T(8,128)S(1)} %copy-done.3, f32[64,512]{1,0:T(8,128)S(1)} %get-tuple-element.12.dy_own_ref, bf16[64,512]{1,0:T(8,128)(2,1)S(1)} %add_convert_fusion.x_own_ref, ...), custom_call_target="tpu_custom_call" | custom-call | flops 268435456 | bytes 1048576 | tf_op jit(solution)/shard_map/doc_sums/pallas_call | solution.py:237
  26.2 1.8 %collective-permute-start.6 = (bf16[32,1024]{1,0:T(8,128)(2,1)S(1)}, bf16[32,1024]{1,0:T(8,128)(2,1)S(1)}, u32[]{:S(2)}, u32[]{:S(2)}) collective-permute-start(bf16[32,1024]{1,0:T(8,128)(2,1)S(1)} %get-tuple-element.21), channel_id=1, source_target_pairs={{0,3},{1,2},{2,1},{3,0},{4,7},{5,6},{6,5},{7,4},{8,11},{9,10},{10,... | collective-permute-start | bytes 196616 | tf_op jit(solution)/shard_map/ppermute | solution.py:26
  28.0 0.7 %collective-permute-start.7 = (bf16[32,1024]{1,0:T(8,128)(2,1)S(1)}, bf16[32,1024]{1,0:T(8,128)(2,1)S(1)}, u32[]{:S(2)}, u32[]{:S(2)}) collective-permute-start(bf16[32,1024]{1,0:T(8,128)(2,1)S(1)} %get-tuple-element.21), channel_id=1, source_target_pairs={{0,2},{1,3},{2,0},{3,1},{4,6},{5,7},{6,4},{7,5},{8,10},{9,11},{10,... | collective-permute-start | bytes 196616 | tf_op jit(solution)/shard_map/ppermute | solution.py:26
  28.6 1.1 %collective-permute-start.8 = (bf16[32,1024]{1,0:T(8,128)(2,1)S(1)}, bf16[32,1024]{1,0:T(8,128)(2,1)S(1)}, u32[]{:S(2)}, u32[]{:S(2)}) collective-permute-start(bf16[32,1024]{1,0:T(8,128)(2,1)S(1)} %get-tuple-element.21), channel_id=1, source_target_pairs={{0,1},{1,0},{2,3},{3,2},{4,5},{5,4},{6,7},{7,6},{8,9},{9,8},{10,11... | collective-permute-start | bytes 196616 | tf_op jit(solution)/shard_map/ppermute | solution.py:26
  29.8 2.6 %collective-permute-start.17 = (bf16[40,1024]{1,0:T(8,128)(2,1)S(1)}, bf16[40,1024]{1,0:T(8,128)(2,1)S(1)}, u32[]{:S(2)}, u32[]{:S(2)}) collective-permute-start(bf16[40,1024]{1,0:T(8,128)(2,1)S(1)} %get-tuple-element.20.rest_8_), channel_id=1, source_target_pairs={{0,16},{4,20},{8,24},{12,28},{16,0},{20,4},{24,8},{28,12},{1,17},{... | collective-permute-start | bytes 245768 | tf_op jit(solution)/shard_map/ppermute | solution.py:26
  32.3 1.6 %collective-permute-start.16 = (bf16[40,1024]{1,0:T(8,128)(2,1)S(1)}, bf16[40,1024]{1,0:T(8,128)(2,1)S(1)}, u32[]{:S(2)}, u32[]{:S(2)}) collective-permute-start(bf16[40,1024]{1,0:T(8,128)(2,1)S(1)} %get-tuple-element.20.rest_8_), channel_id=1, source_target_pairs={{0,8},{4,12},{8,0},{12,4},{16,24},{20,28},{24,16},{28,20},{1,9},{5... | collective-permute-start | bytes 245768 | tf_op jit(solution)/shard_map/ppermute | solution.py:26
  33.9 0.0 collective-permute-done.6
  33.9 0.0 collective-permute-start.19
  33.9 0.0 collective-permute-done.7
  33.9 0.0 collective-permute-done.8
  34.0 0.6 %collective-permute-start.9 = (bf16[32,1024]{1,0:T(8,128)(2,1)S(1)}, bf16[32,1024]{1,0:T(8,128)(2,1)S(1)}, u32[]{:S(2)}, u32[]{:S(2)}) collective-permute-start(bf16[32,1024]{1,0:T(8,128)(2,1)S(1)} %get-tuple-element.24), channel_id=1, source_target_pairs={{0,8},{4,12},{8,0},{12,4},{16,24},{20,28},{24,16},{28,20},{1,9},{5... | collective-permute-start | bytes 196616 | tf_op jit(solution)/shard_map/ppermute | solution.py:26
  34.6 0.5 %collective-permute-done.17.rest_10_ = bf16[40,1024]{1,0:T(8,128)(2,1)S(1)} collective-permute-done((bf16[40,1024]{1,0:T(8,128)(2,1)S(1)}, bf16[40,1024]{1,0:T(8,128)(2,1)S(1)}, u32[]{:S(2)}, u32[]{:S(2)}) %collective-permute-start.17) | collective-permute-done | bytes 81952 | tf_op jit(solution)/shard_map/ppermute | solution.py:26
  35.1 1.6 %collective-permute-start.18 = (bf16[40,1024]{1,0:T(8,128)(2,1)S(1)}, bf16[40,1024]{1,0:T(8,128)(2,1)S(1)}, u32[]{:S(2)}, u32[]{:S(2)}) collective-permute-start(bf16[40,1024]{1,0:T(8,128)(2,1)S(1)} %collective-permute-done.17.rest_10_), channel_id=1, source_target_pairs={{0,8},{4,12},{8,0},{12,4},{16,24},{20,28},{24,16},{28,20},{1,9},{5... | collective-permute-start | bytes 245768 | tf_op jit(solution)/shard_map/ppermute | solution.py:26
  36.7 3.4 %collective-permute-start.10 = (bf16[32,1024]{1,0:T(8,128)(2,1)S(1)}, bf16[32,1024]{1,0:T(8,128)(2,1)S(1)}, u32[]{:S(2)}, u32[]{:S(2)}) collective-permute-start(bf16[32,1024]{1,0:T(8,128)(2,1)S(1)} %get-tuple-element.23), channel_id=1, source_target_pairs={{0,16},{4,20},{8,24},{12,28},{16,0},{20,4},{24,8},{28,12},{1,17},{... | collective-permute-start | bytes 196616 | tf_op jit(solution)/shard_map/ppermute | solution.py:26
  40.1 0.0 collective-permute-done.16.rest_9_
  40.1 0.0 collective-permute-start.20
  40.1 0.0 collective-permute-done.19.rest_12_
  40.1 0.1 collective-permute-start.11
  40.2 0.0 collective-permute-done.9.rest_1_
  40.2 0.5 collective-permute-start.12
  40.7 2.6 %collective-permute-done.10.rest_2_ = bf16[32,1024]{1,0:T(8,128)(2,1)S(1)} collective-permute-done((bf16[32,1024]{1,0:T(8,128)(2,1)S(1)}, bf16[32,1024]{1,0:T(8,128)(2,1)S(1)}, u32[]{:S(2)}, u32[]{:S(2)}) %collective-permute-start.10) | collective-permute-done | bytes 65568 | tf_op jit(solution)/shard_map/ppermute | solution.py:26
  43.3 0.0 collective-permute-start.21
  43.3 0.0 collective-permute-done.18.rest_11_
  43.3 0.5 %collective-permute-start.22 = (bf16[40,1024]{1,0:T(8,128)(2,1)S(1)}, bf16[40,1024]{1,0:T(8,128)(2,1)S(1)}, u32[]{:S(2)}, u32[]{:S(2)}) collective-permute-start(bf16[40,1024]{1,0:T(8,128)(2,1)S(1)} %collective-permute-done.18.rest_11_), channel_id=1, source_target_pairs={{0,4},{4,0},{8,12},{12,8},{16,20},{20,16},{24,28},{28,24},{1,5},{5... | collective-permute-start | bytes 245768 | tf_op jit(solution)/shard_map/ppermute | solution.py:26
  43.9 2.6 %collective-permute-done.11.rest_3_ = bf16[32,1024]{1,0:T(8,128)(2,1)S(1)} collective-permute-done((bf16[32,1024]{1,0:T(8,128)(2,1)S(1)}, bf16[32,1024]{1,0:T(8,128)(2,1)S(1)}, u32[]{:S(2)}, u32[]{:S(2)}) %collective-permute-start.11) | collective-permute-done | bytes 65568 | tf_op jit(solution)/shard_map/ppermute | solution.py:26
  46.4 0.0 collective-permute-start.13
  46.4 0.0 collective-permute-done.12.rest_4_
  46.4 0.5 %collective-permute-start.14 = (bf16[32,1024]{1,0:T(8,128)(2,1)S(1)}, bf16[32,1024]{1,0:T(8,128)(2,1)S(1)}, u32[]{:S(2)}, u32[]{:S(2)}) collective-permute-start(bf16[32,1024]{1,0:T(8,128)(2,1)S(1)} %collective-permute-done.10.rest_2_), channel_id=1, source_target_pairs={{0,4},{4,0},{8,12},{12,8},{16,20},{20,16},{24,28},{28,24},{1,5},{5... | collective-permute-start | bytes 196616 | tf_op jit(solution)/shard_map/ppermute | solution.py:26
  46.9 0.0 collective-permute-done.20.rest_13_
  46.9 0.1 collective-permute-start.15
  47.0 0.6 %slice.3 = bf16[32,1024]{1,0:T(8,128)(2,1)} slice(bf16[40,1024]{1,0:T(8,128)(2,1)S(1)} %get-tuple-element.20.rest_8_), slice={[0:32], [0:1024]} | slice | bytes 131072 | tf_op jit(solution)/shard_map/slice | solution.py:346
  47.6 0.0 collective-permute-done.21.rest_14_
  47.7 0.0 collective-permute-done.13.rest_5_
  47.7 0.2 collective-permute-done.14.rest_6_
  47.8 0.4 collective-permute-done.15.rest_7_
  48.2 0.0 collective-permute-done.22.rest_15_
  48.2 1.6 %fisher_block.1 = f32[512,1024]{1,0:T(8,128)} custom-call(s32[1]{0:T(128)} %bitcast.3.half_ref, bf16[32,1024]{1,0:T(8,128)(2,1)S(1)} %get-tuple-element.25.rest_0_, bf16[32,1024]{1,0:T(8,128)(2,1)S(1)} %collective-permute-done.9.rest_1_, bf16[32,1024]{1,0:T(8,128)(2,1)S(1)} %collective-permute-done.10.rest_2_, ...), custom_call_target="tpu_custom_call" | custom-call | flops 268435456 | bytes 2097152 | tf_op jit(solution)/shard_map/fisher_block/pallas_call | solution.py:290
  (3 shorter events, 0.1 us)
Async XLA Ops:
  0.6 11.2 %copy-start = (bf16[2048,1024]{1,0:T(8,128)(2,1)S(1)}, bf16[2048,1024]{1,0:T(8,128)(2,1)}, u32[]{:S(2)}) copy-start(bf16[2048,1024]{1,0:T(8,128)(2,1)} %grads_ref.1) | copy-start | bytes 12582916
  0.6 11.2 %copy-start.1 = (bf16[3584,64]{0,1:T(8,128)(2,1)S(1)}, bf16[3584,64]{0,1:T(8,128)(2,1)}, u32[]{:S(2)}) copy-start(bf16[3584,64]{0,1:T(8,128)(2,1)} %param.8) | copy-start | bytes 1376260
  0.7 11.2 %copy-start.2 = (bf16[1024,64]{0,1:T(8,128)(2,1)S(1)}, bf16[1024,64]{0,1:T(8,128)(2,1)}, u32[]{:S(2)}) copy-start(bf16[1024,64]{0,1:T(8,128)(2,1)} %param.9) | copy-start | bytes 393220
  7.3 7.4 %collective-permute-start = (bf16[64,512]{1,0:T(8,128)(2,1)S(1)}, bf16[64,512]{1,0:T(8,128)(2,1)S(1)}, u32[]{:S(2)}, u32[]{:S(2)}) collective-permute-start(bf16[64,512]{1,0:T(8,128)(2,1)S(1)} %get-tuple-element.14), channel_id=1, source_target_pairs={{0,1},{1,0},{2,3},{3,2},{4,5},{5,4},{6,7},{7,6},{8,9},{9,8},{10,11... | collective-permute-start | bytes 196616 | tf_op jit(solution)/shard_map/ppermute | solution.py:26
  10.3 4.4 %collective-permute-start.1 = (bf16[64,512]{1,0:T(8,128)(2,1)S(1)}, bf16[64,512]{1,0:T(8,128)(2,1)S(1)}, u32[]{:S(2)}, u32[]{:S(2)}) collective-permute-start(bf16[64,512]{1,0:T(8,128)(2,1)S(1)} %get-tuple-element.15), channel_id=1, source_target_pairs={{0,2},{1,3},{2,0},{3,1},{4,6},{5,7},{6,4},{7,5},{8,10},{9,11},{10,... | collective-permute-start | bytes 196616 | tf_op jit(solution)/shard_map/ppermute | solution.py:26
  11.8 5.2 %collective-permute-start.2 = (bf16[64,512]{1,0:T(8,128)(2,1)S(1)}, bf16[64,512]{1,0:T(8,128)(2,1)S(1)}, u32[]{:S(2)}, u32[]{:S(2)}) collective-permute-start(bf16[64,512]{1,0:T(8,128)(2,1)S(1)} %get-tuple-element.16), channel_id=1, source_target_pairs={{0,3},{1,2},{2,1},{3,0},{4,7},{5,6},{6,5},{7,4},{8,11},{9,10},{10,... | collective-permute-start | bytes 196616 | tf_op jit(solution)/shard_map/ppermute | solution.py:26
  11.9 12.9 %copy-start.3 = (s32[32,2048]{1,0:T(8,128)S(1)}, s32[32,2048]{1,0:T(8,128)}, u32[]{:S(2)}) copy-start(s32[32,2048]{1,0:T(8,128)} %seg_ref.1) | copy-start | bytes 786436
  17.1 5.4 %collective-permute-start.3 = (bf16[128,512]{1,0:T(8,128)(2,1)S(1)}, bf16[128,512]{1,0:T(8,128)(2,1)S(1)}, u32[]{:S(2)}, u32[]{:S(2)}) collective-permute-start(bf16[128,512]{1,0:T(8,128)(2,1)S(1)} %get-tuple-element.28), channel_id=1, source_target_pairs={{0,1},{1,0},{2,3},{3,2},{4,5},{5,4},{6,7},{7,6},{8,9},{9,8},{10,11... | collective-permute-start | bytes 393224 | tf_op jit(solution)/shard_map/ppermute | solution.py:26
  17.7 7.1 %collective-permute-start.4 = (bf16[128,512]{1,0:T(8,128)(2,1)S(1)}, bf16[128,512]{1,0:T(8,128)(2,1)S(1)}, u32[]{:S(2)}, u32[]{:S(2)}) collective-permute-start(bf16[128,512]{1,0:T(8,128)(2,1)S(1)} %get-tuple-element.27), channel_id=1, source_target_pairs={{0,2},{1,3},{2,0},{3,1},{4,6},{5,7},{6,4},{7,5},{8,10},{9,11},{10,... | collective-permute-start | bytes 393224 | tf_op jit(solution)/shard_map/ppermute | solution.py:26
  18.4 6.4 %collective-permute-start.5 = (bf16[128,512]{1,0:T(8,128)(2,1)S(1)}, bf16[128,512]{1,0:T(8,128)(2,1)S(1)}, u32[]{:S(2)}, u32[]{:S(2)}) collective-permute-start(bf16[128,512]{1,0:T(8,128)(2,1)S(1)} %get-tuple-element.26), channel_id=1, source_target_pairs={{0,3},{1,2},{2,1},{3,0},{4,7},{5,6},{6,5},{7,4},{8,11},{9,10},{10,... | collective-permute-start | bytes 393224 | tf_op jit(solution)/shard_map/ppermute | solution.py:26
  26.2 7.7 %collective-permute-start.6 = (bf16[32,1024]{1,0:T(8,128)(2,1)S(1)}, bf16[32,1024]{1,0:T(8,128)(2,1)S(1)}, u32[]{:S(2)}, u32[]{:S(2)}) collective-permute-start(bf16[32,1024]{1,0:T(8,128)(2,1)S(1)} %get-tuple-element.21), channel_id=1, source_target_pairs={{0,3},{1,2},{2,1},{3,0},{4,7},{5,6},{6,5},{7,4},{8,11},{9,10},{10,... | collective-permute-start | bytes 196616 | tf_op jit(solution)/shard_map/ppermute | solution.py:26
  28.0 6.0 %collective-permute-start.7 = (bf16[32,1024]{1,0:T(8,128)(2,1)S(1)}, bf16[32,1024]{1,0:T(8,128)(2,1)S(1)}, u32[]{:S(2)}, u32[]{:S(2)}) collective-permute-start(bf16[32,1024]{1,0:T(8,128)(2,1)S(1)} %get-tuple-element.21), channel_id=1, source_target_pairs={{0,2},{1,3},{2,0},{3,1},{4,6},{5,7},{6,4},{7,5},{8,10},{9,11},{10,... | collective-permute-start | bytes 196616 | tf_op jit(solution)/shard_map/ppermute | solution.py:26
  28.6 5.3 %collective-permute-start.8 = (bf16[32,1024]{1,0:T(8,128)(2,1)S(1)}, bf16[32,1024]{1,0:T(8,128)(2,1)S(1)}, u32[]{:S(2)}, u32[]{:S(2)}) collective-permute-start(bf16[32,1024]{1,0:T(8,128)(2,1)S(1)} %get-tuple-element.21), channel_id=1, source_target_pairs={{0,1},{1,0},{2,3},{3,2},{4,5},{5,4},{6,7},{7,6},{8,9},{9,8},{10,11... | collective-permute-start | bytes 196616 | tf_op jit(solution)/shard_map/ppermute | solution.py:26
  29.8 5.3 %collective-permute-start.17 = (bf16[40,1024]{1,0:T(8,128)(2,1)S(1)}, bf16[40,1024]{1,0:T(8,128)(2,1)S(1)}, u32[]{:S(2)}, u32[]{:S(2)}) collective-permute-start(bf16[40,1024]{1,0:T(8,128)(2,1)S(1)} %get-tuple-element.20.rest_8_), channel_id=1, source_target_pairs={{0,16},{4,20},{8,24},{12,28},{16,0},{20,4},{24,8},{28,12},{1,17},{... | collective-permute-start | bytes 245768 | tf_op jit(solution)/shard_map/ppermute | solution.py:26
  32.3 7.8 %collective-permute-start.16 = (bf16[40,1024]{1,0:T(8,128)(2,1)S(1)}, bf16[40,1024]{1,0:T(8,128)(2,1)S(1)}, u32[]{:S(2)}, u32[]{:S(2)}) collective-permute-start(bf16[40,1024]{1,0:T(8,128)(2,1)S(1)} %get-tuple-element.20.rest_8_), channel_id=1, source_target_pairs={{0,8},{4,12},{8,0},{12,4},{16,24},{20,28},{24,16},{28,20},{1,9},{5... | collective-permute-start | bytes 245768 | tf_op jit(solution)/shard_map/ppermute | solution.py:26
  33.9 6.2 %collective-permute-start.19 = (bf16[40,1024]{1,0:T(8,128)(2,1)S(1)}, bf16[40,1024]{1,0:T(8,128)(2,1)S(1)}, u32[]{:S(2)}, u32[]{:S(2)}) collective-permute-start(bf16[40,1024]{1,0:T(8,128)(2,1)S(1)} %get-tuple-element.20.rest_8_), channel_id=1, source_target_pairs={{0,4},{4,0},{8,12},{12,8},{16,20},{20,16},{24,28},{28,24},{1,5},{5... | collective-permute-start | bytes 245768 | tf_op jit(solution)/shard_map/ppermute | solution.py:26
  34.0 6.2 %collective-permute-start.9 = (bf16[32,1024]{1,0:T(8,128)(2,1)S(1)}, bf16[32,1024]{1,0:T(8,128)(2,1)S(1)}, u32[]{:S(2)}, u32[]{:S(2)}) collective-permute-start(bf16[32,1024]{1,0:T(8,128)(2,1)S(1)} %get-tuple-element.24), channel_id=1, source_target_pairs={{0,8},{4,12},{8,0},{12,4},{16,24},{20,28},{24,16},{28,20},{1,9},{5... | collective-permute-start | bytes 196616 | tf_op jit(solution)/shard_map/ppermute | solution.py:26
  35.1 8.2 %collective-permute-start.18 = (bf16[40,1024]{1,0:T(8,128)(2,1)S(1)}, bf16[40,1024]{1,0:T(8,128)(2,1)S(1)}, u32[]{:S(2)}, u32[]{:S(2)}) collective-permute-start(bf16[40,1024]{1,0:T(8,128)(2,1)S(1)} %collective-permute-done.17.rest_10_), channel_id=1, source_target_pairs={{0,8},{4,12},{8,0},{12,4},{16,24},{20,28},{24,16},{28,20},{1,9},{5... | collective-permute-start | bytes 245768 | tf_op jit(solution)/shard_map/ppermute | solution.py:26
  36.7 6.7 %collective-permute-start.10 = (bf16[32,1024]{1,0:T(8,128)(2,1)S(1)}, bf16[32,1024]{1,0:T(8,128)(2,1)S(1)}, u32[]{:S(2)}, u32[]{:S(2)}) collective-permute-start(bf16[32,1024]{1,0:T(8,128)(2,1)S(1)} %get-tuple-element.23), channel_id=1, source_target_pairs={{0,16},{4,20},{8,24},{12,28},{16,0},{20,4},{24,8},{28,12},{1,17},{... | collective-permute-start | bytes 196616 | tf_op jit(solution)/shard_map/ppermute | solution.py:26
  40.1 6.8 %collective-permute-start.20 = (bf16[40,1024]{1,0:T(8,128)(2,1)S(1)}, bf16[40,1024]{1,0:T(8,128)(2,1)S(1)}, u32[]{:S(2)}, u32[]{:S(2)}) collective-permute-start(bf16[40,1024]{1,0:T(8,128)(2,1)S(1)} %collective-permute-done.16.rest_9_), channel_id=1, source_target_pairs={{0,4},{4,0},{8,12},{12,8},{16,20},{20,16},{24,28},{28,24},{1,5},{5... | collective-permute-start | bytes 245768 | tf_op jit(solution)/shard_map/ppermute | solution.py:26
  40.1 6.3 %collective-permute-start.11 = (bf16[32,1024]{1,0:T(8,128)(2,1)S(1)}, bf16[32,1024]{1,0:T(8,128)(2,1)S(1)}, u32[]{:S(2)}, u32[]{:S(2)}) collective-permute-start(bf16[32,1024]{1,0:T(8,128)(2,1)S(1)} %get-tuple-element.22), channel_id=1, source_target_pairs={{0,24},{4,28},{8,16},{12,20},{16,8},{20,12},{24,0},{28,4},{1,25},{... | collective-permute-start | bytes 196616 | tf_op jit(solution)/shard_map/ppermute | solution.py:26
  40.2 6.2 %collective-permute-start.12 = (bf16[32,1024]{1,0:T(8,128)(2,1)S(1)}, bf16[32,1024]{1,0:T(8,128)(2,1)S(1)}, u32[]{:S(2)}, u32[]{:S(2)}) collective-permute-start(bf16[32,1024]{1,0:T(8,128)(2,1)S(1)} %get-tuple-element.25.rest_0_), channel_id=1, source_target_pairs={{0,4},{4,0},{8,12},{12,8},{16,20},{20,16},{24,28},{28,24},{1,5},{5... | collective-permute-start | bytes 196616 | tf_op jit(solution)/shard_map/ppermute | solution.py:26
  43.3 4.3 %collective-permute-start.21 = (bf16[40,1024]{1,0:T(8,128)(2,1)S(1)}, bf16[40,1024]{1,0:T(8,128)(2,1)S(1)}, u32[]{:S(2)}, u32[]{:S(2)}) collective-permute-start(bf16[40,1024]{1,0:T(8,128)(2,1)S(1)} %collective-permute-done.17.rest_10_), channel_id=1, source_target_pairs={{0,4},{4,0},{8,12},{12,8},{16,20},{20,16},{24,28},{28,24},{1,5},{5... | collective-permute-start | bytes 245768 | tf_op jit(solution)/shard_map/ppermute | solution.py:26
  43.3 4.9 %collective-permute-start.22 = (bf16[40,1024]{1,0:T(8,128)(2,1)S(1)}, bf16[40,1024]{1,0:T(8,128)(2,1)S(1)}, u32[]{:S(2)}, u32[]{:S(2)}) collective-permute-start(bf16[40,1024]{1,0:T(8,128)(2,1)S(1)} %collective-permute-done.18.rest_11_), channel_id=1, source_target_pairs={{0,4},{4,0},{8,12},{12,8},{16,20},{20,16},{24,28},{28,24},{1,5},{5... | collective-permute-start | bytes 245768 | tf_op jit(solution)/shard_map/ppermute | solution.py:26
  46.4 1.3 %collective-permute-start.13 = (bf16[32,1024]{1,0:T(8,128)(2,1)S(1)}, bf16[32,1024]{1,0:T(8,128)(2,1)S(1)}, u32[]{:S(2)}, u32[]{:S(2)}) collective-permute-start(bf16[32,1024]{1,0:T(8,128)(2,1)S(1)} %collective-permute-done.9.rest_1_), channel_id=1, source_target_pairs={{0,4},{4,0},{8,12},{12,8},{16,20},{20,16},{24,28},{28,24},{1,5},{5... | collective-permute-start | bytes 196616 | tf_op jit(solution)/shard_map/ppermute | solution.py:26
  46.4 1.4 %collective-permute-start.14 = (bf16[32,1024]{1,0:T(8,128)(2,1)S(1)}, bf16[32,1024]{1,0:T(8,128)(2,1)S(1)}, u32[]{:S(2)}, u32[]{:S(2)}) collective-permute-start(bf16[32,1024]{1,0:T(8,128)(2,1)S(1)} %collective-permute-done.10.rest_2_), channel_id=1, source_target_pairs={{0,4},{4,0},{8,12},{12,8},{16,20},{20,16},{24,28},{28,24},{1,5},{5... | collective-permute-start | bytes 196616 | tf_op jit(solution)/shard_map/ppermute | solution.py:26
  46.9 1.3 %collective-permute-start.15 = (bf16[32,1024]{1,0:T(8,128)(2,1)S(1)}, bf16[32,1024]{1,0:T(8,128)(2,1)S(1)}, u32[]{:S(2)}, u32[]{:S(2)}) collective-permute-start(bf16[32,1024]{1,0:T(8,128)(2,1)S(1)} %collective-permute-done.11.rest_3_), channel_id=1, source_target_pairs={{0,4},{4,0},{8,12},{12,8},{16,20},{20,16},{24,28},{28,24},{1,5},{5... | collective-permute-start | bytes 196616 | tf_op jit(solution)/shard_map/ppermute | solution.py:26

commit v6 on v5

--- a/solution.py
+++ b/solution.py
@@ -16,7 +16,7 @@
 VMEM = pl.BlockSpec(memory_space=pltpu.VMEM)
 HBM = pl.BlockSpec(memory_space=pltpu.HBM)
 DIGITS = (65536, 256, 1)
-DIGIT_ROWS = 8
+DIGIT_LANES = 128
 TILE = 128
 FIRST_GRANT = 48 << 20
 SECOND_GRANT = 48 << 20
@@ -217,15 +217,15 @@
         wide = wide.astype(BF16)
         span = slice(a * rank, (a + lanes) * rank)
         inner_ref[:, span] = wide
-        shared_ref[:docs, span] = wide
+        shared_ref[:, span] = wide
     left = jnp.sum(live_tokens)
-    row = lax.broadcasted_iota(jnp.int32, (DIGIT_ROWS, part * rank), 0)
+    row = lax.broadcasted_iota(jnp.int32, (docs, DIGIT_LANES), 0)
     digits = jnp.zeros(row.shape, jnp.int32)
     for n, unit in enumerate(DIGITS):
         digit = left // unit
         left = left - digit * unit
         digits = jnp.where(row == n, digit, digits)
-    shared_ref[docs:, :] = digits.astype(F32).astype(BF16)
+    shared_ref[:, part * rank :] = digits.astype(F32).astype(BF16)
 
 
 def doc_sums(pos, counts, seg, dy_own, x_own, messages):
@@ -240,7 +240,7 @@
         out_specs=[VMEM, VMEM],
         out_shape=[
             jax.ShapeDtypeStruct((docs, part * rank), BF16),
-            jax.ShapeDtypeStruct((docs + DIGIT_ROWS, part * rank), BF16),
+            jax.ShapeDtypeStruct((docs, part * rank + DIGIT_LANES), BF16),
         ],
         scratch_shapes=[
             pltpu.VMEM((rows * size, chunk), F32),
@@ -257,12 +257,12 @@
 def fisher_kernel(shards, half_ref, *rest):
     rows, cols = rest[:shards], rest[shards : 2 * shards]
     out_ref, right_ref, tiles_ref, sems = rest[2 * shards :]
-    docs, _ = rows[0].shape
+    docs, width = rows[0].shape
     count, tile, _ = tiles_ref.shape
     total = jnp.zeros((1, 1), F32)
     for n, c in enumerate(cols):
-        right_ref[n * docs : (n + 1) * docs, :] = c[:docs, :]
-        digits = c[docs:, 0:1].astype(F32)
+        right_ref[n * docs : (n + 1) * docs, :] = c[:, :width]
+        digits = c[:, width : width + 1].astype(F32)
         for d, unit in enumerate(DIGITS):
             total = total + digits[d : d + 1, :] * float(unit)
     scale = 1.0 / total
@@ -343,7 +343,7 @@
     cols = [cols[j] for j in range(size)]
     cols += [swap(c, "dp", 1) for c in cols]
     rows += [swap(r, "dp", 1) for r in rows]
-    return shared[: inner.shape[0]], fisher_block(half1, rows, cols)
+    return shared[:, : inner.shape[1]], fisher_block(half1, rows, cols)
 
 
 def solution(mesh):

time: 50 us -> 49.8 us (level)
  no operation moved by 1% of the time
where the time goes in v6:
time: 49.8 us; the launch traced here: 49.7 us
  starting transfers between devices  23 us (46%)
  Pallas kernels  12.5 us (25%)
  waiting for transfers between devices  12 us (24%)
  between operations  1.42 us (3%)
  local copies, waits for them, and re-layouts  0.65 us (1%)
    ppermute x23, starting transfers between devices, swap(): lax.ppermute(value, axis, [(i, i ^ step) for i in range(lax.axis_size(axi...  23 us
    ppermute x23, waiting for transfers between devices, swap(): lax.ppermute(value, axis, [(i, i ^ step) for i in range(lax.axis_size(axi...  12 us
    pallas_call x1, Pallas kernels, peer_partials(): pl.pallas_call(functools.partial(peers_kernel, size), in_specs=[SMEM, HBM...  6.63 us
    pallas_call x1, Pallas kernels, own_partials(): pl.pallas_call(functools.partial(own_kernel, size), in_specs=[SMEM, HBM,...  2.83 us
    pallas_call x1, Pallas kernels, fisher_block(): pl.pallas_call(functools.partial(fisher_kernel, shards), in_specs=[SMEM]...  1.63 us
    pallas_call x1, Pallas kernels, doc_sums(): pl.pallas_call(functools.partial(docs_kernel, size), in_specs=[SMEM, SMEM...  1.38 us
  transfers between devices with their start and end apart: 23, of which 8 were waited for; matrix products, arithmetic and copies ran while one was open for 1% of the time, Pallas kernels for 6%

profile of v6, /device:TPU:0, one launch (start us, length us, event | category | flops | bytes accessed | tf_op | source)
XLA Modules:
  0.0 49.7 jit_solution(5485474168965696061)
XLA Ops:
  0.6 0.0 copy-start
  0.6 0.0 copy-start.1
  0.7 0.0 copy-start.2
  0.7 6.6 %peer_partials.1 = (bf16[64,512]{1,0:T(8,128)(2,1)S(1)}, bf16[64,512]{1,0:T(8,128)(2,1)S(1)}, bf16[64,512]{1,0:T(8,128)(2,1)S(1)}) custom-call(s32[1]{0:T(128)} %bitcast.pos_ref, bf16[2048,3584]{1,0:T(8,128)(2,1)} %acts_ref.3, bf16[64,3584]{1,0:T(8,128)(2,1)} %bitcast.4), custom_call_target="tpu_custom_call" | custom-call | flops 704643072 | bytes 11010048 | tf_op jit(solution)/shard_map/peer_partials/pallas_call | solution.py:100
  7.3 3.0 %collective-permute-start = (bf16[64,512]{1,0:T(8,128)(2,1)S(1)}, bf16[64,512]{1,0:T(8,128)(2,1)S(1)}, u32[]{:S(2)}, u32[]{:S(2)}) collective-permute-start(bf16[64,512]{1,0:T(8,128)(2,1)S(1)} %get-tuple-element.14), channel_id=1, source_target_pairs={{0,1},{1,0},{2,3},{3,2},{4,5},{5,4},{6,7},{7,6},{8,9},{9,8},{10,11... | collective-permute-start | bytes 196616 | tf_op jit(solution)/shard_map/ppermute | solution.py:26
  10.3 1.5 %collective-permute-start.1 = (bf16[64,512]{1,0:T(8,128)(2,1)S(1)}, bf16[64,512]{1,0:T(8,128)(2,1)S(1)}, u32[]{:S(2)}, u32[]{:S(2)}) collective-permute-start(bf16[64,512]{1,0:T(8,128)(2,1)S(1)} %get-tuple-element.15), channel_id=1, source_target_pairs={{0,2},{1,3},{2,0},{3,1},{4,6},{5,7},{6,4},{7,5},{8,10},{9,11},{10,... | collective-permute-start | bytes 196616 | tf_op jit(solution)/shard_map/ppermute | solution.py:26
  11.8 0.0 collective-permute-start.2
  11.9 0.0 copy-done
  11.9 0.0 copy-done.1
  11.9 0.0 copy-done.2
  11.9 0.0 copy-start.3
  11.9 2.8 %own_partials.1 = (f32[64,512]{1,0:T(8,128)S(1)}, f32[64,512]{1,0:T(8,128)S(1)}, bf16[64,512]{1,0:T(8,128)(2,1)S(1)}, bf16[64,512]{1,0:T(8,128)(2,1)S(1)}, bf16[64,512]{1,0:T(8,128)(2,1)S(1)}) custom-call(s32[1]{0:T(128)} %bitcast.pos_ref, bf16[2048,3584]{1,0:T(8,128)(2,1)} %acts_ref.3, bf16[2048,1024]{1,0:T(8,128)(2,1)S(1)} %copy-done, ...), custom_call_target="tpu_custom_call" | custom-call | flops 503316480 | bytes 7864320 | tf_op jit(solution)/shard_map/own_partials/pallas_call | solution.py:159
  14.7 0.0 collective-permute-done
  14.7 0.0 collective-permute-done.1
  14.7 2.3 %collective-permute-done.2 = bf16[64,512]{1,0:T(8,128)(2,1)S(1)} collective-permute-done((bf16[64,512]{1,0:T(8,128)(2,1)S(1)}, bf16[64,512]{1,0:T(8,128)(2,1)S(1)}, u32[]{:S(2)}, u32[]{:S(2)}) %collective-permute-start.2) | collective-permute-done | bytes 65568 | tf_op jit(solution)/shard_map/ppermute | solution.py:26
  17.1 0.6 %collective-permute-start.3 = (bf16[128,512]{1,0:T(8,128)(2,1)S(1)}, bf16[128,512]{1,0:T(8,128)(2,1)S(1)}, u32[]{:S(2)}, u32[]{:S(2)}) collective-permute-start(bf16[128,512]{1,0:T(8,128)(2,1)S(1)} %get-tuple-element.28), channel_id=1, source_target_pairs={{0,1},{1,0},{2,3},{3,2},{4,5},{5,4},{6,7},{7,6},{8,9},{9,8},{10,11... | collective-permute-start | bytes 393224 | tf_op jit(solution)/shard_map/ppermute | solution.py:26
  17.7 0.7 %collective-permute-start.4 = (bf16[128,512]{1,0:T(8,128)(2,1)S(1)}, bf16[128,512]{1,0:T(8,128)(2,1)S(1)}, u32[]{:S(2)}, u32[]{:S(2)}) collective-permute-start(bf16[128,512]{1,0:T(8,128)(2,1)S(1)} %get-tuple-element.27), channel_id=1, source_target_pairs={{0,2},{1,3},{2,0},{3,1},{4,6},{5,7},{6,4},{7,5},{8,10},{9,11},{10,... | collective-permute-start | bytes 393224 | tf_op jit(solution)/shard_map/ppermute | solution.py:26
  18.4 2.3 %collective-permute-start.5 = (bf16[128,512]{1,0:T(8,128)(2,1)S(1)}, bf16[128,512]{1,0:T(8,128)(2,1)S(1)}, u32[]{:S(2)}, u32[]{:S(2)}) collective-permute-start(bf16[128,512]{1,0:T(8,128)(2,1)S(1)} %get-tuple-element.26), channel_id=1, source_target_pairs={{0,3},{1,2},{2,1},{3,0},{4,7},{5,6},{6,5},{7,4},{8,11},{9,10},{10,... | collective-permute-start | bytes 393224 | tf_op jit(solution)/shard_map/ppermute | solution.py:26
  21.3 1.2 %collective-permute-done.3.rest_0_ = bf16[128,512]{1,0:T(8,128)(2,1)S(1)} collective-permute-done((bf16[128,512]{1,0:T(8,128)(2,1)S(1)}, bf16[128,512]{1,0:T(8,128)(2,1)S(1)}, u32[]{:S(2)}, u32[]{:S(2)}) %collective-permute-start.3) | collective-permute-done | bytes 131104 | tf_op jit(solution)/shard_map/ppermute | solution.py:26
  22.5 2.3 %collective-permute-done.4.rest_1_ = bf16[128,512]{1,0:T(8,128)(2,1)S(1)} collective-permute-done((bf16[128,512]{1,0:T(8,128)(2,1)S(1)}, bf16[128,512]{1,0:T(8,128)(2,1)S(1)}, u32[]{:S(2)}, u32[]{:S(2)}) %collective-permute-start.4) | collective-permute-done | bytes 131104 | tf_op jit(solution)/shard_map/ppermute | solution.py:26
  24.8 0.0 collective-permute-done.5.rest_2_
  24.8 0.0 copy-done.3
  24.8 1.4 %doc_sums.1 = (bf16[32,1024]{1,0:T(8,128)(2,1)S(1)}, bf16[32,1152]{1,0:T(8,128)(2,1)S(1)}) custom-call(s32[1]{0:T(128)} %bitcast.pos_ref, s32[1]{0:T(128)S(6)} %copy.8.counts_ref, s32[32,2048]{1,0:T(8,128)S(1)} %copy-done.3, f32[64,512]{1,0:T(8,128)S(1)} %get-tuple-element.12.dy_own_ref, bf16[64,512]{1,0:T(8,128)(2,1)S(1)} %add_convert_fusion.x_own_ref, ...), custom_call_target="tpu_custom_call" | custom-call | flops 268435456 | bytes 1048576 | tf_op jit(solution)/shard_map/doc_sums/pallas_call | solution.py:237
  26.2 1.8 %collective-permute-start.6 = (bf16[32,1024]{1,0:T(8,128)(2,1)S(1)}, bf16[32,1024]{1,0:T(8,128)(2,1)S(1)}, u32[]{:S(2)}, u32[]{:S(2)}) collective-permute-start(bf16[32,1024]{1,0:T(8,128)(2,1)S(1)} %get-tuple-element.21), channel_id=1, source_target_pairs={{0,3},{1,2},{2,1},{3,0},{4,7},{5,6},{6,5},{7,4},{8,11},{9,10},{10,... | collective-permute-start | bytes 196616 | tf_op jit(solution)/shard_map/ppermute | solution.py:26
  28.0 0.7 %collective-permute-start.7 = (bf16[32,1024]{1,0:T(8,128)(2,1)S(1)}, bf16[32,1024]{1,0:T(8,128)(2,1)S(1)}, u32[]{:S(2)}, u32[]{:S(2)}) collective-permute-start(bf16[32,1024]{1,0:T(8,128)(2,1)S(1)} %get-tuple-element.21), channel_id=1, source_target_pairs={{0,2},{1,3},{2,0},{3,1},{4,6},{5,7},{6,4},{7,5},{8,10},{9,11},{10,... | collective-permute-start | bytes 196616 | tf_op jit(solution)/shard_map/ppermute | solution.py:26
  28.7 1.1 %collective-permute-start.8 = (bf16[32,1024]{1,0:T(8,128)(2,1)S(1)}, bf16[32,1024]{1,0:T(8,128)(2,1)S(1)}, u32[]{:S(2)}, u32[]{:S(2)}) collective-permute-start(bf16[32,1024]{1,0:T(8,128)(2,1)S(1)} %get-tuple-element.21), channel_id=1, source_target_pairs={{0,1},{1,0},{2,3},{3,2},{4,5},{5,4},{6,7},{7,6},{8,9},{9,8},{10,11... | collective-permute-start | bytes 196616 | tf_op jit(solution)/shard_map/ppermute | solution.py:26
  29.8 2.6 %collective-permute-start.17 = (bf16[32,1152]{1,0:T(8,128)(2,1)S(1)}, bf16[32,1152]{1,0:T(8,128)(2,1)S(1)}, u32[]{:S(2)}, u32[]{:S(2)}) collective-permute-start(bf16[32,1152]{1,0:T(8,128)(2,1)S(1)} %get-tuple-element.20.rest_8_), channel_id=1, source_target_pairs={{0,16},{4,20},{8,24},{12,28},{16,0},{20,4},{24,8},{28,12},{1,17},{... | collective-permute-start | bytes 221192 | tf_op jit(solution)/shard_map/ppermute | solution.py:26
  32.3 1.6 %collective-permute-start.16 = (bf16[32,1152]{1,0:T(8,128)(2,1)S(1)}, bf16[32,1152]{1,0:T(8,128)(2,1)S(1)}, u32[]{:S(2)}, u32[]{:S(2)}) collective-permute-start(bf16[32,1152]{1,0:T(8,128)(2,1)S(1)} %get-tuple-element.20.rest_8_), channel_id=1, source_target_pairs={{0,8},{4,12},{8,0},{12,4},{16,24},{20,28},{24,16},{28,20},{1,9},{5... | collective-permute-start | bytes 221192 | tf_op jit(solution)/shard_map/ppermute | solution.py:26
  33.9 0.0 collective-permute-done.6
  33.9 0.0 collective-permute-start.19
  33.9 0.0 collective-permute-done.7
  33.9 0.0 collective-permute-done.8
  34.0 0.6 %collective-permute-start.9 = (bf16[32,1024]{1,0:T(8,128)(2,1)S(1)}, bf16[32,1024]{1,0:T(8,128)(2,1)S(1)}, u32[]{:S(2)}, u32[]{:S(2)}) collective-permute-start(bf16[32,1024]{1,0:T(8,128)(2,1)S(1)} %get-tuple-element.24), channel_id=1, source_target_pairs={{0,8},{4,12},{8,0},{12,4},{16,24},{20,28},{24,16},{28,20},{1,9},{5... | collective-permute-start | bytes 196616 | tf_op jit(solution)/shard_map/ppermute | solution.py:26
  34.6 0.4 collective-permute-done.17.rest_10_
  35.0 1.6 %collective-permute-start.18 = (bf16[32,1152]{1,0:T(8,128)(2,1)S(1)}, bf16[32,1152]{1,0:T(8,128)(2,1)S(1)}, u32[]{:S(2)}, u32[]{:S(2)}) collective-permute-start(bf16[32,1152]{1,0:T(8,128)(2,1)S(1)} %collective-permute-done.17.rest_10_), channel_id=1, source_target_pairs={{0,8},{4,12},{8,0},{12,4},{16,24},{20,28},{24,16},{28,20},{1,9},{5... | collective-permute-start | bytes 221192 | tf_op jit(solution)/shard_map/ppermute | solution.py:26
  36.6 3.4 %collective-permute-start.10 = (bf16[32,1024]{1,0:T(8,128)(2,1)S(1)}, bf16[32,1024]{1,0:T(8,128)(2,1)S(1)}, u32[]{:S(2)}, u32[]{:S(2)}) collective-permute-start(bf16[32,1024]{1,0:T(8,128)(2,1)S(1)} %get-tuple-element.23), channel_id=1, source_target_pairs={{0,16},{4,20},{8,24},{12,28},{16,0},{20,4},{24,8},{28,12},{1,17},{... | collective-permute-start | bytes 196616 | tf_op jit(solution)/shard_map/ppermute | solution.py:26
  39.9 0.0 collective-permute-done.16.rest_9_
  39.9 0.0 collective-permute-start.20
  40.0 0.0 collective-permute-done.19.rest_12_
  40.0 0.1 collective-permute-start.11
  40.0 0.0 collective-permute-done.9.rest_1_
  40.0 0.5 collective-permute-start.12
  40.5 2.7 %collective-permute-done.10.rest_2_ = bf16[32,1024]{1,0:T(8,128)(2,1)S(1)} collective-permute-done((bf16[32,1024]{1,0:T(8,128)(2,1)S(1)}, bf16[32,1024]{1,0:T(8,128)(2,1)S(1)}, u32[]{:S(2)}, u32[]{:S(2)}) %collective-permute-start.10) | collective-permute-done | bytes 65568 | tf_op jit(solution)/shard_map/ppermute | solution.py:26
  43.3 0.0 collective-permute-start.21
  43.3 0.0 collective-permute-done.18.rest_11_
  43.3 0.5 %collective-permute-start.22 = (bf16[32,1152]{1,0:T(8,128)(2,1)S(1)}, bf16[32,1152]{1,0:T(8,128)(2,1)S(1)}, u32[]{:S(2)}, u32[]{:S(2)}) collective-permute-start(bf16[32,1152]{1,0:T(8,128)(2,1)S(1)} %collective-permute-done.18.rest_11_), channel_id=1, source_target_pairs={{0,4},{4,0},{8,12},{12,8},{16,20},{20,16},{24,28},{28,24},{1,5},{5... | collective-permute-start | bytes 221192 | tf_op jit(solution)/shard_map/ppermute | solution.py:26
  43.8 2.5 %collective-permute-done.11.rest_3_ = bf16[32,1024]{1,0:T(8,128)(2,1)S(1)} collective-permute-done((bf16[32,1024]{1,0:T(8,128)(2,1)S(1)}, bf16[32,1024]{1,0:T(8,128)(2,1)S(1)}, u32[]{:S(2)}, u32[]{:S(2)}) %collective-permute-start.11) | collective-permute-done | bytes 65568 | tf_op jit(solution)/shard_map/ppermute | solution.py:26
  46.3 0.0 collective-permute-start.13
  46.3 0.0 collective-permute-done.12.rest_4_
  46.3 0.5 %collective-permute-start.14 = (bf16[32,1024]{1,0:T(8,128)(2,1)S(1)}, bf16[32,1024]{1,0:T(8,128)(2,1)S(1)}, u32[]{:S(2)}, u32[]{:S(2)}) collective-permute-start(bf16[32,1024]{1,0:T(8,128)(2,1)S(1)} %collective-permute-done.10.rest_2_), channel_id=1, source_target_pairs={{0,4},{4,0},{8,12},{12,8},{16,20},{20,16},{24,28},{28,24},{1,5},{5... | collective-permute-start | bytes 196616 | tf_op jit(solution)/shard_map/ppermute | solution.py:26
  46.8 0.0 collective-permute-done.20.rest_13_
  46.8 0.1 collective-permute-start.15
  46.8 0.6 %slice.3 = bf16[32,1024]{1,0:T(8,128)(2,1)} slice(bf16[32,1152]{1,0:T(8,128)(2,1)S(1)} %get-tuple-element.20.rest_8_), slice={[0:32], [0:1024]} | slice | bytes 131072 | tf_op jit(solution)/shard_map/slice | solution.py:346
  47.5 0.0 collective-permute-done.21.rest_14_
  47.5 0.0 collective-permute-done.13.rest_5_
  47.5 0.2 collective-permute-done.14.rest_6_
  47.7 0.4 collective-permute-done.15.rest_7_
  48.0 0.0 collective-permute-done.22.rest_15_
  48.0 1.6 %fisher_block.1 = f32[512,1024]{1,0:T(8,128)} custom-call(s32[1]{0:T(128)} %bitcast.3.half_ref, bf16[32,1024]{1,0:T(8,128)(2,1)S(1)} %get-tuple-element.25.rest_0_, bf16[32,1024]{1,0:T(8,128)(2,1)S(1)} %collective-permute-done.9.rest_1_, bf16[32,1024]{1,0:T(8,128)(2,1)S(1)} %collective-permute-done.10.rest_2_, ...), custom_call_target="tpu_custom_call" | custom-call | flops 268435456 | bytes 2097152 | tf_op jit(solution)/shard_map/fisher_block/pallas_call | solution.py:290
  (3 shorter events, 0.1 us)
Async XLA Ops:
  0.6 11.2 %copy-start = (bf16[2048,1024]{1,0:T(8,128)(2,1)S(1)}, bf16[2048,1024]{1,0:T(8,128)(2,1)}, u32[]{:S(2)}) copy-start(bf16[2048,1024]{1,0:T(8,128)(2,1)} %grads_ref.1) | copy-start | bytes 12582916
  0.6 11.2 %copy-start.1 = (bf16[3584,64]{0,1:T(8,128)(2,1)S(1)}, bf16[3584,64]{0,1:T(8,128)(2,1)}, u32[]{:S(2)}) copy-start(bf16[3584,64]{0,1:T(8,128)(2,1)} %param.8) | copy-start | bytes 1376260
  0.7 11.2 %copy-start.2 = (bf16[1024,64]{0,1:T(8,128)(2,1)S(1)}, bf16[1024,64]{0,1:T(8,128)(2,1)}, u32[]{:S(2)}) copy-start(bf16[1024,64]{0,1:T(8,128)(2,1)} %param.9) | copy-start | bytes 393220
  7.3 7.4 %collective-permute-start = (bf16[64,512]{1,0:T(8,128)(2,1)S(1)}, bf16[64,512]{1,0:T(8,128)(2,1)S(1)}, u32[]{:S(2)}, u32[]{:S(2)}) collective-permute-start(bf16[64,512]{1,0:T(8,128)(2,1)S(1)} %get-tuple-element.14), channel_id=1, source_target_pairs={{0,1},{1,0},{2,3},{3,2},{4,5},{5,4},{6,7},{7,6},{8,9},{9,8},{10,11... | collective-permute-start | bytes 196616 | tf_op jit(solution)/shard_map/ppermute | solution.py:26
  10.3 4.4 %collective-permute-start.1 = (bf16[64,512]{1,0:T(8,128)(2,1)S(1)}, bf16[64,512]{1,0:T(8,128)(2,1)S(1)}, u32[]{:S(2)}, u32[]{:S(2)}) collective-permute-start(bf16[64,512]{1,0:T(8,128)(2,1)S(1)} %get-tuple-element.15), channel_id=1, source_target_pairs={{0,2},{1,3},{2,0},{3,1},{4,6},{5,7},{6,4},{7,5},{8,10},{9,11},{10,... | collective-permute-start | bytes 196616 | tf_op jit(solution)/shard_map/ppermute | solution.py:26
  11.8 5.2 %collective-permute-start.2 = (bf16[64,512]{1,0:T(8,128)(2,1)S(1)}, bf16[64,512]{1,0:T(8,128)(2,1)S(1)}, u32[]{:S(2)}, u32[]{:S(2)}) collective-permute-start(bf16[64,512]{1,0:T(8,128)(2,1)S(1)} %get-tuple-element.16), channel_id=1, source_target_pairs={{0,3},{1,2},{2,1},{3,0},{4,7},{5,6},{6,5},{7,4},{8,11},{9,10},{10,... | collective-permute-start | bytes 196616 | tf_op jit(solution)/shard_map/ppermute | solution.py:26
  11.9 12.9 %copy-start.3 = (s32[32,2048]{1,0:T(8,128)S(1)}, s32[32,2048]{1,0:T(8,128)}, u32[]{:S(2)}) copy-start(s32[32,2048]{1,0:T(8,128)} %seg_ref.1) | copy-start | bytes 786436
  17.1 5.4 %collective-permute-start.3 = (bf16[128,512]{1,0:T(8,128)(2,1)S(1)}, bf16[128,512]{1,0:T(8,128)(2,1)S(1)}, u32[]{:S(2)}, u32[]{:S(2)}) collective-permute-start(bf16[128,512]{1,0:T(8,128)(2,1)S(1)} %get-tuple-element.28), channel_id=1, source_target_pairs={{0,1},{1,0},{2,3},{3,2},{4,5},{5,4},{6,7},{7,6},{8,9},{9,8},{10,11... | collective-permute-start | bytes 393224 | tf_op jit(solution)/shard_map/ppermute | solution.py:26
  17.7 7.1 %collective-permute-start.4 = (bf16[128,512]{1,0:T(8,128)(2,1)S(1)}, bf16[128,512]{1,0:T(8,128)(2,1)S(1)}, u32[]{:S(2)}, u32[]{:S(2)}) collective-permute-start(bf16[128,512]{1,0:T(8,128)(2,1)S(1)} %get-tuple-element.27), channel_id=1, source_target_pairs={{0,2},{1,3},{2,0},{3,1},{4,6},{5,7},{6,4},{7,5},{8,10},{9,11},{10,... | collective-permute-start | bytes 393224 | tf_op jit(solution)/shard_map/ppermute | solution.py:26
  18.4 6.4 %collective-permute-start.5 = (bf16[128,512]{1,0:T(8,128)(2,1)S(1)}, bf16[128,512]{1,0:T(8,128)(2,1)S(1)}, u32[]{:S(2)}, u32[]{:S(2)}) collective-permute-start(bf16[128,512]{1,0:T(8,128)(2,1)S(1)} %get-tuple-element.26), channel_id=1, source_target_pairs={{0,3},{1,2},{2,1},{3,0},{4,7},{5,6},{6,5},{7,4},{8,11},{9,10},{10,... | collective-permute-start | bytes 393224 | tf_op jit(solution)/shard_map/ppermute | solution.py:26
  26.2 7.7 %collective-permute-start.6 = (bf16[32,1024]{1,0:T(8,128)(2,1)S(1)}, bf16[32,1024]{1,0:T(8,128)(2,1)S(1)}, u32[]{:S(2)}, u32[]{:S(2)}) collective-permute-start(bf16[32,1024]{1,0:T(8,128)(2,1)S(1)} %get-tuple-element.21), channel_id=1, source_target_pairs={{0,3},{1,2},{2,1},{3,0},{4,7},{5,6},{6,5},{7,4},{8,11},{9,10},{10,... | collective-permute-start | bytes 196616 | tf_op jit(solution)/shard_map/ppermute | solution.py:26
  28.0 6.0 %collective-permute-start.7 = (bf16[32,1024]{1,0:T(8,128)(2,1)S(1)}, bf16[32,1024]{1,0:T(8,128)(2,1)S(1)}, u32[]{:S(2)}, u32[]{:S(2)}) collective-permute-start(bf16[32,1024]{1,0:T(8,128)(2,1)S(1)} %get-tuple-element.21), channel_id=1, source_target_pairs={{0,2},{1,3},{2,0},{3,1},{4,6},{5,7},{6,4},{7,5},{8,10},{9,11},{10,... | collective-permute-start | bytes 196616 | tf_op jit(solution)/shard_map/ppermute | solution.py:26
  28.7 5.3 %collective-permute-start.8 = (bf16[32,1024]{1,0:T(8,128)(2,1)S(1)}, bf16[32,1024]{1,0:T(8,128)(2,1)S(1)}, u32[]{:S(2)}, u32[]{:S(2)}) collective-permute-start(bf16[32,1024]{1,0:T(8,128)(2,1)S(1)} %get-tuple-element.21), channel_id=1, source_target_pairs={{0,1},{1,0},{2,3},{3,2},{4,5},{5,4},{6,7},{7,6},{8,9},{9,8},{10,11... | collective-permute-start | bytes 196616 | tf_op jit(solution)/shard_map/ppermute | solution.py:26
  29.8 5.3 %collective-permute-start.17 = (bf16[32,1152]{1,0:T(8,128)(2,1)S(1)}, bf16[32,1152]{1,0:T(8,128)(2,1)S(1)}, u32[]{:S(2)}, u32[]{:S(2)}) collective-permute-start(bf16[32,1152]{1,0:T(8,128)(2,1)S(1)} %get-tuple-element.20.rest_8_), channel_id=1, source_target_pairs={{0,16},{4,20},{8,24},{12,28},{16,0},{20,4},{24,8},{28,12},{1,17},{... | collective-permute-start | bytes 221192 | tf_op jit(solution)/shard_map/ppermute | solution.py:26
  32.3 7.6 %collective-permute-start.16 = (bf16[32,1152]{1,0:T(8,128)(2,1)S(1)}, bf16[32,1152]{1,0:T(8,128)(2,1)S(1)}, u32[]{:S(2)}, u32[]{:S(2)}) collective-permute-start(bf16[32,1152]{1,0:T(8,128)(2,1)S(1)} %get-tuple-element.20.rest_8_), channel_id=1, source_target_pairs={{0,8},{4,12},{8,0},{12,4},{16,24},{20,28},{24,16},{28,20},{1,9},{5... | collective-permute-start | bytes 221192 | tf_op jit(solution)/shard_map/ppermute | solution.py:26
  33.9 6.0 %collective-permute-start.19 = (bf16[32,1152]{1,0:T(8,128)(2,1)S(1)}, bf16[32,1152]{1,0:T(8,128)(2,1)S(1)}, u32[]{:S(2)}, u32[]{:S(2)}) collective-permute-start(bf16[32,1152]{1,0:T(8,128)(2,1)S(1)} %get-tuple-element.20.rest_8_), channel_id=1, source_target_pairs={{0,4},{4,0},{8,12},{12,8},{16,20},{20,16},{24,28},{28,24},{1,5},{5... | collective-permute-start | bytes 221192 | tf_op jit(solution)/shard_map/ppermute | solution.py:26
  34.0 6.0 %collective-permute-start.9 = (bf16[32,1024]{1,0:T(8,128)(2,1)S(1)}, bf16[32,1024]{1,0:T(8,128)(2,1)S(1)}, u32[]{:S(2)}, u32[]{:S(2)}) collective-permute-start(bf16[32,1024]{1,0:T(8,128)(2,1)S(1)} %get-tuple-element.24), channel_id=1, source_target_pairs={{0,8},{4,12},{8,0},{12,4},{16,24},{20,28},{24,16},{28,20},{1,9},{5... | collective-permute-start | bytes 196616 | tf_op jit(solution)/shard_map/ppermute | solution.py:26
  35.0 8.3 %collective-permute-start.18 = (bf16[32,1152]{1,0:T(8,128)(2,1)S(1)}, bf16[32,1152]{1,0:T(8,128)(2,1)S(1)}, u32[]{:S(2)}, u32[]{:S(2)}) collective-permute-start(bf16[32,1152]{1,0:T(8,128)(2,1)S(1)} %collective-permute-done.17.rest_10_), channel_id=1, source_target_pairs={{0,8},{4,12},{8,0},{12,4},{16,24},{20,28},{24,16},{28,20},{1,9},{5... | collective-permute-start | bytes 221192 | tf_op jit(solution)/shard_map/ppermute | solution.py:26
  36.6 6.7 %collective-permute-start.10 = (bf16[32,1024]{1,0:T(8,128)(2,1)S(1)}, bf16[32,1024]{1,0:T(8,128)(2,1)S(1)}, u32[]{:S(2)}, u32[]{:S(2)}) collective-permute-start(bf16[32,1024]{1,0:T(8,128)(2,1)S(1)} %get-tuple-element.23), channel_id=1, source_target_pairs={{0,16},{4,20},{8,24},{12,28},{16,0},{20,4},{24,8},{28,12},{1,17},{... | collective-permute-start | bytes 196616 | tf_op jit(solution)/shard_map/ppermute | solution.py:26
  39.9 6.8 %collective-permute-start.20 = (bf16[32,1152]{1,0:T(8,128)(2,1)S(1)}, bf16[32,1152]{1,0:T(8,128)(2,1)S(1)}, u32[]{:S(2)}, u32[]{:S(2)}) collective-permute-start(bf16[32,1152]{1,0:T(8,128)(2,1)S(1)} %collective-permute-done.16.rest_9_), channel_id=1, source_target_pairs={{0,4},{4,0},{8,12},{12,8},{16,20},{20,16},{24,28},{28,24},{1,5},{5... | collective-permute-start | bytes 221192 | tf_op jit(solution)/shard_map/ppermute | solution.py:26
  40.0 6.3 %collective-permute-start.11 = (bf16[32,1024]{1,0:T(8,128)(2,1)S(1)}, bf16[32,1024]{1,0:T(8,128)(2,1)S(1)}, u32[]{:S(2)}, u32[]{:S(2)}) collective-permute-start(bf16[32,1024]{1,0:T(8,128)(2,1)S(1)} %get-tuple-element.22), channel_id=1, source_target_pairs={{0,24},{4,28},{8,16},{12,20},{16,8},{20,12},{24,0},{28,4},{1,25},{... | collective-permute-start | bytes 196616 | tf_op jit(solution)/shard_map/ppermute | solution.py:26
  40.0 6.2 %collective-permute-start.12 = (bf16[32,1024]{1,0:T(8,128)(2,1)S(1)}, bf16[32,1024]{1,0:T(8,128)(2,1)S(1)}, u32[]{:S(2)}, u32[]{:S(2)}) collective-permute-start(bf16[32,1024]{1,0:T(8,128)(2,1)S(1)} %get-tuple-element.25.rest_0_), channel_id=1, source_target_pairs={{0,4},{4,0},{8,12},{12,8},{16,20},{20,16},{24,28},{28,24},{1,5},{5... | collective-permute-start | bytes 196616 | tf_op jit(solution)/shard_map/ppermute | solution.py:26
  43.3 4.2 %collective-permute-start.21 = (bf16[32,1152]{1,0:T(8,128)(2,1)S(1)}, bf16[32,1152]{1,0:T(8,128)(2,1)S(1)}, u32[]{:S(2)}, u32[]{:S(2)}) collective-permute-start(bf16[32,1152]{1,0:T(8,128)(2,1)S(1)} %collective-permute-done.17.rest_10_), channel_id=1, source_target_pairs={{0,4},{4,0},{8,12},{12,8},{16,20},{20,16},{24,28},{28,24},{1,5},{5... | collective-permute-start | bytes 221192 | tf_op jit(solution)/shard_map/ppermute | solution.py:26
  43.3 4.8 %collective-permute-start.22 = (bf16[32,1152]{1,0:T(8,128)(2,1)S(1)}, bf16[32,1152]{1,0:T(8,128)(2,1)S(1)}, u32[]{:S(2)}, u32[]{:S(2)}) collective-permute-start(bf16[32,1152]{1,0:T(8,128)(2,1)S(1)} %collective-permute-done.18.rest_11_), channel_id=1, source_target_pairs={{0,4},{4,0},{8,12},{12,8},{16,20},{20,16},{24,28},{28,24},{1,5},{5... | collective-permute-start | bytes 221192 | tf_op jit(solution)/shard_map/ppermute | solution.py:26
  46.3 1.3 %collective-permute-start.13 = (bf16[32,1024]{1,0:T(8,128)(2,1)S(1)}, bf16[32,1024]{1,0:T(8,128)(2,1)S(1)}, u32[]{:S(2)}, u32[]{:S(2)}) collective-permute-start(bf16[32,1024]{1,0:T(8,128)(2,1)S(1)} %collective-permute-done.9.rest_1_), channel_id=1, source_target_pairs={{0,4},{4,0},{8,12},{12,8},{16,20},{20,16},{24,28},{28,24},{1,5},{5... | collective-permute-start | bytes 196616 | tf_op jit(solution)/shard_map/ppermute | solution.py:26
  46.3 1.4 %collective-permute-start.14 = (bf16[32,1024]{1,0:T(8,128)(2,1)S(1)}, bf16[32,1024]{1,0:T(8,128)(2,1)S(1)}, u32[]{:S(2)}, u32[]{:S(2)}) collective-permute-start(bf16[32,1024]{1,0:T(8,128)(2,1)S(1)} %collective-permute-done.10.rest_2_), channel_id=1, source_target_pairs={{0,4},{4,0},{8,12},{12,8},{16,20},{20,16},{24,28},{28,24},{1,5},{5... | collective-permute-start | bytes 196616 | tf_op jit(solution)/shard_map/ppermute | solution.py:26
  46.8 1.3 %collective-permute-start.15 = (bf16[32,1024]{1,0:T(8,128)(2,1)S(1)}, bf16[32,1024]{1,0:T(8,128)(2,1)S(1)}, u32[]{:S(2)}, u32[]{:S(2)}) collective-permute-start(bf16[32,1024]{1,0:T(8,128)(2,1)S(1)} %collective-permute-done.11.rest_3_), channel_id=1, source_target_pairs={{0,4},{4,0},{8,12},{12,8},{16,20},{20,16},{24,28},{28,24},{1,5},{5... | collective-permute-start | bytes 196616 | tf_op jit(solution)/shard_map/ppermute | solution.py:26
